TPU v7x, 512 devices: a whole 4x8x8 slice. The times are simulated.
512 devices in a mesh: row: 16 (over y, core), col: 32 (over x, z).
Axes of the slice: x: 4, y: 8, z: 8, core: 2. Of those that a mesh axis runs over, the one named last changes fastest.
Arguments:
- excitons: float32 [1024, 1024], P('row', 'col'), may hold values from -500 to 500
- valence_energy: float32 [1024], P('row'), may hold values from -3 to -1
- conduction_energy: float32 [1024], P('col'), may hold values from 1 to 3
- psi_valence: float32 [4096, 1024], P('row', 'col'), may hold values from -0.1875 to 0.1875
- psi_conduction: float32 [4096, 1024], P('col', 'row'), may hold values from -0.1875 to 0.1875
- screened: float32 [4096, 4096], P('row', 'col'), may hold values from -0.9 to 0.975, as said below
Outputs:
- next_vector: float32 [1024, 1024], P('row', 'col')
- coefficients: float32 [4], replicated
Inputs may be any that keep to these rules, and one draw needn't show every extreme that they name: symmetric: screened[p, p'] = screened[p', p].
All inputs are finite; a program needn't handle non-finite values.
Results may differ from a plain program's by a relative error of at most 0.0003.
Values sent between devices are 32-bit elements; how exact they have to be, the bound alone decides.
No kernel may reach another device: no remote copies, remote signals or barrier semaphores. Data moves between devices by JAX's collectives and lax.ppermute only.
A program may use at most 64 MiB of HBM per device.

v0:
```python
import functools

import jax
import jax.numpy as jnp
from jax import lax
from jax.sharding import Mesh
from jax.sharding import PartitionSpec as P

NV = 1024
NC = 1024
STEPS = 2
COL = ("col_0", "col_1")
ROW = ("row_0", "row_1")
ROW_COL = ("row_0", "row_1", "col_0", "col_1")


EPS = 1e-06


def copy_for_each(value, axis):
    size = lax.axis_size(axis)
    return lax.all_to_all(
        jnp.broadcast_to(value[None], (size, *value.shape)), axis, 0, 0, tiled=True
    )


def in_order(parts, dim):
    parts = jnp.moveaxis(parts, 0, dim)
    dims = parts.shape
    return parts.reshape(*dims[:dim], dims[dim] * dims[dim + 1], *dims[dim + 2 :])


def gathered_copies(value, axis, dim):
    parts = copy_for_each(value, axis)
    return in_order(parts, dim)


def cut_along(value, dim, size):
    dims = value.shape
    parts = value.reshape(*dims[:dim], size, dims[dim] // size, *dims[dim + 1 :])
    return jnp.moveaxis(parts, dim, 0)


def sum_at_owner(value, axis, dim):
    parts = cut_along(value, dim, lax.axis_size(axis))
    arrived = lax.all_to_all(parts, axis, split_axis=0, concat_axis=0, tiled=True)
    return arrived.sum(axis=0)


def over_axes(value, axes):
    return functools.reduce(lax.psum, axes, value)


def shards(excitons, valence_energy, conduction_energy, psi_valence, psi_conduction, screened):
    high = lax.Precision.HIGHEST
    count = NV * NC
    energy_gap = conduction_energy[None, :] - valence_energy[:, None]
    total = over_axes(jnp.sum(excitons * excitons), ROW_COL)
    vector = excitons / jnp.sqrt(total / count + EPS)
    previous = jnp.zeros_like(vector)
    beta_prev = jnp.zeros((), jnp.float32)
    values = []
    for step in range(STEPS):
        panel_valence = gathered_copies(psi_valence, COL, 1)
        panel_conduction = gathered_copies(psi_conduction, ROW, 1)
        full_rows = gathered_copies(vector, COL, 1)
        image_block = jnp.dot(full_rows, panel_conduction.T, precision=high)
        image_columns = lax.all_gather(image_block, ROW, axis=0, tiled=True)
        points = jnp.dot(panel_valence, image_columns, precision=high)
        weighted = points * screened
        back_valence = sum_at_owner(jnp.dot(panel_valence.T, weighted, precision=high), ROW, 0)
        back_flipped = back_valence.T
        kernel_flipped = sum_at_owner(
            jnp.dot(panel_conduction.T, back_flipped, precision=high), COL, 0
        )
        image = energy_gap * vector - kernel_flipped.T
        cross, square, older = (
            over_axes(jnp.sum(vector * image), ROW_COL),
            over_axes(jnp.sum(image * image), ROW_COL),
            over_axes(jnp.sum(previous * image), ROW_COL),
        )
        alpha = cross / count
        residual = image - alpha * vector - beta_prev * previous
        squared = (
            square / count - alpha * alpha - 2.0 * beta_prev * older / count + beta_prev * beta_prev
        )
        beta = jnp.sqrt(squared + EPS)
        previous = vector
        vector = residual / beta
        beta_prev = beta
        values.append(alpha)
        values.append(beta)
    return (vector, jnp.stack(values))


def solution(mesh):
    finer = Mesh(mesh.devices.reshape(8, 2, 4, 8), ("row_0", "row_1", "col_0", "col_1"))
    placed = (P(ROW, COL), P(ROW), P(COL), P(ROW, COL), P(COL, ROW), P(ROW, COL))
    return jax.shard_map(
        shards, mesh=finer, in_specs=placed, out_specs=(P(ROW, COL), P()), check_vma=False
    )
```

profile of v0, /device:TPU:1, one launch (start us, length us, event | category | flops | bytes accessed | tf_op | source)
XLA Modules:
  0.0 346.9 jit_solution(16004232356385606627)
XLA Ops:
  2.0 15.3 %psum.196 = f32[]{:T(128)} all-reduce(f32[]{:T(128)} %multiply_reduce_fusion.6), channel_id=1, replica_groups=mesh['row_0'=8,'row_1'=2,'col_0'=4,'col_1'=8] {'row_0'}, use_global_device_ids=true, to_apply=%region_1.0 | all-reduce | flops 1 | bytes 8 | tf_op jit(solution)/shard_map/psum | solution.py:51
  17.3 9.1 %psum.197 = f32[]{:T(128)} all-reduce(f32[]{:T(128)} %psum.196), channel_id=1, replica_groups=mesh['row_0'=8,'row_1'=2,'col_0'=4,'col_1'=8] {'row_1'}, use_global_device_ids=true, to_apply=%region_2.0 | all-reduce | flops 1 | bytes 8 | tf_op jit(solution)/shard_map/psum | solution.py:51
  26.4 7.2 %psum.198 = f32[]{:T(128)} all-reduce(f32[]{:T(128)} %psum.197), channel_id=1, replica_groups=mesh['row_0'=8,'row_1'=2,'col_0'=4,'col_1'=8] {'col_0'}, use_global_device_ids=true, to_apply=%region_3.0 | all-reduce | flops 1 | bytes 8 | tf_op jit(solution)/shard_map/psum | solution.py:51
  33.6 20.0 %psum.199 = f32[]{:T(128)} all-reduce(f32[]{:T(128)} %psum.198), channel_id=1, replica_groups=mesh['row_0'=8,'row_1'=2,'col_0'=4,'col_1'=8] {'col_1'}, use_global_device_ids=true, to_apply=%region_4.0 | all-reduce | flops 1 | bytes 8 | tf_op jit(solution)/shard_map/psum | solution.py:51
  54.7 12.6 %all_to_all.42 = f32[32,1,2048]{2,1,0:T(1,128)S(1)} all-to-all(f32[32,1,2048]{2,1,0:T(1,128)S(1)} %reshape.44), channel_id=1, replica_groups=mesh['row_0'=8,'row_1'=2,'col_0'=4,'col_1'=8] {'col_0','col_1'}, dimensions={0} | all-to-all | bytes 524288 | tf_op jit(solution)/shard_map/all_to_all | solution.py:22
  67.4 28.9 %all_to_all.43 = f32[16,128,64]{1,2,0:T(8,128)S(1)} all-to-all(f32[16,128,64]{1,2,0:T(8,128)S(1)} %broadcast_in_dim.11), channel_id=1, replica_groups=mesh['row_0'=8,'row_1'=2,'col_0'=4,'col_1'=8] {'row_0','row_1'}, dimensions={0} | all-to-all | bytes 1048576 | tf_op jit(solution)/shard_map/all_to_all | solution.py:22
  97.5 4.4 %all-to-all-start.2 = ((f32[32,256,32]{1,2,0:T(8,128)}), f32[32,256,32]{1,2,0:T(8,128)S(1)}, u32[]{:S(2)}, u32[]{:S(2)}) async-start(f32[32,256,32]{1,2,0:T(8,128)} %broadcast_in_dim.12), calls=%async_computation.2 | async-start | bytes 2097152 | tf_op jit(solution)/shard_map/all_to_all | solution.py:22
  104.9 16.0 %all_gather.6 = f32[1024,128]{1,0:T(8,128)S(1)} all-gather(f32[64,128]{1,0:T(8,128)S(1)} %fusion.4), channel_id=1, replica_groups=mesh['row_0'=8,'row_1'=2,'col_0'=4,'col_1'=8] {'row_0','row_1'}, dimensions={0}, use_global_device_ids=true | all-gather | bytes 557056 | tf_op jit(solution)/shard_map/all_gather | solution.py:68
  120.9 9.0 %all-to-all-done.2 = f32[32,256,32]{1,2,0:T(8,128)S(1)} async-done(((f32[32,256,32]{1,2,0:T(8,128)}), f32[32,256,32]{1,2,0:T(8,128)S(1)}, u32[]{:S(2)}, u32[]{:S(2)}) %all-to-all-start.2) | async-done | bytes 1048608 | tf_op jit(solution)/shard_map/all_to_all | solution.py:22
  133.2 21.1 %all_to_all.44 = f32[16,64,128]{2,1,0:T(8,128)S(1)} all-to-all(f32[16,64,128]{2,1,0:T(8,128)S(1)} %bitcast.89), channel_id=1, replica_groups=mesh['row_0'=8,'row_1'=2,'col_0'=4,'col_1'=8] {'row_0','row_1'}, dimensions={0} | all-to-all | bytes 1048576 | tf_op jit(solution)/shard_map/all_to_all | solution.py:46
  155.5 15.9 %all_to_all.45 = f32[32,1,2048]{2,1,0:T(1,128)S(1)} all-to-all(f32[32,1,2048]{2,1,0:T(1,128)S(1)} %reshape.46), channel_id=1, replica_groups=mesh['row_0'=8,'row_1'=2,'col_0'=4,'col_1'=8] {'col_0','col_1'}, dimensions={0} | all-to-all | bytes 524288 | tf_op jit(solution)/shard_map/all_to_all | solution.py:46
  174.4 11.6 %all-reduce.3 = (f32[]{:T(128)}, f32[]{:T(128)}, f32[]{:T(128)}) all-reduce(f32[]{:T(128)} %get-tuple-element.6, f32[]{:T(128)} %get-tuple-element.7, f32[]{:T(128)} %get-tuple-element.5), channel_id=1, replica_groups=mesh['row_0'=8,'row_1'=2,'col_0'=4,'col_1'=8] {'row_0'}, use_global_device_ids=true, to_apply=%region_13.0 | all-reduce | flops 3 | bytes 24 | tf_op jit(solution)/shard_map/psum | solution.py:51
  186.0 7.2 %all-reduce.7 = (f32[]{:T(128)}, f32[]{:T(128)}, f32[]{:T(128)}) all-reduce(f32[]{:T(128)} %get-tuple-element.17, f32[]{:T(128)} %get-tuple-element.18, f32[]{:T(128)} %get-tuple-element.19), channel_id=1, replica_groups=mesh['row_0'=8,'row_1'=2,'col_0'=4,'col_1'=8] {'row_1'}, use_global_device_ids=true, to_apply=%region_14.0 | all-reduce | flops 3 | bytes 24 | tf_op jit(solution)/shard_map/psum | solution.py:51
  193.1 7.6 %all-reduce.5 = (f32[]{:T(128)}, f32[]{:T(128)}, f32[]{:T(128)}) all-reduce(f32[]{:T(128)} %get-tuple-element.29, f32[]{:T(128)} %get-tuple-element.30, f32[]{:T(128)} %get-tuple-element.31), channel_id=1, replica_groups=mesh['row_0'=8,'row_1'=2,'col_0'=4,'col_1'=8] {'col_0'}, use_global_device_ids=true, to_apply=%region_15.0 | all-reduce | flops 3 | bytes 24 | tf_op jit(solution)/shard_map/psum | solution.py:51
  200.7 12.7 %all-reduce.1 = (f32[]{:T(128)}, f32[]{:T(128)}, f32[]{:T(128)}) all-reduce(f32[]{:T(128)} %get-tuple-element.23, f32[]{:T(128)} %get-tuple-element.24, f32[]{:T(128)} %get-tuple-element.25), channel_id=1, replica_groups=mesh['row_0'=8,'row_1'=2,'col_0'=4,'col_1'=8] {'col_1'}, use_global_device_ids=true, to_apply=%region_16.0 | all-reduce | flops 3 | bytes 24 | tf_op jit(solution)/shard_map/psum | solution.py:51
  217.1 14.1 %all_to_all.46 = f32[32,1,2048]{2,1,0:T(1,128)S(1)} all-to-all(f32[32,1,2048]{2,1,0:T(1,128)S(1)} %reshape.48), channel_id=1, replica_groups=mesh['row_0'=8,'row_1'=2,'col_0'=4,'col_1'=8] {'col_0','col_1'}, dimensions={0} | all-to-all | bytes 524288 | tf_op jit(solution)/shard_map/all_to_all | solution.py:22
  233.7 24.8 %all_gather.7 = f32[1024,128]{1,0:T(8,128)S(1)} all-gather(f32[64,128]{1,0:T(8,128)S(1)} %fusion.5), channel_id=1, replica_groups=mesh['row_0'=8,'row_1'=2,'col_0'=4,'col_1'=8] {'row_0','row_1'}, dimensions={0}, use_global_device_ids=true | all-gather | bytes 557056 | tf_op jit(solution)/shard_map/all_gather | solution.py:68
  261.8 22.1 %all_to_all.47 = f32[16,64,128]{2,1,0:T(8,128)S(1)} all-to-all(f32[16,64,128]{2,1,0:T(8,128)S(1)} %bitcast.91), channel_id=1, replica_groups=mesh['row_0'=8,'row_1'=2,'col_0'=4,'col_1'=8] {'row_0','row_1'}, dimensions={0} | all-to-all | bytes 1048576 | tf_op jit(solution)/shard_map/all_to_all | solution.py:46
  285.7 4.4 %all-to-all-start.7 = ((f32[32,1,2048]{2,1,0:T(1,128)}), f32[32,1,2048]{2,1,0:T(1,128)S(1)}, u32[]{:S(2)}, u32[]{:S(2)}) async-start(f32[32,1,2048]{2,1,0:T(1,128)} %reshape.50), calls=%async_computation.7 | async-start | bytes 524288 | tf_op jit(solution)/shard_map/all_to_all | solution.py:46
  290.1 11.3 %all-to-all-done.7 = f32[32,1,2048]{2,1,0:T(1,128)S(1)} async-done(((f32[32,1,2048]{2,1,0:T(1,128)}), f32[32,1,2048]{2,1,0:T(1,128)S(1)}, u32[]{:S(2)}, u32[]{:S(2)}) %all-to-all-start.7) | async-done | bytes 262176 | tf_op jit(solution)/shard_map/all_to_all | solution.py:46
  303.6 11.6 %all-reduce.2 = (f32[]{:T(128)}, f32[]{:T(128)}, f32[]{:T(128)}) all-reduce(f32[]{:T(128)} %get-tuple-element.3, f32[]{:T(128)} %get-tuple-element.4, f32[]{:T(128)} %get-tuple-element.2), channel_id=1, replica_groups=mesh['row_0'=8,'row_1'=2,'col_0'=4,'col_1'=8] {'row_0'}, use_global_device_ids=true, to_apply=%region_30.0 | all-reduce | flops 3 | bytes 24 | tf_op jit(solution)/shard_map/psum | solution.py:51
  315.3 7.1 %all-reduce.6 = (f32[]{:T(128)}, f32[]{:T(128)}, f32[]{:T(128)}) all-reduce(f32[]{:T(128)} %get-tuple-element.14, f32[]{:T(128)} %get-tuple-element.15, f32[]{:T(128)} %get-tuple-element.16), channel_id=1, replica_groups=mesh['row_0'=8,'row_1'=2,'col_0'=4,'col_1'=8] {'row_1'}, use_global_device_ids=true, to_apply=%region_31.0 | all-reduce | flops 3 | bytes 24 | tf_op jit(solution)/shard_map/psum | solution.py:51
  322.3 7.6 %all-reduce.4 = (f32[]{:T(128)}, f32[]{:T(128)}, f32[]{:T(128)}) all-reduce(f32[]{:T(128)} %get-tuple-element.26, f32[]{:T(128)} %get-tuple-element.27, f32[]{:T(128)} %get-tuple-element.28), channel_id=1, replica_groups=mesh['row_0'=8,'row_1'=2,'col_0'=4,'col_1'=8] {'col_0'}, use_global_device_ids=true, to_apply=%region_32.0 | all-reduce | flops 3 | bytes 24 | tf_op jit(solution)/shard_map/psum | solution.py:51
  329.9 12.7 %all-reduce = (f32[]{:T(128)}, f32[]{:T(128)}, f32[]{:T(128)}) all-reduce(f32[]{:T(128)} %get-tuple-element.20, f32[]{:T(128)} %get-tuple-element.21, f32[]{:T(128)} %get-tuple-element.22), channel_id=1, replica_groups=mesh['row_0'=8,'row_1'=2,'col_0'=4,'col_1'=8] {'col_1'}, use_global_device_ids=true, to_apply=%region_33.0 | all-reduce | flops 3 | bytes 24 | tf_op jit(solution)/shard_map/psum | solution.py:51
  (52 shorter events, 24.8 us)
Async XLA Ops:
  0.6 53.7 %copy-start = (f32[64,32]{0,1:T(8,128)S(1)}, f32[64,32]{0,1:T(8,128)}, u32[]{:S(2)}) copy-start(f32[64,32]{0,1:T(8,128)} %param.6) | copy-start | bytes 24580
  54.7 12.6 %copy-start.2 = (f32[128,64]{0,1:T(8,128)S(1)}, f32[128,64]{0,1:T(8,128)}, u32[]{:S(2)}) copy-start(f32[128,64]{0,1:T(8,128)} %param.10) | copy-start | bytes 98308
  67.4 28.9 %copy-start.3 = (f32[256,32]{0,1:T(8,128)S(1)}, f32[256,32]{0,1:T(8,128)}, u32[]{:S(2)}) copy-start(f32[256,32]{0,1:T(8,128)} %param.9) | copy-start | bytes 98308
  97.5 32.5 %all-to-all-start.2 = ((f32[32,256,32]{1,2,0:T(8,128)}), f32[32,256,32]{1,2,0:T(8,128)S(1)}, u32[]{:S(2)}, u32[]{:S(2)}) async-start(f32[32,256,32]{1,2,0:T(8,128)} %broadcast_in_dim.12), calls=%async_computation.2 | async-start | bytes 2097152 | tf_op jit(solution)/shard_map/all_to_all | solution.py:22
  104.9 25.1 %copy-start.1 = (f32[256,128]{1,0:T(8,128)S(1)}, f32[256,128]{1,0:T(8,128)}, u32[]{:S(2)}) copy-start(f32[256,128]{1,0:T(8,128)} %param.11) | copy-start | bytes 393220
  172.9 0.7 copy-start.4
  173.0 0.7 copy-start.5
  285.7 15.7 %all-to-all-start.7 = ((f32[32,1,2048]{2,1,0:T(1,128)}), f32[32,1,2048]{2,1,0:T(1,128)S(1)}, u32[]{:S(2)}, u32[]{:S(2)}) async-start(f32[32,1,2048]{2,1,0:T(1,128)} %reshape.50), calls=%async_computation.7 | async-start | bytes 524288 | tf_op jit(solution)/shard_map/all_to_all | solution.py:46
where the time goes:
time: 353 us; the launch traced here: 347 us
  blocking collectives  285 us (81%)
  waiting for transfers between devices  20.3 us (6%)
  matrix products  9.45 us (3%)
  other arithmetic  9.38 us (3%)
  starting transfers between devices  8.75 us (2%)
  between operations  7.88 us (2%)
  local copies, waits for them, and re-layouts  6.02 us (2%)
    psum x12, blocking collectives, over_axes(): return functools.reduce(lax.psum, axes, value)  130 us
    all_to_all x3, blocking collectives, sum_at_owner(): lax.all_to_all(parts, axis, split_axis=0, concat_axis=0, tiled=True)  59.1 us
    all_to_all x3, blocking collectives, copy_for_each(): lax.all_to_all(jnp.broadcast_to(value[None], (size, *value.shape)), axis,...  55.7 us
    all_gather x2, blocking collectives, shards(): image_columns = lax.all_gather(image_block, ROW, axis=0, tiled=True)  40.8 us
    all_to_all x1, waiting for transfers between devices, sum_at_owner(): lax.all_to_all(parts, axis, split_axis=0, concat_axis=0, tiled=True)  11.3 us
    all_to_all x1, waiting for transfers between devices, copy_for_each(): lax.all_to_all(jnp.broadcast_to(value[None], (size, *value.shape)), axis,...  9.01 us
  transfers between devices with their start and end apart: 2, of which 2 were waited for; matrix products, arithmetic and copies ran while one was open for 1% of the time, Pallas kernels for 0%

commit v1 on v0

v1 whole, which is shorter than its diff:
```python
import jax
import jax.numpy as jnp
from jax import lax
from jax.sharding import Mesh
from jax.sharding import PartitionSpec as P

NV = 1024
NC = 1024
COUNT = NV * NC
COL = ("col_0", "col_1")
ROW = ("row_0", "row_1")
EPS = 1e-06
SHIFT = 4.0
HIGH = lax.Precision.HIGHEST


def exchange(value, axis):
    return lax.all_to_all(value, axis, 0, 0, tiled=True)


def copies(value, axis):
    size = lax.axis_size(axis)
    return exchange(jnp.broadcast_to(value[None], (size, *value.shape)), axis)


def pack(block):
    return jnp.concatenate([block[:16], block[16:]], axis=1)


def unpack(packed):
    return jnp.concatenate([packed[:, :64], packed[:, 64:]], axis=0)


def dot(a, b, dims):
    return lax.dot_general(a, b, (dims, ((), ())), precision=HIGH)


def points_of(gathered, lo, hi):
    return dot(gathered[:, :64], lo, ((0,), (0,))) + dot(gathered[:, 64:], hi, ((0,), (0,)))


def shards(excitons, valence_energy, conduction_energy, psi_valence, psi_conduction, screened):
    x = pack(excitons.T)
    gap = pack(conduction_energy[:, None] - valence_energy[None, :]) - SHIFT
    panel_valence = copies(psi_valence.T, COL).reshape(1024, 256)
    panel_conduction = lax.all_gather(psi_conduction.T, ROW, axis=0, tiled=True)
    halves = panel_conduction.reshape(32, 2, 16, 128)
    lo = halves[:, 0].reshape(512, 128)
    hi = halves[:, 1].reshape(512, 128)

    def middle(image):
        points = dot(panel_valence, image, ((0,), (0,)))
        back = dot(panel_valence, points * screened, ((1,), (0,)))
        back = exchange(back.reshape(16, 64, 128), ROW).sum(axis=0)
        kernel = jnp.concatenate(
            [dot(lo, back, ((1,), (1,))), dot(hi, back, ((1,), (1,)))], axis=1
        )
        return exchange(kernel.reshape(32, 16, 128), COL).sum(axis=0)

    x_rows = copies(x, COL).reshape(512, 128)
    image = lax.all_gather(points_of(x_rows, lo, hi), ROW, axis=0, tiled=True)
    y = gap * x - middle(image)

    y_rows = copies(y, COL).reshape(512, 128)
    sums = jnp.stack(
        [
            jnp.sum(x_rows * x_rows, axis=0),
            jnp.sum(x_rows * y_rows, axis=0),
            jnp.sum(y_rows * y_rows, axis=0),
        ]
    )
    sums = jnp.pad(sums, ((0, 5), (0, 0)))
    message = jnp.concatenate([points_of(y_rows, lo, hi), sums], axis=0)
    arrived = lax.all_gather(message, ROW, axis=0, tiled=True).reshape(16, 72, 128)
    moments = jnp.sum(arrived[:, 64:], axis=(0, 2)) / COUNT
    z = gap * y - middle(arrived[:, :64].reshape(1024, 128))

    inverse = 1.0 / jnp.sqrt(moments[0] + EPS)
    first_norm = moments[0] * inverse * inverse
    first_cross = moments[1] * inverse * inverse
    alpha_1 = first_cross + SHIFT * first_norm
    rest_1 = alpha_1 - SHIFT
    beta_1 = jnp.sqrt(
        moments[2] * inverse * inverse
        - 2.0 * rest_1 * first_cross
        + rest_1 * rest_1 * first_norm
        + EPS
    )
    q_1 = x * inverse
    scale = inverse / beta_1
    q_2 = (y - rest_1 * x) * scale
    u = (z - rest_1 * y) * scale - beta_1 * q_1
    parts = jnp.stack(
        [
            jnp.sum(u * u, axis=0),
            jnp.sum(u * q_2, axis=0),
            jnp.sum(q_2 * q_2, axis=0),
            jnp.sum(q_1 * q_2, axis=0),
        ]
    )
    parts = copies(jnp.pad(parts, ((0, 4), (0, 0))), ROW).sum(axis=0)
    parts = copies(parts, COL).sum(axis=0)
    parts = jnp.sum(parts, axis=1) / COUNT
    uu, uq, qq, oq = parts[0], parts[1], parts[2], parts[3]
    alpha_2 = uq + beta_1 * oq + SHIFT * qq
    rest_2 = alpha_2 - SHIFT
    beta_2 = jnp.sqrt(uu - 2.0 * rest_2 * uq + rest_2 * rest_2 * qq + EPS)
    q_3 = (u - rest_2 * q_2) / beta_2
    return unpack(q_3).T, jnp.stack([alpha_1, beta_1, alpha_2, beta_2])


def solution(mesh):
    finer = Mesh(mesh.devices.reshape(8, 2, 4, 8), ("row_0", "row_1", "col_0", "col_1"))
    placed = (P(ROW, COL), P(ROW), P(COL), P(ROW, COL), P(COL, ROW), P(ROW, COL))
    return jax.shard_map(
        shards, mesh=finer, in_specs=placed, out_specs=(P(ROW, COL), P()), check_vma=False
    )
```

time: 353 us -> 228 us (0.65); the launches traced: 347 us -> 227 us
  blocking collectives: 285 us -> 164 us
  starting transfers between devices: 8.75 us -> 20.3 us
  other arithmetic: 9.38 us -> 2.14 us
    psum x12 -> x0, blocking collectives: 130 us -> none  [over_axes(): return functools.reduce(lax.psum, axes, value)]
    all_gather x2 -> x3, blocking collectives: 40.8 us -> 56.5 us  [the longest x1 20.7 us: shards(): panel_conduction = lax.all_gather(psi_conduction.T, ROW, axis=0, tiled=True)]
    all_to_all x2 -> x3, starting transfers between devices: 8.75 us -> 20.3 us  [exchange(): return lax.all_to_all(value, axis, 0, 0, tiled=True)]
    all_to_all x6, blocking collectives: 115 us -> 107 us  [exchange(): return lax.all_to_all(value, axis, 0, 0, tiled=True)]
    all_to_all x4 -> x0, other arithmetic: 5.03 us -> none  [the longest x2 2.51 us: sum_at_owner(): lax.all_to_all(parts, axis, split_axis=0, concat_axis=0, tiled=True)]
    all_to_all x2 -> x3, waiting for transfers between devices: 20.3 us -> 19 us  [exchange(): return lax.all_to_all(value, axis, 0, 0, tiled=True)]
    dot_general x8 -> x12, matrix products: 9.45 us -> 8.55 us  [dot(): return lax.dot_general(a, b, (dims, ((), ())), precision=HIGH)]
  transfers between devices with their start and end apart: 2 -> 3, of which waited for: 2 -> 2; matrix products, arithmetic and copies ran while one was open for 1% -> 1% of each run, Pallas kernels for 0% -> 0%
where the time goes in v1:
time: 228 us; the launch traced here: 227 us
  blocking collectives  164 us (72%)
  starting transfers between devices  20.3 us (9%)
  waiting for transfers between devices  19 us (8%)
  matrix products  8.55 us (4%)
  between operations  7.36 us (3%)
  local copies, waits for them, and re-layouts  6.17 us (3%)
    all_to_all x6, blocking collectives, exchange(): return lax.all_to_all(value, axis, 0, 0, tiled=True)  107 us
    all_gather x1, blocking collectives, shards(): panel_conduction = lax.all_gather(psi_conduction.T, ROW, axis=0, tiled=True)  20.7 us
    all_to_all x3, starting transfers between devices, exchange(): return lax.all_to_all(value, axis, 0, 0, tiled=True)  20.3 us
    all_gather x1, blocking collectives, shards(): lax.all_gather(message, ROW, axis=0, tiled=True).reshape(16, 72, 128)  19.5 us
    all_to_all x3, waiting for transfers between devices, exchange(): return lax.all_to_all(value, axis, 0, 0, tiled=True)  19 us
    all_gather x1, blocking collectives, shards(): image = lax.all_gather(points_of(x_rows, lo, hi), ROW, axis=0, tiled=True)  16.4 us
    dot_general x12, matrix products, dot(): return lax.dot_general(a, b, (dims, ((), ())), precision=HIGH)  8.55 us
  transfers between devices with their start and end apart: 3, of which 2 were waited for; matrix products, arithmetic and copies ran while one was open for 1% of the time, Pallas kernels for 0%

profile of v1, /device:TPU:1, one launch (start us, length us, event | category | flops | bytes accessed | tf_op | source)
XLA Modules:
  0.0 227.1 jit_solution(8264259051333897023)
XLA Ops:
  0.6 0.7 fusion.10
  1.5 23.2 %all_to_all.45 = f32[32,16,128]{2,1,0:T(8,128)S(1)} all-to-all(f32[32,16,128]{2,1,0:T(8,128)S(1)} %broadcast_in_dim.10), channel_id=1, replica_groups=mesh['row_0'=8,'row_1'=2,'col_0'=4,'col_1'=8] {'col_0','col_1'}, dimensions={0} | all-to-all | bytes 524288 | tf_op jit(solution)/shard_map/all_to_all | solution.py:18
  24.7 1.1 broadcast_in_dim.11
  25.8 6.4 %all-to-all-start.1 = ((f32[32,32,256]{2,1,0:T(8,128)}), f32[32,32,256]{2,1,0:T(8,128)S(1)}, u32[]{:S(2)}, u32[]{:S(2)}) async-start(f32[32,32,256]{2,1,0:T(8,128)} %broadcast_in_dim.11), calls=%async_computation.1 | async-start | bytes 2097152 | tf_op jit(solution)/shard_map/all_to_all | solution.py:18
  33.0 20.7 %all_gather.9 = f32[1024,128]{1,0:T(8,128)S(1)} all-gather(f32[64,128]{1,0:T(8,128)S(1)} %bitcast.98), channel_id=1, replica_groups=mesh['row_0'=8,'row_1'=2,'col_0'=4,'col_1'=8] {'row_0','row_1'}, dimensions={0}, use_global_device_ids=true | all-gather | bytes 557056 | tf_op jit(solution)/shard_map/all_gather | solution.py:46
  54.3 0.7 convolution_add_fusion.1
  55.0 16.4 %all_gather.10 = f32[1024,128]{1,0:T(8,128)S(1)} all-gather(f32[64,128]{1,0:T(8,128)S(1)} %convolution_add_fusion.1), channel_id=1, replica_groups=mesh['row_0'=8,'row_1'=2,'col_0'=4,'col_1'=8] {'row_0','row_1'}, dimensions={0}, use_global_device_ids=true | all-gather | bytes 557056 | tf_op jit(solution)/shard_map/all_gather | solution.py:61
  71.3 1.0 fusion.1
  72.4 1.2 convolution_bitcast_fusion.1
  73.8 22.1 %all_to_all.46 = f32[16,64,128]{2,1,0:T(8,128)S(1)} all-to-all(f32[16,64,128]{2,1,0:T(8,128)S(1)} %bitcast.95), channel_id=1, replica_groups=mesh['row_0'=8,'row_1'=2,'col_0'=4,'col_1'=8] {'row_0','row_1'}, dimensions={0} | all-to-all | bytes 1048576 | tf_op jit(solution)/shard_map/all_to_all | solution.py:18
  96.8 0.8 copy.14
  97.6 9.6 %all-to-all-start.3 = ((f32[32,16,128]{2,1,0:T(8,128)}), f32[32,16,128]{2,1,0:T(8,128)S(1)}, u32[]{:S(2)}, u32[]{:S(2)}) async-start(f32[32,16,128]{2,1,0:T(8,128)} %bitcast.13), calls=%async_computation.3 | async-start | bytes 524288 | tf_op jit(solution)/shard_map/all_to_all | solution.py:18
  107.3 11.2 %all-to-all-done.3 = f32[32,16,128]{2,1,0:T(8,128)S(1)} async-done(((f32[32,16,128]{2,1,0:T(8,128)}), f32[32,16,128]{2,1,0:T(8,128)S(1)}, u32[]{:S(2)}, u32[]{:S(2)}) %all-to-all-start.3) | async-done | bytes 262176 | tf_op jit(solution)/shard_map/all_to_all | solution.py:18
  118.7 14.6 %all_to_all.47 = f32[32,16,128]{2,1,0:T(8,128)S(1)} all-to-all(f32[32,16,128]{2,1,0:T(8,128)S(1)} %broadcast_in_dim.12), channel_id=1, replica_groups=mesh['row_0'=8,'row_1'=2,'col_0'=4,'col_1'=8] {'col_0','col_1'}, dimensions={0} | all-to-all | bytes 524288 | tf_op jit(solution)/shard_map/all_to_all | solution.py:18
  133.9 0.7 convolution_add_fusion
  134.7 19.5 %all_gather.11 = f32[1152,128]{1,0:T(8,128)S(1)} all-gather(f32[72,128]{1,0:T(8,128)S(1)} %pad_maximum_fusion.2), channel_id=1, replica_groups=mesh['row_0'=8,'row_1'=2,'col_0'=4,'col_1'=8] {'row_0','row_1'}, dimensions={0}, use_global_device_ids=true | all-gather | bytes 626688 | tf_op jit(solution)/shard_map/all_gather | solution.py:74
  154.2 1.0 fusion
  155.3 1.2 convolution_bitcast_fusion
  156.7 21.8 %all_to_all.48 = f32[16,64,128]{2,1,0:T(8,128)S(1)} all-to-all(f32[16,64,128]{2,1,0:T(8,128)S(1)} %bitcast.96), channel_id=1, replica_groups=mesh['row_0'=8,'row_1'=2,'col_0'=4,'col_1'=8] {'row_0','row_1'}, dimensions={0} | all-to-all | bytes 1048576 | tf_op jit(solution)/shard_map/all_to_all | solution.py:18
  179.4 0.8 copy.17
  180.2 4.2 %all-to-all-start.6 = ((f32[32,16,128]{2,1,0:T(8,128)}), f32[32,16,128]{2,1,0:T(8,128)S(1)}, u32[]{:S(2)}, u32[]{:S(2)}) async-start(f32[32,16,128]{2,1,0:T(8,128)} %bitcast.25), calls=%async_computation.6 | async-start | bytes 524288 | tf_op jit(solution)/shard_map/all_to_all | solution.py:18
  187.9 7.8 %all-to-all-done.6 = f32[32,16,128]{2,1,0:T(8,128)S(1)} async-done(((f32[32,16,128]{2,1,0:T(8,128)}), f32[32,16,128]{2,1,0:T(8,128)S(1)}, u32[]{:S(2)}, u32[]{:S(2)}) %all-to-all-start.6) | async-done | bytes 262176 | tf_op jit(solution)/shard_map/all_to_all | solution.py:18
  195.9 12.2 %all_to_all.49 = f32[16,8,128]{2,1,0:T(8,128)S(1)} all-to-all(f32[16,8,128]{2,1,0:T(8,128)S(1)} %broadcast_in_dim.13), channel_id=1, replica_groups=mesh['row_0'=8,'row_1'=2,'col_0'=4,'col_1'=8] {'row_0','row_1'}, dimensions={0} | all-to-all | bytes 131072 | tf_op jit(solution)/shard_map/all_to_all | solution.py:18
  208.1 13.1 %all_to_all.50 = f32[32,8,128]{2,1,0:T(8,128)S(1)} all-to-all(f32[32,8,128]{2,1,0:T(8,128)S(1)} %broadcast_in_dim.14), channel_id=1, replica_groups=mesh['row_0'=8,'row_1'=2,'col_0'=4,'col_1'=8] {'col_0','col_1'}, dimensions={0} | all-to-all | bytes 262144 | tf_op jit(solution)/shard_map/all_to_all | solution.py:18
  (52 shorter events, 7.5 us)
Async XLA Ops:
  1.4 23.2 %copy-start.1 = (f32[256,32]{0,1:T(8,128)S(1)}, f32[256,32]{0,1:T(8,128)}, u32[]{:S(2)}) copy-start(f32[256,32]{0,1:T(8,128)} %param.9) | copy-start | bytes 98308
  25.8 6.4 %copy-start = (f32[256,128]{1,0:T(8,128)S(1)}, f32[256,128]{1,0:T(8,128)}, u32[]{:S(2)}) copy-start(f32[256,128]{1,0:T(8,128)} %param.11) | copy-start | bytes 393220
  25.8 45.6 %all-to-all-start.1 = ((f32[32,32,256]{2,1,0:T(8,128)}), f32[32,32,256]{2,1,0:T(8,128)S(1)}, u32[]{:S(2)}, u32[]{:S(2)}) async-start(f32[32,32,256]{2,1,0:T(8,128)} %broadcast_in_dim.11), calls=%async_computation.1 | async-start | bytes 2097152 | tf_op jit(solution)/shard_map/all_to_all | solution.py:18
  32.2 0.8 copy-start.2
  97.6 9.7 %copy-start.3 = (f32[64]{0:T(128)S(1)}, f32[64]{0:T(128)}, u32[]{:S(2)}) copy-start(f32[64]{0:T(128)} %param.7) | copy-start | bytes 772
  97.6 9.7 %copy-start.4 = (f32[32]{0:T(128)S(1)}, f32[32]{0:T(128)}, u32[]{:S(2)}) copy-start(f32[32]{0:T(128)} %param.8) | copy-start | bytes 388
  97.6 20.9 %all-to-all-start.3 = ((f32[32,16,128]{2,1,0:T(8,128)}), f32[32,16,128]{2,1,0:T(8,128)S(1)}, u32[]{:S(2)}, u32[]{:S(2)}) async-start(f32[32,16,128]{2,1,0:T(8,128)} %bitcast.13), calls=%async_computation.3 | async-start | bytes 524288 | tf_op jit(solution)/shard_map/all_to_all | solution.py:18
  180.2 15.5 %all-to-all-start.6 = ((f32[32,16,128]{2,1,0:T(8,128)}), f32[32,16,128]{2,1,0:T(8,128)S(1)}, u32[]{:S(2)}, u32[]{:S(2)}) async-start(f32[32,16,128]{2,1,0:T(8,128)} %bitcast.25), calls=%async_computation.6 | async-start | bytes 524288 | tf_op jit(solution)/shard_map/all_to_all | solution.py:18

commit v2 on v1

--- a/solution.py
+++ b/solution.py
@@ -42,13 +42,12 @@
 def shards(excitons, valence_energy, conduction_energy, psi_valence, psi_conduction, screened):
     x = pack(excitons.T)
     gap = pack(conduction_energy[:, None] - valence_energy[None, :]) - SHIFT
-    panel_valence = copies(psi_valence.T, COL).reshape(1024, 256)
     panel_conduction = lax.all_gather(psi_conduction.T, ROW, axis=0, tiled=True)
     halves = panel_conduction.reshape(32, 2, 16, 128)
     lo = halves[:, 0].reshape(512, 128)
     hi = halves[:, 1].reshape(512, 128)
 
-    def middle(image):
+    def middle(image, panel_valence):
         points = dot(panel_valence, image, ((0,), (0,)))
         back = dot(panel_valence, points * screened, ((1,), (0,)))
         back = exchange(back.reshape(16, 64, 128), ROW).sum(axis=0)
@@ -58,8 +57,10 @@
         return exchange(kernel.reshape(32, 16, 128), COL).sum(axis=0)
 
     x_rows = copies(x, COL).reshape(512, 128)
-    image = lax.all_gather(points_of(x_rows, lo, hi), ROW, axis=0, tiled=True)
-    y = gap * x - middle(image)
+    first, own_valence = lax.optimization_barrier((points_of(x_rows, lo, hi), psi_valence.T))
+    panel_valence = copies(own_valence, COL).reshape(1024, 256)
+    image = lax.all_gather(first, ROW, axis=0, tiled=True)
+    y = gap * x - middle(image, panel_valence)
 
     y_rows = copies(y, COL).reshape(512, 128)
     sums = jnp.stack(
@@ -73,7 +74,7 @@
     message = jnp.concatenate([points_of(y_rows, lo, hi), sums], axis=0)
     arrived = lax.all_gather(message, ROW, axis=0, tiled=True).reshape(16, 72, 128)
     moments = jnp.sum(arrived[:, 64:], axis=(0, 2)) / COUNT
-    z = gap * y - middle(arrived[:, :64].reshape(1024, 128))
+    z = gap * y - middle(arrived[:, :64].reshape(1024, 128), panel_valence)
 
     inverse = 1.0 / jnp.sqrt(moments[0] + EPS)
     first_norm = moments[0] * inverse * inverse
@@ -91,17 +92,12 @@
     q_2 = (y - rest_1 * x) * scale
     u = (z - rest_1 * y) * scale - beta_1 * q_1
     parts = jnp.stack(
-        [
-            jnp.sum(u * u, axis=0),
-            jnp.sum(u * q_2, axis=0),
-            jnp.sum(q_2 * q_2, axis=0),
-            jnp.sum(q_1 * q_2, axis=0),
-        ]
+        [jnp.sum(u * u), jnp.sum(u * q_2), jnp.sum(q_2 * q_2), jnp.sum(q_1 * q_2)]
     )
-    parts = copies(jnp.pad(parts, ((0, 4), (0, 0))), ROW).sum(axis=0)
-    parts = copies(parts, COL).sum(axis=0)
-    parts = jnp.sum(parts, axis=1) / COUNT
-    uu, uq, qq, oq = parts[0], parts[1], parts[2], parts[3]
+    parts = jnp.repeat(parts, 32)
+    parts = copies(parts, ROW).sum(axis=0)
+    parts = copies(parts, COL).sum(axis=0) / COUNT
+    uu, uq, qq, oq = parts[0], parts[32], parts[64], parts[96]
     alpha_2 = uq + beta_1 * oq + SHIFT * qq
     rest_2 = alpha_2 - SHIFT
     beta_2 = jnp.sqrt(uu - 2.0 * rest_2 * uq + rest_2 * rest_2 * qq + EPS)

time: 228 us -> 231 us (1.013)
  blocking collectives: 164 us -> 142 us
  starting transfers between devices: 20.3 us -> 32.5 us
  waiting for transfers between devices: 19 us -> 27.5 us
  other arithmetic: 2.14 us -> 5.29 us
    all_to_all x6 -> x5, blocking collectives: 107 us -> 86.1 us  [exchange(): return lax.all_to_all(value, axis, 0, 0, tiled=True)]
    all_to_all x3 -> x4, starting transfers between devices: 20.3 us -> 32.5 us  [exchange(): return lax.all_to_all(value, axis, 0, 0, tiled=True)]
    all_to_all x3 -> x4, waiting for transfers between devices: 19 us -> 27.5 us  [exchange(): return lax.all_to_all(value, axis, 0, 0, tiled=True)]
    another operation x1, other arithmetic: 0.01 us -> 2.62 us  [shards(): jnp.stack([jnp.sum(u * u), jnp.sum(u * q_2), jnp.sum(q_2 * q_2), jnp.sum(...]
  transfers between devices with their start and end apart: 3 -> 4, of which waited for: 2 -> 3; matrix products, arithmetic and copies ran while one was open for 1% -> 0% of each run, Pallas kernels for 0% -> 0%
where the time goes in v2:
time: 231 us
  blocking collectives  142 us (61%)
  starting transfers between devices  32.5 us (14%)
  waiting for transfers between devices  27.5 us (12%)
  matrix products  9.68 us (4%)
  between operations  7.34 us (3%)
  local copies, waits for them, and re-layouts  5.95 us (3%)
  other arithmetic  5.29 us (2%)
    all_to_all x5, blocking collectives, exchange(): return lax.all_to_all(value, axis, 0, 0, tiled=True)  86.1 us
    all_to_all x4, starting transfers between devices, exchange(): return lax.all_to_all(value, axis, 0, 0, tiled=True)  32.5 us
    all_to_all x4, waiting for transfers between devices, exchange(): return lax.all_to_all(value, axis, 0, 0, tiled=True)  27.5 us
    all_gather x1, blocking collectives, shards(): panel_conduction = lax.all_gather(psi_conduction.T, ROW, axis=0, tiled=True)  19.8 us
    all_gather x1, blocking collectives, shards(): lax.all_gather(message, ROW, axis=0, tiled=True).reshape(16, 72, 128)  19.5 us
    all_gather x1, blocking collectives, shards(): image = lax.all_gather(first, ROW, axis=0, tiled=True)  16.8 us
    dot_general x12, matrix products, dot(): return lax.dot_general(a, b, (dims, ((), ())), precision=HIGH)  9.68 us
  transfers between devices with their start and end apart: 4, of which 3 were waited for; matrix products, arithmetic and copies ran while one was open for 0% of the time, Pallas kernels for 0%

profile of v2, /device:TPU:1, one launch (start us, length us, event | category | flops | bytes accessed | tf_op | source)
XLA Modules:
  0.0 230.5 jit_solution(7902089509263625893)
XLA Ops:
  2.1 13.8 %all-to-all-start = ((f32[32,16,128]{2,1,0:T(8,128)}), f32[32,16,128]{2,1,0:T(8,128)S(1)}, u32[]{:S(2)}, u32[]{:S(2)}) async-start(f32[32,16,128]{2,1,0:T(8,128)} %broadcast_in_dim.14), calls=%async_computation | async-start | bytes 524288 | tf_op jit(solution)/shard_map/all_to_all | solution.py:18
  16.0 19.8 %all_gather.9 = f32[1024,128]{1,0:T(8,128)S(1)} all-gather(f32[64,128]{1,0:T(8,128)S(1)} %bitcast.89), channel_id=1, replica_groups=mesh['row_0'=8,'row_1'=2,'col_0'=4,'col_1'=8] {'row_0','row_1'}, dimensions={0}, use_global_device_ids=true | all-gather | bytes 557056 | tf_op jit(solution)/shard_map/all_gather | solution.py:45
  37.2 1.1 broadcast_in_dim.15
  38.3 9.5 %all-to-all-start.1 = ((f32[32,32,256]{2,1,0:T(8,128)}), f32[32,32,256]{2,1,0:T(8,128)S(1)}, u32[]{:S(2)}, u32[]{:S(2)}) async-start(f32[32,32,256]{2,1,0:T(8,128)} %broadcast_in_dim.15), calls=%async_computation.1 | async-start | bytes 2097152 | tf_op jit(solution)/shard_map/all_to_all | solution.py:18
  47.9 16.8 %all_gather.10 = f32[1024,128]{1,0:T(8,128)S(1)} all-gather(f32[64,128]{1,0:T(8,128)S(1)} %convolution_add_fusion.1), channel_id=1, replica_groups=mesh['row_0'=8,'row_1'=2,'col_0'=4,'col_1'=8] {'row_0','row_1'}, dimensions={0}, use_global_device_ids=true | all-gather | bytes 557056 | tf_op jit(solution)/shard_map/all_gather | solution.py:62
  64.6 8.5 %all-to-all-done.1 = f32[32,32,256]{2,1,0:T(8,128)S(1)} async-done(((f32[32,32,256]{2,1,0:T(8,128)}), f32[32,32,256]{2,1,0:T(8,128)S(1)}, u32[]{:S(2)}, u32[]{:S(2)}) %all-to-all-start.1) | async-done | bytes 1048608 | tf_op jit(solution)/shard_map/all_to_all | solution.py:18
  73.1 1.8 fusion.1
  74.9 1.0 fusion.14
  75.9 25.7 %all_to_all.47 = f32[16,64,128]{2,1,0:T(8,128)S(1)} all-to-all(f32[16,64,128]{2,1,0:T(8,128)S(1)} %fusion.14), channel_id=1, replica_groups=mesh['row_0'=8,'row_1'=2,'col_0'=4,'col_1'=8] {'row_0','row_1'}, dimensions={0} | all-to-all | bytes 1048576 | tf_op jit(solution)/shard_map/all_to_all | solution.py:18
  102.5 0.8 copy.12
  103.3 5.0 %all-to-all-start.3 = ((f32[32,16,128]{2,1,0:T(8,128)}), f32[32,16,128]{2,1,0:T(8,128)S(1)}, u32[]{:S(2)}, u32[]{:S(2)}) async-start(f32[32,16,128]{2,1,0:T(8,128)} %bitcast.12), calls=%async_computation.3 | async-start | bytes 524288 | tf_op jit(solution)/shard_map/all_to_all | solution.py:18
  108.4 11.2 %all-to-all-done.3 = f32[32,16,128]{2,1,0:T(8,128)S(1)} async-done(((f32[32,16,128]{2,1,0:T(8,128)}), f32[32,16,128]{2,1,0:T(8,128)S(1)}, u32[]{:S(2)}, u32[]{:S(2)}) %all-to-all-start.3) | async-done | bytes 262176 | tf_op jit(solution)/shard_map/all_to_all | solution.py:18
  119.7 14.6 %all_to_all.48 = f32[32,16,128]{2,1,0:T(8,128)S(1)} all-to-all(f32[32,16,128]{2,1,0:T(8,128)S(1)} %broadcast_in_dim.16), channel_id=1, replica_groups=mesh['row_0'=8,'row_1'=2,'col_0'=4,'col_1'=8] {'col_0','col_1'}, dimensions={0} | all-to-all | bytes 524288 | tf_op jit(solution)/shard_map/all_to_all | solution.py:18
  135.7 19.5 %all_gather.11 = f32[1152,128]{1,0:T(8,128)S(1)} all-gather(f32[72,128]{1,0:T(8,128)S(1)} %pad_maximum_fusion.2), channel_id=1, replica_groups=mesh['row_0'=8,'row_1'=2,'col_0'=4,'col_1'=8] {'row_0','row_1'}, dimensions={0}, use_global_device_ids=true | all-gather | bytes 626688 | tf_op jit(solution)/shard_map/all_gather | solution.py:75
  155.3 1.8 fusion
  157.1 1.0 fusion.15
  158.1 21.8 %all_to_all.49 = f32[16,64,128]{2,1,0:T(8,128)S(1)} all-to-all(f32[16,64,128]{2,1,0:T(8,128)S(1)} %fusion.15), channel_id=1, replica_groups=mesh['row_0'=8,'row_1'=2,'col_0'=4,'col_1'=8] {'row_0','row_1'}, dimensions={0} | all-to-all | bytes 1048576 | tf_op jit(solution)/shard_map/all_to_all | solution.py:18
  180.8 0.8 copy.13
  181.6 4.2 %all-to-all-start.6 = ((f32[32,16,128]{2,1,0:T(8,128)}), f32[32,16,128]{2,1,0:T(8,128)S(1)}, u32[]{:S(2)}, u32[]{:S(2)}) async-start(f32[32,16,128]{2,1,0:T(8,128)} %bitcast.22), calls=%async_computation.6 | async-start | bytes 524288 | tf_op jit(solution)/shard_map/all_to_all | solution.py:18
  189.3 7.8 %all-to-all-done.6 = f32[32,16,128]{2,1,0:T(8,128)S(1)} async-done(((f32[32,16,128]{2,1,0:T(8,128)}), f32[32,16,128]{2,1,0:T(8,128)S(1)}, u32[]{:S(2)}, u32[]{:S(2)}) %all-to-all-start.6) | async-done | bytes 262176 | tf_op jit(solution)/shard_map/all_to_all | solution.py:18
  197.1 0.8 multiply_reduce_fusion.6
  197.9 2.6 %pad_maximum_fusion.4 = f32[4]{0:T(128)S(1)} fusion(f32[1]{0:T(128)} %bitcast.29, f32[1]{0:T(128)} %bitcast.28, f32[1]{0:T(128)} %bitcast.27, f32[1]{0:T(128)} %bitcast.26), kind=kLoop, calls=%fused_computation.38 | loop fusion | flops 12 | bytes 32 | tf_op jit(solution)/shard_map/stack | solution.py:94
  200.7 11.4 %all_to_all.50 = f32[16,1,128]{2,1,0:T(1,128)S(1)} all-to-all(f32[16,1,128]{2,1,0:T(1,128)S(1)} %broadcast_in_dim.19), channel_id=1, replica_groups=mesh['row_0'=8,'row_1'=2,'col_0'=4,'col_1'=8] {'row_0','row_1'}, dimensions={0} | all-to-all | bytes 16384 | tf_op jit(solution)/shard_map/all_to_all | solution.py:18
  212.2 12.6 %all_to_all.51 = f32[32,1,128]{2,1,0:T(1,128)S(1)} all-to-all(f32[32,1,128]{2,1,0:T(1,128)S(1)} %broadcast_in_dim.20), channel_id=1, replica_groups=mesh['row_0'=8,'row_1'=2,'col_0'=4,'col_1'=8] {'col_0','col_1'}, dimensions={0} | all-to-all | bytes 32768 | tf_op jit(solution)/shard_map/all_to_all | solution.py:18
  (52 shorter events, 9.2 us)
Async XLA Ops:
  2.1 13.9 %copy-start.1 = (f32[128,64]{0,1:T(8,128)S(1)}, f32[128,64]{0,1:T(8,128)}, u32[]{:S(2)}) copy-start(f32[128,64]{0,1:T(8,128)} %param.10) | copy-start | bytes 98308
  2.1 33.7 %all-to-all-start = ((f32[32,16,128]{2,1,0:T(8,128)}), f32[32,16,128]{2,1,0:T(8,128)S(1)}, u32[]{:S(2)}, u32[]{:S(2)}) async-start(f32[32,16,128]{2,1,0:T(8,128)} %broadcast_in_dim.14), calls=%async_computation | async-start | bytes 524288 | tf_op jit(solution)/shard_map/all_to_all | solution.py:18
  36.5 0.8 copy-start.2
  38.3 34.8 %all-to-all-start.1 = ((f32[32,32,256]{2,1,0:T(8,128)}), f32[32,32,256]{2,1,0:T(8,128)S(1)}, u32[]{:S(2)}, u32[]{:S(2)}) async-start(f32[32,32,256]{2,1,0:T(8,128)} %broadcast_in_dim.15), calls=%async_computation.1 | async-start | bytes 2097152 | tf_op jit(solution)/shard_map/all_to_all | solution.py:18
  47.8 25.3 %copy-start = (f32[256,128]{1,0:T(8,128)S(1)}, f32[256,128]{1,0:T(8,128)}, u32[]{:S(2)}) copy-start(f32[256,128]{1,0:T(8,128)} %param.11) | copy-start | bytes 393220
  103.3 5.0 %copy-start.3 = (f32[64]{0:T(128)S(1)}, f32[64]{0:T(128)}, u32[]{:S(2)}) copy-start(f32[64]{0:T(128)} %param.7) | copy-start | bytes 772
  103.3 5.0 %copy-start.4 = (f32[32]{0:T(128)S(1)}, f32[32]{0:T(128)}, u32[]{:S(2)}) copy-start(f32[32]{0:T(128)} %param.8) | copy-start | bytes 388
  103.3 16.2 %all-to-all-start.3 = ((f32[32,16,128]{2,1,0:T(8,128)}), f32[32,16,128]{2,1,0:T(8,128)S(1)}, u32[]{:S(2)}, u32[]{:S(2)}) async-start(f32[32,16,128]{2,1,0:T(8,128)} %bitcast.12), calls=%async_computation.3 | async-start | bytes 524288 | tf_op jit(solution)/shard_map/all_to_all | solution.py:18
  181.6 15.5 %all-to-all-start.6 = ((f32[32,16,128]{2,1,0:T(8,128)}), f32[32,16,128]{2,1,0:T(8,128)S(1)}, u32[]{:S(2)}, u32[]{:S(2)}) async-start(f32[32,16,128]{2,1,0:T(8,128)} %bitcast.22), calls=%async_computation.6 | async-start | bytes 524288 | tf_op jit(solution)/shard_map/all_to_all | solution.py:18

commit v3 on v2

v3 whole, which is shorter than its diff:
```python
import jax
import jax.numpy as jnp
from jax import lax
from jax.experimental import pallas as pl
from jax.experimental.pallas import tpu as pltpu
from jax.sharding import Mesh
from jax.sharding import PartitionSpec as P

NV = 1024
NC = 1024
COUNT = NV * NC
COL = ("col_0", "col_1")
ROW = ("row_0", "row_1")
EPS = 1e-06
SHIFT = 4.0
HIGH = lax.Precision.HIGHEST
F32 = jnp.float32


def exchange(value, axis):
    return lax.all_to_all(value, axis, 0, 0, tiled=True)


def copies(value, axis):
    size = lax.axis_size(axis)
    return exchange(jnp.broadcast_to(value[None], (size, *value.shape)), axis)


def dot(a, b, left, right):
    return lax.dot_general(
        a, b, (((left,), (right,)), ((), ())), precision=HIGH, preferred_element_type=F32
    )


def call(body, outs, name, smem=()):
    shapes = tuple(jax.ShapeDtypeStruct(s, F32) for s in outs)
    specs = tuple(
        pl.BlockSpec(memory_space=pltpu.SMEM if i in smem else pltpu.VMEM)
        for i in range(len(outs))
    )
    return pl.pallas_call(
        body,
        out_shape=shapes,
        out_specs=specs,
        name=name,
        compiler_params=pltpu.CompilerParams(vmem_limit_bytes=32 * 1024 * 1024),
    )


def start_body(block, packed, spread):
    value = jnp.concatenate([block[0:16, :], block[16:32, :]], axis=1)
    packed[...] = value
    spread[...] = jnp.broadcast_to(value[None], spread.shape)


def points_of(rows, panel):
    lo = dot(rows, panel[:, 0].reshape(512, 128), 0, 0)
    hi = dot(rows, panel[:, 1].reshape(512, 128), 0, 0)
    return lo[0:64] + hi[64:128]


def first_points_body(rows, panel, out):
    out[...] = points_of(rows[...].reshape(512, 128), panel)


def second_points_body(x_rows, y_rows, panel, out):
    x = x_rows[...].reshape(512, 128)
    y = y_rows[...].reshape(512, 128)
    out[0:64, :] = points_of(y, panel)
    out[64:65, :] = jnp.sum(x * x, axis=0, keepdims=True)
    out[65:66, :] = jnp.sum(x * y, axis=0, keepdims=True)
    out[66:67, :] = jnp.sum(y * y, axis=0, keepdims=True)
    out[67:72, :] = jnp.zeros((5, 128), F32)


def weigh(image, panel, screened, out):
    points = dot(panel, image, 0, 0)
    out[...] = dot(panel, points * screened, 1, 0).reshape(16, 64, 128)


def first_weigh_body(image, panel, screened, out):
    weigh(image[...], panel[...], screened[...], out)


def second_weigh_body(arrived, panel, screened, out, moments):
    image = arrived[:, 0:64, :].reshape(1024, 128)
    weigh(image, panel[...], screened[...], out)
    moments[...] = jnp.sum(arrived[:, 64:72, :], axis=0)


def conduct_body(parts, panel, out):
    back = jnp.sum(parts[...], axis=0)
    zero = jnp.zeros_like(back)
    lo = dot(panel[:, 0].reshape(512, 128), jnp.concatenate([back, zero], axis=0), 1, 1)
    hi = dot(panel[:, 1].reshape(512, 128), jnp.concatenate([zero, back], axis=0), 1, 1)
    out[...] = (lo + hi).reshape(32, 16, 128)


def update_body(parts, gap, x, packed, spread):
    value = gap[...] * x[...] - jnp.sum(parts[...], axis=0)
    packed[...] = value
    spread[...] = jnp.broadcast_to(value[None], spread.shape)


def total(value):
    return jnp.sum(jnp.sum(value, axis=0, keepdims=True), axis=1, keepdims=True)


def last_body(parts, gap, x, y, moments, u_out, q_out, message, scalars):
    norm = total(moments[0:1, :]) / COUNT
    inverse = 1.0 / jnp.sqrt(norm + EPS)
    first_norm = norm * inverse * inverse
    first_cross = total(moments[1:2, :]) / COUNT * inverse * inverse
    alpha = first_cross + SHIFT * first_norm
    rest = alpha - SHIFT
    beta = jnp.sqrt(
        total(moments[2:3, :]) / COUNT * inverse * inverse
        - 2.0 * rest * first_cross
        + rest * rest * first_norm
        + EPS
    )
    z = gap[...] * y[...] - jnp.sum(parts[...], axis=0)
    q_1 = x[...] * inverse
    scale = inverse / beta
    q_2 = (y[...] - rest * x[...]) * scale
    u = (z - rest * y[...]) * scale - beta * q_1
    u_out[...] = u
    q_out[...] = q_2
    lane = lax.broadcasted_iota(jnp.int32, (1, 128), 1)
    row = jnp.where(lane < 32, total(u * u), total(u * q_2))
    row = jnp.where(lane < 64, row, jnp.where(lane < 96, total(q_2 * q_2), total(q_1 * q_2)))
    message[...] = jnp.broadcast_to(row[None], message.shape)
    scalars[...] = jnp.where(lane < 64, alpha, beta)


def fold_body(parts, message):
    row = jnp.sum(parts[...], axis=0)
    message[...] = jnp.broadcast_to(row[None], message.shape)


def finish_body(parts, u, q_2, scalars, out, coefficients):
    row = jnp.sum(parts[...], axis=0) / COUNT
    uu, uq, qq, oq = row[:, 0:1], row[:, 32:33], row[:, 64:65], row[:, 96:97]
    beta_1 = scalars[:, 64:65]
    alpha = uq + beta_1 * oq + SHIFT * qq
    rest = alpha - SHIFT
    beta = jnp.sqrt(uu - 2.0 * rest * uq + rest * rest * qq + EPS)
    value = (u[...] - rest * q_2[...]) / beta
    out[0:16, :] = value[:, 0:64]
    out[16:32, :] = value[:, 64:128]
    coefficients[0] = scalars[0, 0]
    coefficients[1] = scalars[0, 64]
    coefficients[2] = alpha[0, 0]
    coefficients[3] = beta[0, 0]


def shards(excitons, valence_energy, conduction_energy, psi_valence, psi_conduction, screened):
    x, spread = call(start_body, [(16, 128), (32, 16, 128)], "start")(excitons.T)
    gap = conduction_energy[:, None] - valence_energy[None, :] - SHIFT
    gap = jnp.concatenate([gap[:16], gap[16:]], axis=1)
    x_rows = exchange(spread, COL)
    panel_valence = copies(psi_valence.T, COL).reshape(1024, 256)
    panel_conduction = lax.all_gather(psi_conduction.T, ROW, axis=0, tiled=True)
    panel_conduction = panel_conduction.reshape(32, 2, 16, 128)

    def returned(back):
        back = exchange(back, ROW)
        (kernel,) = call(conduct_body, [(32, 16, 128)], "conduct")(back, panel_conduction)
        return exchange(kernel, COL)

    (image,) = call(first_points_body, [(64, 128)], "points_one")(x_rows, panel_conduction)
    image = lax.all_gather(image, ROW, axis=0, tiled=True)
    (back,) = call(first_weigh_body, [(16, 64, 128)], "weigh_one")(image, panel_valence, screened)
    y, spread = call(update_body, [(16, 128), (32, 16, 128)], "update")(returned(back), gap, x)

    y_rows = exchange(spread, COL)
    (image,) = call(second_points_body, [(72, 128)], "points_two")(x_rows, y_rows, panel_conduction)
    image = lax.all_gather(image, ROW, axis=0, tiled=True).reshape(16, 72, 128)
    back, moments = call(second_weigh_body, [(16, 64, 128), (8, 128)], "weigh_two")(
        image, panel_valence, screened
    )
    u, q_2, message, scalars = call(
        last_body, [(16, 128), (16, 128), (16, 1, 128), (1, 128)], "last"
    )(returned(back), gap, x, y, moments)
    (message,) = call(fold_body, [(32, 1, 128)], "fold")(exchange(message, ROW))
    out, coefficients = call(finish_body, [(32, 64), (4,)], "finish", smem=(1,))(
        exchange(message, COL), u, q_2, scalars
    )
    return out.T, coefficients


def solution(mesh):
    finer = Mesh(mesh.devices.reshape(8, 2, 4, 8), ("row_0", "row_1", "col_0", "col_1"))
    placed = (P(ROW, COL), P(ROW), P(COL), P(ROW, COL), P(COL, ROW), P(ROW, COL))
    return jax.shard_map(
        shards, mesh=finer, in_specs=placed, out_specs=(P(ROW, COL), P()), check_vma=False
    )
```

time: 231 us -> 220 us (0.952)
  blocking collectives: 142 us -> 178 us
  starting transfers between devices: 32.5 us -> 16.1 us
  waiting for transfers between devices: 27.5 us -> 11.1 us
  Pallas kernels: 0 us -> 11.5 us
  matrix products: 9.68 us -> 0 us
  between operations: 7.34 us -> 0.75 us
  other arithmetic: 5.29 us -> 0.15 us
  local copies, waits for them, and re-layouts: 5.95 us -> 1.84 us
    all_to_all x5 -> x7, blocking collectives: 86.1 us -> 121 us  [exchange(): return lax.all_to_all(value, axis, 0, 0, tiled=True)]
    all_to_all x4 -> x2, starting transfers between devices: 32.5 us -> 16.1 us  [exchange(): return lax.all_to_all(value, axis, 0, 0, tiled=True)]
    all_to_all x4 -> x2, waiting for transfers between devices: 27.5 us -> 11.1 us  [exchange(): return lax.all_to_all(value, axis, 0, 0, tiled=True)]
    pallas_call x0 -> x11, Pallas kernels: none -> 11.5 us  [the longest x1 3.53 us: shards(): call(first_weigh_body, [(16, 64, 128)], 'weigh_one')]
    dot_general x12 -> x0, matrix products: 9.68 us -> none  [dot(): return lax.dot_general(a, b, (dims, ((), ())), precision=HIGH)]
    another operation x3 -> x0, other arithmetic: 3.21 us -> none  [the longest x1 2.62 us: shards(): jnp.stack([jnp.sum(u * u), jnp.sum(u * q_2), jnp.sum(q_2 * q_2), jnp.sum(...]
  transfers between devices with their start and end apart: 4 -> 2, of which waited for: 3 -> 1; matrix products, arithmetic and copies ran while one was open for 0% -> 0% of each run, Pallas kernels for 0% -> 0%
where the time goes in v3:
time: 220 us; the launch traced here: 219 us
  blocking collectives  178 us (81%)
  starting transfers between devices  16.1 us (7%)
  Pallas kernels  11.5 us (5%)
  waiting for transfers between devices  11.1 us (5%)
    all_to_all x7, blocking collectives, exchange(): return lax.all_to_all(value, axis, 0, 0, tiled=True)  121 us
    all_gather x1, blocking collectives, shards(): panel_conduction = lax.all_gather(psi_conduction.T, ROW, axis=0, tiled=True)  20.7 us
    all_gather x1, blocking collectives, shards(): image = lax.all_gather(image, ROW, axis=0, tiled=True).reshape(16, 72, 128)  19.5 us
    all_gather x1, blocking collectives, shards(): image = lax.all_gather(image, ROW, axis=0, tiled=True)  16.5 us
    all_to_all x2, starting transfers between devices, exchange(): return lax.all_to_all(value, axis, 0, 0, tiled=True)  16.1 us
    all_to_all x2, waiting for transfers between devices, exchange(): return lax.all_to_all(value, axis, 0, 0, tiled=True)  11.1 us
  transfers between devices with their start and end apart: 2, of which 1 were waited for; matrix products, arithmetic and copies ran while one was open for 0% of the time, Pallas kernels for 0%

profile of v3, /device:TPU:1, one launch (start us, length us, event | category | flops | bytes accessed | tf_op | source)
XLA Modules:
  0.0 219.2 jit_solution(311443587368990375)
XLA Ops:
  0.6 0.7 copy-done.1
  1.3 0.1 start.1
  1.4 23.2 %all_to_all.45.rows.x_rows = f32[32,16,128]{2,1,0:T(8,128)S(1)} all-to-all(f32[32,16,128]{2,1,0:T(8,128)S(1)} %get-tuple-element.14), channel_id=1, replica_groups=mesh['row_0'=8,'row_1'=2,'col_0'=4,'col_1'=8] {'col_0','col_1'}, dimensions={0} | all-to-all | bytes 524288 | tf_op jit(solution)/shard_map/all_to_all | solution.py:21
  24.7 1.1 broadcast_in_dim.2
  25.8 6.4 %all-to-all-start.1 = ((f32[32,32,256]{2,1,0:T(8,128)}), f32[32,32,256]{2,1,0:T(8,128)S(1)}, u32[]{:S(2)}, u32[]{:S(2)}) async-start(f32[32,32,256]{2,1,0:T(8,128)} %broadcast_in_dim.2), calls=%async_computation.1 | async-start | bytes 2097152 | tf_op jit(solution)/shard_map/all_to_all | solution.py:21
  32.2 20.7 %all_gather.9 = f32[1024,128]{1,0:T(8,128)S(1)} all-gather(f32[64,128]{1,0:T(8,128)S(1)} %bitcast.16), channel_id=1, replica_groups=mesh['row_0'=8,'row_1'=2,'col_0'=4,'col_1'=8] {'row_0','row_1'}, dimensions={0}, use_global_device_ids=true | all-gather | bytes 557056 | tf_op jit(solution)/shard_map/all_gather | solution.py:163
  52.9 0.6 points_one.1
  53.5 16.5 %all_gather.10.image = f32[1024,128]{1,0:T(8,128)S(1)} all-gather(f32[64,128]{1,0:T(8,128)S(1)} %points_one.1), channel_id=1, replica_groups=mesh['row_0'=8,'row_1'=2,'col_0'=4,'col_1'=8] {'row_0','row_1'}, dimensions={0}, use_global_device_ids=true | all-gather | bytes 557056 | tf_op jit(solution)/shard_map/all_gather | solution.py:172
  70.0 3.5 %weigh_one.1 = f32[16,64,128]{2,1,0:T(8,128)S(1)} custom-call(f32[1024,128]{1,0:T(8,128)S(1)} %all_gather.10.image, f32[1024,256]{1,0:T(8,128)S(1)} %bitcast.11, f32[256,128]{1,0:T(8,128)S(1)} %copy-done), custom_call_target="tpu_custom_call" | custom-call | tf_op jit(solution)/shard_map/weigh_one/pallas_call | solution.py:173
  73.6 22.1 %all_to_all.46.parts = f32[16,64,128]{2,1,0:T(8,128)S(1)} all-to-all(f32[16,64,128]{2,1,0:T(8,128)S(1)} %weigh_one.1), channel_id=1, replica_groups=mesh['row_0'=8,'row_1'=2,'col_0'=4,'col_1'=8] {'row_0','row_1'}, dimensions={0} | all-to-all | bytes 1048576 | tf_op jit(solution)/shard_map/all_to_all | solution.py:21
  95.7 1.3 conduct.2
  97.0 9.6 %all-to-all-start.3 = ((f32[32,16,128]{2,1,0:T(8,128)}), f32[32,16,128]{2,1,0:T(8,128)S(1)}, u32[]{:S(2)}, u32[]{:S(2)}) async-start(f32[32,16,128]{2,1,0:T(8,128)} %conduct.2), calls=%async_computation.3 | async-start | bytes 524288 | tf_op jit(solution)/shard_map/all_to_all | solution.py:21
  106.8 11.1 %all-to-all-done.3.parts = f32[32,16,128]{2,1,0:T(8,128)S(1)} async-done(((f32[32,16,128]{2,1,0:T(8,128)}), f32[32,16,128]{2,1,0:T(8,128)S(1)}, u32[]{:S(2)}, u32[]{:S(2)}) %all-to-all-start.3) | async-done | bytes 262176 | tf_op jit(solution)/shard_map/all_to_all | solution.py:21
  118.0 14.6 %all_to_all.47.y_rows = f32[32,16,128]{2,1,0:T(8,128)S(1)} all-to-all(f32[32,16,128]{2,1,0:T(8,128)S(1)} %get-tuple-element.16), channel_id=1, replica_groups=mesh['row_0'=8,'row_1'=2,'col_0'=4,'col_1'=8] {'col_0','col_1'}, dimensions={0} | all-to-all | bytes 524288 | tf_op jit(solution)/shard_map/all_to_all | solution.py:21
  132.6 0.6 points_two.1
  133.2 19.5 %all_gather.11 = f32[1152,128]{1,0:T(8,128)S(1)} all-gather(f32[72,128]{1,0:T(8,128)S(1)} %points_two.1), channel_id=1, replica_groups=mesh['row_0'=8,'row_1'=2,'col_0'=4,'col_1'=8] {'row_0','row_1'}, dimensions={0}, use_global_device_ids=true | all-gather | bytes 626688 | tf_op jit(solution)/shard_map/all_gather | solution.py:178
  152.7 3.5 %weigh_two.1 = (f32[16,64,128]{2,1,0:T(8,128)S(1)}, f32[8,128]{1,0:T(8,128)S(1)}) custom-call(f32[16,72,128]{2,1,0:T(8,128)S(1)} %bitcast.13, f32[1024,256]{1,0:T(8,128)S(1)} %bitcast.12, f32[256,128]{1,0:T(8,128)S(1)} %copy-done), custom_call_target="tpu_custom_call" | custom-call | tf_op jit(solution)/shard_map/weigh_two/pallas_call | solution.py:179
  156.3 21.8 %all_to_all.48.parts = f32[16,64,128]{2,1,0:T(8,128)S(1)} all-to-all(f32[16,64,128]{2,1,0:T(8,128)S(1)} %get-tuple-element.17), channel_id=1, replica_groups=mesh['row_0'=8,'row_1'=2,'col_0'=4,'col_1'=8] {'row_0','row_1'}, dimensions={0} | all-to-all | bytes 1048576 | tf_op jit(solution)/shard_map/all_to_all | solution.py:21
  178.1 0.6 conduct.3
  178.7 15.3 %all_to_all.49.parts = f32[32,16,128]{2,1,0:T(8,128)S(1)} all-to-all(f32[32,16,128]{2,1,0:T(8,128)S(1)} %conduct.3), channel_id=1, replica_groups=mesh['row_0'=8,'row_1'=2,'col_0'=4,'col_1'=8] {'col_0','col_1'}, dimensions={0} | all-to-all | bytes 524288 | tf_op jit(solution)/shard_map/all_to_all | solution.py:21
  194.0 0.2 last.1
  194.2 11.4 %all_to_all.50.parts = f32[16,1,128]{2,1,0:T(1,128)S(1)} all-to-all(f32[16,1,128]{2,1,0:T(1,128)S(1)} %get-tuple-element.20), channel_id=1, replica_groups=mesh['row_0'=8,'row_1'=2,'col_0'=4,'col_1'=8] {'row_0','row_1'}, dimensions={0} | all-to-all | bytes 16384 | tf_op jit(solution)/shard_map/all_to_all | solution.py:21
  205.6 12.6 %all_to_all.51.parts = f32[32,1,128]{2,1,0:T(1,128)S(1)} all-to-all(f32[32,1,128]{2,1,0:T(1,128)S(1)} %fold.1), channel_id=1, replica_groups=mesh['row_0'=8,'row_1'=2,'col_0'=4,'col_1'=8] {'col_0','col_1'}, dimensions={0} | all-to-all | bytes 32768 | tf_op jit(solution)/shard_map/all_to_all | solution.py:21
  218.2 1.0 finish.1
  (17 shorter events, 0.3 us)
Async XLA Ops:
  0.6 0.7 copy-start.1
  1.4 23.2 %copy-start.2 = (f32[256,32]{0,1:T(8,128)S(1)}, f32[256,32]{0,1:T(8,128)}, u32[]{:S(2)}) copy-start(f32[256,32]{0,1:T(8,128)} %param.9) | copy-start | bytes 98308
  25.8 6.4 %copy-start.3 = (f32[128,64]{0,1:T(8,128)S(1)}, f32[128,64]{0,1:T(8,128)}, u32[]{:S(2)}) copy-start(f32[128,64]{0,1:T(8,128)} %param.10) | copy-start | bytes 98308
  25.8 44.3 %all-to-all-start.1 = ((f32[32,32,256]{2,1,0:T(8,128)}), f32[32,32,256]{2,1,0:T(8,128)S(1)}, u32[]{:S(2)}, u32[]{:S(2)}) async-start(f32[32,32,256]{2,1,0:T(8,128)} %broadcast_in_dim.2), calls=%async_computation.1 | async-start | bytes 2097152 | tf_op jit(solution)/shard_map/all_to_all | solution.py:21
  53.5 16.5 %copy-start = (f32[256,128]{1,0:T(8,128)S(1)}, f32[256,128]{1,0:T(8,128)}, u32[]{:S(2)}) copy-start(f32[256,128]{1,0:T(8,128)} %screened.3) | copy-start | bytes 393220
  97.0 9.6 %copy-start.4 = (f32[64]{0:T(128)S(1)}, f32[64]{0:T(128)}, u32[]{:S(2)}) copy-start(f32[64]{0:T(128)} %param.7) | copy-start | bytes 772
  97.0 9.7 %copy-start.5 = (f32[32]{0:T(128)S(1)}, f32[32]{0:T(128)}, u32[]{:S(2)}) copy-start(f32[32]{0:T(128)} %param.8) | copy-start | bytes 388
  97.0 20.9 %all-to-all-start.3 = ((f32[32,16,128]{2,1,0:T(8,128)}), f32[32,16,128]{2,1,0:T(8,128)S(1)}, u32[]{:S(2)}, u32[]{:S(2)}) async-start(f32[32,16,128]{2,1,0:T(8,128)} %conduct.2), calls=%async_computation.3 | async-start | bytes 524288 | tf_op jit(solution)/shard_map/all_to_all | solution.py:21

commit v4 on v3

--- a/solution.py
+++ b/solution.py
@@ -21,11 +21,6 @@
     return lax.all_to_all(value, axis, 0, 0, tiled=True)
 
 
-def copies(value, axis):
-    size = lax.axis_size(axis)
-    return exchange(jnp.broadcast_to(value[None], (size, *value.shape)), axis)
-
-
 def dot(a, b, left, right):
     return lax.dot_general(
         a, b, (((left,), (right,)), ((), ())), precision=HIGH, preferred_element_type=F32
@@ -47,10 +42,12 @@
     )
 
 
-def start_body(block, packed, spread):
+def start_body(block, valence, packed, first, second):
     value = jnp.concatenate([block[0:16, :], block[16:32, :]], axis=1)
     packed[...] = value
-    spread[...] = jnp.broadcast_to(value[None], spread.shape)
+    first[:, 0:16, :] = jnp.broadcast_to(value[None], (32, 16, 128))
+    first[:, 16:48, :] = jnp.broadcast_to(valence[:, 0:128][None], (32, 32, 128))
+    second[...] = jnp.broadcast_to(valence[:, 128:256][None], second.shape)
 
 
 def points_of(rows, panel):
@@ -59,12 +56,12 @@
     return lo[0:64] + hi[64:128]
 
 
-def first_points_body(rows, panel, out):
-    out[...] = points_of(rows[...].reshape(512, 128), panel)
-
-
-def second_points_body(x_rows, y_rows, panel, out):
-    x = x_rows[...].reshape(512, 128)
+def first_points_body(first, panel, out):
+    out[...] = points_of(first[:, 0:16, :].reshape(512, 128), panel)
+
+
+def second_points_body(first, y_rows, panel, out):
+    x = first[:, 0:16, :].reshape(512, 128)
     y = y_rows[...].reshape(512, 128)
     out[0:64, :] = points_of(y, panel)
     out[64:65, :] = jnp.sum(x * x, axis=0, keepdims=True)
@@ -73,18 +70,20 @@
     out[67:72, :] = jnp.zeros((5, 128), F32)
 
 
-def weigh(image, panel, screened, out):
-    points = dot(panel, image, 0, 0)
-    out[...] = dot(panel, points * screened, 1, 0).reshape(16, 64, 128)
-
-
-def first_weigh_body(image, panel, screened, out):
-    weigh(image[...], panel[...], screened[...], out)
-
-
-def second_weigh_body(arrived, panel, screened, out, moments):
-    image = arrived[:, 0:64, :].reshape(1024, 128)
-    weigh(image, panel[...], screened[...], out)
+def weigh(image, first, second, screened, out):
+    panel = jnp.concatenate(
+        [first[:, 16:48, :].reshape(1024, 128), second[...].reshape(1024, 128)], axis=1
+    )
+    points = dot(image.T, panel, 1, 0).T
+    out[...] = dot(panel, points * screened[...], 1, 0).reshape(16, 64, 128)
+
+
+def first_weigh_body(image, first, second, screened, out):
+    weigh(image[...], first, second, screened, out)
+
+
+def second_weigh_body(arrived, first, second, screened, out, moments):
+    weigh(arrived[:, 0:64, :].reshape(1024, 128), first, second, screened, out)
     moments[...] = jnp.sum(arrived[:, 64:72, :], axis=0)
 
 
@@ -96,8 +95,15 @@
     out[...] = (lo + hi).reshape(32, 16, 128)
 
 
-def update_body(parts, gap, x, packed, spread):
-    value = gap[...] * x[...] - jnp.sum(parts[...], axis=0)
+def update_body(parts, valence, conduction, x, packed, spread, gap_out):
+    rows = lax.broadcasted_iota(jnp.int32, (32, 32), 0)
+    lanes = lax.broadcasted_iota(jnp.int32, (32, 32), 1)
+    column = jnp.sum(jnp.where(rows == lanes, conduction[...], 0.0), axis=1, keepdims=True)
+    half = lax.broadcasted_iota(jnp.int32, (16, 128), 1) < 64
+    upper = jnp.where(half, column[0:16], column[16:32])
+    gap = upper - jnp.concatenate([valence[...], valence[...]], axis=1) - SHIFT
+    gap_out[...] = gap
+    value = gap * x[...] - jnp.sum(parts[...], axis=0)
     packed[...] = value
     spread[...] = jnp.broadcast_to(value[None], spread.shape)
 
@@ -155,11 +161,10 @@
 
 
 def shards(excitons, valence_energy, conduction_energy, psi_valence, psi_conduction, screened):
-    x, spread = call(start_body, [(16, 128), (32, 16, 128)], "start")(excitons.T)
-    gap = conduction_energy[:, None] - valence_energy[None, :] - SHIFT
-    gap = jnp.concatenate([gap[:16], gap[16:]], axis=1)
-    x_rows = exchange(spread, COL)
-    panel_valence = copies(psi_valence.T, COL).reshape(1024, 256)
+    x, first, second = call(start_body, [(16, 128), (32, 48, 128), (32, 32, 128)], "start")(
+        excitons.T, psi_valence.T
+    )
+    first = exchange(first, COL)
     panel_conduction = lax.all_gather(psi_conduction.T, ROW, axis=0, tiled=True)
     panel_conduction = panel_conduction.reshape(32, 2, 16, 128)
 
@@ -168,16 +173,20 @@
         (kernel,) = call(conduct_body, [(32, 16, 128)], "conduct")(back, panel_conduction)
         return exchange(kernel, COL)
 
-    (image,) = call(first_points_body, [(64, 128)], "points_one")(x_rows, panel_conduction)
+    (image,) = call(first_points_body, [(64, 128)], "points_one")(first, panel_conduction)
+    image, second = lax.optimization_barrier((image, second))
+    second = exchange(second, COL)
     image = lax.all_gather(image, ROW, axis=0, tiled=True)
-    (back,) = call(first_weigh_body, [(16, 64, 128)], "weigh_one")(image, panel_valence, screened)
-    y, spread = call(update_body, [(16, 128), (32, 16, 128)], "update")(returned(back), gap, x)
+    (back,) = call(first_weigh_body, [(16, 64, 128)], "weigh_one")(image, first, second, screened)
+    y, spread, gap = call(update_body, [(16, 128), (32, 16, 128), (16, 128)], "update")(
+        returned(back), valence_energy[None], conduction_energy[None], x
+    )
 
     y_rows = exchange(spread, COL)
-    (image,) = call(second_points_body, [(72, 128)], "points_two")(x_rows, y_rows, panel_conduction)
+    (image,) = call(second_points_body, [(72, 128)], "points_two")(first, y_rows, panel_conduction)
     image = lax.all_gather(image, ROW, axis=0, tiled=True).reshape(16, 72, 128)
     back, moments = call(second_weigh_body, [(16, 64, 128), (8, 128)], "weigh_two")(
-        image, panel_valence, screened
+        image, first, second, screened
     )
     u, q_2, message, scalars = call(
         last_body, [(16, 128), (16, 128), (16, 1, 128), (1, 128)], "last"

time: 220 us -> 213 us (0.968)
  waiting for transfers between devices: 11.1 us -> 0.01 us
  starting transfers between devices: 16.1 us -> 23.4 us
    all_to_all x2, waiting for transfers between devices: 11.1 us -> 0.01 us  [exchange(): return lax.all_to_all(value, axis, 0, 0, tiled=True)]
    all_to_all x2, starting transfers between devices: 16.1 us -> 23.4 us  [exchange(): return lax.all_to_all(value, axis, 0, 0, tiled=True)]
    all_to_all x7, blocking collectives: 121 us -> 118 us  [exchange(): return lax.all_to_all(value, axis, 0, 0, tiled=True)]
    all_gather x1, blocking collectives: 16.5 us -> 18.7 us  [shards(): image = lax.all_gather(image, ROW, axis=0, tiled=True)]
  transfers between devices with their start and end apart: 2 -> 2, of which waited for: 1 -> 0; matrix products, arithmetic and copies ran while one was open for 0% -> 0% of each run, Pallas kernels for 0% -> 0%
where the time goes in v4:
time: 213 us; the launch traced here: 212 us
  blocking collectives  176 us (83%)
  starting transfers between devices  23.4 us (11%)
  Pallas kernels  9.92 us (5%)
  local copies, waits for them, and re-layouts  2.15 us (1%)
    all_to_all x7, blocking collectives, exchange(): return lax.all_to_all(value, axis, 0, 0, tiled=True)  118 us
    all_to_all x2, starting transfers between devices, exchange(): return lax.all_to_all(value, axis, 0, 0, tiled=True)  23.4 us
    all_gather x1, blocking collectives, shards(): panel_conduction = lax.all_gather(psi_conduction.T, ROW, axis=0, tiled=True)  19.8 us
    all_gather x1, blocking collectives, shards(): image = lax.all_gather(image, ROW, axis=0, tiled=True).reshape(16, 72, 128)  19.5 us
    all_gather x1, blocking collectives, shards(): image = lax.all_gather(image, ROW, axis=0, tiled=True)  18.7 us
  transfers between devices with their start and end apart: 2, of which 0 were waited for; matrix products, arithmetic and copies ran while one was open for 0% of the time, Pallas kernels for 0%

profile of v4, /device:TPU:1, one launch (start us, length us, event | category | flops | bytes accessed | tf_op | source)
XLA Modules:
  0.0 212.1 jit_solution(15654089454505069763)
XLA Ops:
  0.6 0.7 copy-done.1
  1.4 0.7 copy-done.2
  2.1 1.2 start.1
  3.3 13.8 %all-to-all-start = ((f32[32,48,128]{2,1,0:T(8,128)}), f32[32,48,128]{2,1,0:T(8,128)S(1)}, u32[]{:S(2)}, u32[]{:S(2)}) async-start(f32[32,48,128]{2,1,0:T(8,128)} %get-tuple-element.18), calls=%async_computation | async-start | bytes 1572864 | tf_op jit(solution)/shard_map/all_to_all | solution.py:21
  17.1 19.8 %all_gather.9 = f32[1024,128]{1,0:T(8,128)S(1)} all-gather(f32[64,128]{1,0:T(8,128)S(1)} %bitcast.17), channel_id=1, replica_groups=mesh['row_0'=8,'row_1'=2,'col_0'=4,'col_1'=8] {'row_0','row_1'}, dimensions={0}, use_global_device_ids=true | all-gather | bytes 557056 | tf_op jit(solution)/shard_map/all_gather | solution.py:168
  36.9 0.6 points_one.1
  37.6 9.5 %all-to-all-start.1 = ((f32[32,32,128]{2,1,0:T(8,128)}), f32[32,32,128]{2,1,0:T(8,128)S(1)}, u32[]{:S(2)}, u32[]{:S(2)}) async-start(f32[32,32,128]{2,1,0:T(8,128)} %get-tuple-element.21), calls=%async_computation.1 | async-start | bytes 1048576 | tf_op jit(solution)/shard_map/all_to_all | solution.py:21
  47.1 18.7 %all_gather.10.image = f32[1024,128]{1,0:T(8,128)S(1)} all-gather(f32[64,128]{1,0:T(8,128)S(1)} %points_one.1), channel_id=1, replica_groups=mesh['row_0'=8,'row_1'=2,'col_0'=4,'col_1'=8] {'row_0','row_1'}, dimensions={0}, use_global_device_ids=true | all-gather | bytes 557056 | tf_op jit(solution)/shard_map/all_gather | solution.py:179
  65.8 2.5 %weigh_one.1 = f32[16,64,128]{2,1,0:T(8,128)S(1)} custom-call(f32[1024,128]{1,0:T(8,128)S(1)} %all_gather.10.image, f32[32,48,128]{2,1,0:T(8,128)S(1)} %all-to-all-done.first, f32[32,32,128]{2,1,0:T(8,128)S(1)} %all-to-all-done.1.second, f32[256,128]{1,0:T(8,128)S(1)} %copy-done), custom_call_target="tpu_custom_call" | custom-call | tf_op jit(solution)/shard_map/weigh_one/pallas_call | solution.py:180
  68.3 22.1 %all_to_all.45.parts = f32[16,64,128]{2,1,0:T(8,128)S(1)} all-to-all(f32[16,64,128]{2,1,0:T(8,128)S(1)} %weigh_one.1), channel_id=1, replica_groups=mesh['row_0'=8,'row_1'=2,'col_0'=4,'col_1'=8] {'row_0','row_1'}, dimensions={0} | all-to-all | bytes 1048576 | tf_op jit(solution)/shard_map/all_to_all | solution.py:21
  90.4 0.6 conduct.2
  91.0 20.1 %all_to_all.46.parts = f32[32,16,128]{2,1,0:T(8,128)S(1)} all-to-all(f32[32,16,128]{2,1,0:T(8,128)S(1)} %conduct.2), channel_id=1, replica_groups=mesh['row_0'=8,'row_1'=2,'col_0'=4,'col_1'=8] {'col_0','col_1'}, dimensions={0} | all-to-all | bytes 524288 | tf_op jit(solution)/shard_map/all_to_all | solution.py:21
  111.1 0.7 copy-done.3
  111.9 14.6 %all_to_all.47.y_rows = f32[32,16,128]{2,1,0:T(8,128)S(1)} all-to-all(f32[32,16,128]{2,1,0:T(8,128)S(1)} %get-tuple-element.23), channel_id=1, replica_groups=mesh['row_0'=8,'row_1'=2,'col_0'=4,'col_1'=8] {'col_0','col_1'}, dimensions={0} | all-to-all | bytes 524288 | tf_op jit(solution)/shard_map/all_to_all | solution.py:21
  126.5 0.6 points_two.1
  127.2 19.5 %all_gather.11 = f32[1152,128]{1,0:T(8,128)S(1)} all-gather(f32[72,128]{1,0:T(8,128)S(1)} %points_two.1), channel_id=1, replica_groups=mesh['row_0'=8,'row_1'=2,'col_0'=4,'col_1'=8] {'row_0','row_1'}, dimensions={0}, use_global_device_ids=true | all-gather | bytes 626688 | tf_op jit(solution)/shard_map/all_gather | solution.py:187
  146.7 2.5 %weigh_two.1 = (f32[16,64,128]{2,1,0:T(8,128)S(1)}, f32[8,128]{1,0:T(8,128)S(1)}) custom-call(f32[16,72,128]{2,1,0:T(8,128)S(1)} %bitcast.12, f32[32,48,128]{2,1,0:T(8,128)S(1)} %all-to-all-done.first, f32[32,32,128]{2,1,0:T(8,128)S(1)} %all-to-all-done.1.second, f32[256,128]{1,0:T(8,128)S(1)} %copy-done), custom_call_target="tpu_custom_call" | custom-call | tf_op jit(solution)/shard_map/weigh_two/pallas_call | solution.py:188
  149.2 21.8 %all_to_all.48.parts = f32[16,64,128]{2,1,0:T(8,128)S(1)} all-to-all(f32[16,64,128]{2,1,0:T(8,128)S(1)} %get-tuple-element.24), channel_id=1, replica_groups=mesh['row_0'=8,'row_1'=2,'col_0'=4,'col_1'=8] {'row_0','row_1'}, dimensions={0} | all-to-all | bytes 1048576 | tf_op jit(solution)/shard_map/all_to_all | solution.py:21
  171.0 0.6 conduct.3
  171.6 15.3 %all_to_all.49.parts = f32[32,16,128]{2,1,0:T(8,128)S(1)} all-to-all(f32[32,16,128]{2,1,0:T(8,128)S(1)} %conduct.3), channel_id=1, replica_groups=mesh['row_0'=8,'row_1'=2,'col_0'=4,'col_1'=8] {'col_0','col_1'}, dimensions={0} | all-to-all | bytes 524288 | tf_op jit(solution)/shard_map/all_to_all | solution.py:21
  186.9 0.2 last.1
  187.1 11.4 %all_to_all.50.parts = f32[16,1,128]{2,1,0:T(1,128)S(1)} all-to-all(f32[16,1,128]{2,1,0:T(1,128)S(1)} %get-tuple-element.28), channel_id=1, replica_groups=mesh['row_0'=8,'row_1'=2,'col_0'=4,'col_1'=8] {'row_0','row_1'}, dimensions={0} | all-to-all | bytes 16384 | tf_op jit(solution)/shard_map/all_to_all | solution.py:21
  198.6 12.6 %all_to_all.51.parts = f32[32,1,128]{2,1,0:T(1,128)S(1)} all-to-all(f32[32,1,128]{2,1,0:T(1,128)S(1)} %fold.1), channel_id=1, replica_groups=mesh['row_0'=8,'row_1'=2,'col_0'=4,'col_1'=8] {'col_0','col_1'}, dimensions={0} | all-to-all | bytes 32768 | tf_op jit(solution)/shard_map/all_to_all | solution.py:21
  211.1 1.0 finish.1
  (13 shorter events, 0.2 us)
Async XLA Ops:
  0.6 0.8 copy-start.1
  1.4 0.7 copy-start.2
  3.3 13.9 %copy-start.5 = (f32[128,64]{0,1:T(8,128)S(1)}, f32[128,64]{0,1:T(8,128)}, u32[]{:S(2)}) copy-start(f32[128,64]{0,1:T(8,128)} %param.10) | copy-start | bytes 98308
  3.3 33.7 %all-to-all-start = ((f32[32,48,128]{2,1,0:T(8,128)}), f32[32,48,128]{2,1,0:T(8,128)S(1)}, u32[]{:S(2)}, u32[]{:S(2)}) async-start(f32[32,48,128]{2,1,0:T(8,128)} %get-tuple-element.18), calls=%async_computation | async-start | bytes 1572864 | tf_op jit(solution)/shard_map/all_to_all | solution.py:21
  37.6 28.2 %all-to-all-start.1 = ((f32[32,32,128]{2,1,0:T(8,128)}), f32[32,32,128]{2,1,0:T(8,128)S(1)}, u32[]{:S(2)}, u32[]{:S(2)}) async-start(f32[32,32,128]{2,1,0:T(8,128)} %get-tuple-element.21), calls=%async_computation.1 | async-start | bytes 1048576 | tf_op jit(solution)/shard_map/all_to_all | solution.py:21
  47.1 18.7 %copy-start = (f32[256,128]{1,0:T(8,128)S(1)}, f32[256,128]{1,0:T(8,128)}, u32[]{:S(2)}) copy-start(f32[256,128]{1,0:T(8,128)} %screened.3) | copy-start | bytes 393220
  111.1 0.7 copy-start.3
  111.1 0.7 copy-start.4

commit v5 on v4

--- a/solution.py
+++ b/solution.py
@@ -27,6 +27,20 @@
     )
 
 
+def halves(value):
+    upper = value.astype(jnp.bfloat16)
+    return upper, (value - upper.astype(F32)).astype(jnp.bfloat16)
+
+
+def dot_halves(a, b):
+    (a_hi, a_lo), (b_hi, b_lo) = a, b
+    return (
+        jnp.dot(a_lo, b_hi, preferred_element_type=F32)
+        + jnp.dot(a_hi, b_lo, preferred_element_type=F32)
+        + jnp.dot(a_hi, b_hi, preferred_element_type=F32)
+    )
+
+
 def call(body, outs, name, smem=()):
     shapes = tuple(jax.ShapeDtypeStruct(s, F32) for s in outs)
     specs = tuple(
@@ -42,12 +56,36 @@
     )
 
 
-def start_body(block, valence, packed, first, second):
+def start_body(
+    block_in, panel_in, valence_in, conduction_in, packed, gap, first, second,
+    block, panel, valence, conduction, arrived,
+):
+    moves = [
+        pltpu.make_async_copy(source, target, arrived.at[i])
+        for i, (source, target) in enumerate(
+            [
+                (block_in, block),
+                (panel_in, panel),
+                (valence_in, valence),
+                (conduction_in, conduction),
+            ]
+        )
+    ]
+    for move in moves:
+        move.start()
+    for move in moves:
+        move.wait()
     value = jnp.concatenate([block[0:16, :], block[16:32, :]], axis=1)
     packed[...] = value
     first[:, 0:16, :] = jnp.broadcast_to(value[None], (32, 16, 128))
-    first[:, 16:48, :] = jnp.broadcast_to(valence[:, 0:128][None], (32, 32, 128))
-    second[...] = jnp.broadcast_to(valence[:, 128:256][None], second.shape)
+    first[:, 16:48, :] = jnp.broadcast_to(panel[:, 0:128][None], (32, 32, 128))
+    second[...] = jnp.broadcast_to(panel[:, 128:256][None], second.shape)
+    rows = lax.broadcasted_iota(jnp.int32, (32, 32), 0)
+    lanes = lax.broadcasted_iota(jnp.int32, (32, 32), 1)
+    column = jnp.sum(jnp.where(rows == lanes, conduction[...], 0.0), axis=1, keepdims=True)
+    half = lax.broadcasted_iota(jnp.int32, (16, 128), 1) < 64
+    upper = jnp.where(half, column[0:16], column[16:32])
+    gap[...] = upper - jnp.concatenate([valence[...], valence[...]], axis=1) - SHIFT
 
 
 def points_of(rows, panel):
@@ -74,8 +112,9 @@
     panel = jnp.concatenate(
         [first[:, 16:48, :].reshape(1024, 128), second[...].reshape(1024, 128)], axis=1
     )
-    points = dot(image.T, panel, 1, 0).T
-    out[...] = dot(panel, points * screened[...], 1, 0).reshape(16, 64, 128)
+    panel = halves(panel)
+    points = dot_halves(halves(image.T), panel).T
+    out[...] = dot_halves(panel, halves(points * screened[...])).reshape(16, 64, 128)
 
 
 def first_weigh_body(image, first, second, screened, out):
@@ -95,15 +134,8 @@
     out[...] = (lo + hi).reshape(32, 16, 128)
 
 
-def update_body(parts, valence, conduction, x, packed, spread, gap_out):
-    rows = lax.broadcasted_iota(jnp.int32, (32, 32), 0)
-    lanes = lax.broadcasted_iota(jnp.int32, (32, 32), 1)
-    column = jnp.sum(jnp.where(rows == lanes, conduction[...], 0.0), axis=1, keepdims=True)
-    half = lax.broadcasted_iota(jnp.int32, (16, 128), 1) < 64
-    upper = jnp.where(half, column[0:16], column[16:32])
-    gap = upper - jnp.concatenate([valence[...], valence[...]], axis=1) - SHIFT
-    gap_out[...] = gap
-    value = gap * x[...] - jnp.sum(parts[...], axis=0)
+def update_body(parts, gap, x, packed, spread):
+    value = gap[...] * x[...] - jnp.sum(parts[...], axis=0)
     packed[...] = value
     spread[...] = jnp.broadcast_to(value[None], spread.shape)
 
@@ -161,8 +193,33 @@
 
 
 def shards(excitons, valence_energy, conduction_energy, psi_valence, psi_conduction, screened):
-    x, first, second = call(start_body, [(16, 128), (32, 48, 128), (32, 32, 128)], "start")(
-        excitons.T, psi_valence.T
+    x, gap, first, second = pl.pallas_call(
+        start_body,
+        out_shape=tuple(
+            jax.ShapeDtypeStruct(shape, F32)
+            for shape in [(16, 128), (16, 128), (32, 48, 128), (32, 32, 128)]
+        ),
+        in_specs=[pl.BlockSpec(memory_space=pltpu.HBM)] * 4,
+        out_specs=(pl.BlockSpec(memory_space=pltpu.VMEM),) * 4,
+        scratch_shapes=[
+            pltpu.VMEM((32, 64), F32),
+            pltpu.VMEM((32, 256), F32),
+            pltpu.VMEM((1, 64), F32),
+            pltpu.VMEM((1, 32), F32),
+            pltpu.SemaphoreType.DMA((4,)),
+        ],
+        name="start",
+        compiler_params=pltpu.CompilerParams(vmem_limit_bytes=32 * 1024 * 1024),
+    )(
+        *(
+            pltpu.with_memory_space_constraint(value, pltpu.HBM)
+            for value in (
+                excitons.T,
+                psi_valence.T,
+                valence_energy[None],
+                conduction_energy[None],
+            )
+        )
     )
     first = exchange(first, COL)
     panel_conduction = lax.all_gather(psi_conduction.T, ROW, axis=0, tiled=True)
@@ -178,9 +235,7 @@
     second = exchange(second, COL)
     image = lax.all_gather(image, ROW, axis=0, tiled=True)
     (back,) = call(first_weigh_body, [(16, 64, 128)], "weigh_one")(image, first, second, screened)
-    y, spread, gap = call(update_body, [(16, 128), (32, 16, 128), (16, 128)], "update")(
-        returned(back), valence_energy[None], conduction_energy[None], x
-    )
+    y, spread = call(update_body, [(16, 128), (32, 16, 128)], "update")(returned(back), gap, x)
 
     y_rows = exchange(spread, COL)
     (image,) = call(second_points_body, [(72, 128)], "points_two")(first, y_rows, panel_conduction)

time: 213 us -> 209 us (0.981)
  local copies, waits for them, and re-layouts: 2.15 us -> 0.01 us
    unnamed x12 -> x4, local copies, waits for them, and re-layouts: 2.15 us -> 0.01 us
where the time goes in v5:
time: 209 us; the launch traced here: 208 us
  blocking collectives  176 us (84%)
  starting transfers between devices  23.2 us (11%)
  Pallas kernels  8.46 us (4%)
    all_to_all x7, blocking collectives, exchange(): return lax.all_to_all(value, axis, 0, 0, tiled=True)  118 us
    all_to_all x2, starting transfers between devices, exchange(): return lax.all_to_all(value, axis, 0, 0, tiled=True)  23.2 us
    all_gather x1, blocking collectives, shards(): panel_conduction = lax.all_gather(psi_conduction.T, ROW, axis=0, tiled=True)  19.8 us
    all_gather x1, blocking collectives, shards(): image = lax.all_gather(image, ROW, axis=0, tiled=True).reshape(16, 72, 128)  19.5 us
    all_gather x1, blocking collectives, shards(): image = lax.all_gather(image, ROW, axis=0, tiled=True)  18.7 us
  transfers between devices with their start and end apart: 2, of which 0 were waited for; matrix products, arithmetic and copies ran while one was open for 0% of the time, Pallas kernels for 0%

profile of v5, /device:TPU:1, one launch (start us, length us, event | category | flops | bytes accessed | tf_op | source)
XLA Modules:
  0.0 208.4 jit_solution(8851633950076741613)
XLA Ops:
  0.6 2.0 start.1
  2.6 0.0 copy-start.1
  2.6 13.7 %all-to-all-start = ((f32[32,48,128]{2,1,0:T(8,128)}), f32[32,48,128]{2,1,0:T(8,128)S(1)}, u32[]{:S(2)}, u32[]{:S(2)}) async-start(f32[32,48,128]{2,1,0:T(8,128)} %get-tuple-element.18), calls=%async_computation | async-start | bytes 1572864 | tf_op jit(solution)/shard_map/all_to_all | solution.py:21
  16.3 19.8 %all_gather.9 = f32[1024,128]{1,0:T(8,128)S(1)} all-gather(f32[64,128]{1,0:T(8,128)S(1)} %bitcast.13), channel_id=1, replica_groups=mesh['row_0'=8,'row_1'=2,'col_0'=4,'col_1'=8] {'row_0','row_1'}, dimensions={0}, use_global_device_ids=true | all-gather | bytes 557056 | tf_op jit(solution)/shard_map/all_gather | solution.py:225
  36.2 0.6 points_one.1
  36.8 9.5 %all-to-all-start.1 = ((f32[32,32,128]{2,1,0:T(8,128)}), f32[32,32,128]{2,1,0:T(8,128)S(1)}, u32[]{:S(2)}, u32[]{:S(2)}) async-start(f32[32,32,128]{2,1,0:T(8,128)} %get-tuple-element.21), calls=%async_computation.1 | async-start | bytes 1048576 | tf_op jit(solution)/shard_map/all_to_all | solution.py:21
  46.3 0.0 copy-start
  46.3 18.7 %all_gather.10.image = f32[1024,128]{1,0:T(8,128)S(1)} all-gather(f32[64,128]{1,0:T(8,128)S(1)} %points_one.1), channel_id=1, replica_groups=mesh['row_0'=8,'row_1'=2,'col_0'=4,'col_1'=8] {'row_0','row_1'}, dimensions={0}, use_global_device_ids=true | all-gather | bytes 557056 | tf_op jit(solution)/shard_map/all_gather | solution.py:236
  65.0 1.4 weigh_one.1
  66.5 22.1 %all_to_all.45.parts = f32[16,64,128]{2,1,0:T(8,128)S(1)} all-to-all(f32[16,64,128]{2,1,0:T(8,128)S(1)} %weigh_one.1), channel_id=1, replica_groups=mesh['row_0'=8,'row_1'=2,'col_0'=4,'col_1'=8] {'row_0','row_1'}, dimensions={0} | all-to-all | bytes 1048576 | tf_op jit(solution)/shard_map/all_to_all | solution.py:21
  88.5 0.6 conduct.2
  89.1 20.1 %all_to_all.46.parts = f32[32,16,128]{2,1,0:T(8,128)S(1)} all-to-all(f32[32,16,128]{2,1,0:T(8,128)S(1)} %conduct.2), channel_id=1, replica_groups=mesh['row_0'=8,'row_1'=2,'col_0'=4,'col_1'=8] {'col_0','col_1'}, dimensions={0} | all-to-all | bytes 524288 | tf_op jit(solution)/shard_map/all_to_all | solution.py:21
  109.2 0.1 update.1
  109.3 14.6 %all_to_all.47.y_rows = f32[32,16,128]{2,1,0:T(8,128)S(1)} all-to-all(f32[32,16,128]{2,1,0:T(8,128)S(1)} %get-tuple-element.24), channel_id=1, replica_groups=mesh['row_0'=8,'row_1'=2,'col_0'=4,'col_1'=8] {'col_0','col_1'}, dimensions={0} | all-to-all | bytes 524288 | tf_op jit(solution)/shard_map/all_to_all | solution.py:21
  123.9 0.6 points_two.1
  124.5 19.5 %all_gather.11 = f32[1152,128]{1,0:T(8,128)S(1)} all-gather(f32[72,128]{1,0:T(8,128)S(1)} %points_two.1), channel_id=1, replica_groups=mesh['row_0'=8,'row_1'=2,'col_0'=4,'col_1'=8] {'row_0','row_1'}, dimensions={0}, use_global_device_ids=true | all-gather | bytes 626688 | tf_op jit(solution)/shard_map/all_gather | solution.py:242
  144.1 1.4 weigh_two.1
  145.5 21.8 %all_to_all.48.parts = f32[16,64,128]{2,1,0:T(8,128)S(1)} all-to-all(f32[16,64,128]{2,1,0:T(8,128)S(1)} %get-tuple-element.25), channel_id=1, replica_groups=mesh['row_0'=8,'row_1'=2,'col_0'=4,'col_1'=8] {'row_0','row_1'}, dimensions={0} | all-to-all | bytes 1048576 | tf_op jit(solution)/shard_map/all_to_all | solution.py:21
  167.3 0.6 conduct.3
  167.9 15.3 %all_to_all.49.parts = f32[32,16,128]{2,1,0:T(8,128)S(1)} all-to-all(f32[32,16,128]{2,1,0:T(8,128)S(1)} %conduct.3), channel_id=1, replica_groups=mesh['row_0'=8,'row_1'=2,'col_0'=4,'col_1'=8] {'col_0','col_1'}, dimensions={0} | all-to-all | bytes 524288 | tf_op jit(solution)/shard_map/all_to_all | solution.py:21
  183.2 0.2 last.1
  183.4 11.4 %all_to_all.50.parts = f32[16,1,128]{2,1,0:T(1,128)S(1)} all-to-all(f32[16,1,128]{2,1,0:T(1,128)S(1)} %get-tuple-element.28), channel_id=1, replica_groups=mesh['row_0'=8,'row_1'=2,'col_0'=4,'col_1'=8] {'row_0','row_1'}, dimensions={0} | all-to-all | bytes 16384 | tf_op jit(solution)/shard_map/all_to_all | solution.py:21
  194.8 12.6 %all_to_all.51.parts = f32[32,1,128]{2,1,0:T(1,128)S(1)} all-to-all(f32[32,1,128]{2,1,0:T(1,128)S(1)} %fold.1), channel_id=1, replica_groups=mesh['row_0'=8,'row_1'=2,'col_0'=4,'col_1'=8] {'col_0','col_1'}, dimensions={0} | all-to-all | bytes 32768 | tf_op jit(solution)/shard_map/all_to_all | solution.py:21
  207.4 1.0 finish.1
  (5 shorter events, 0.0 us)
Async XLA Ops:
  2.6 13.7 %copy-start.1 = (f32[128,64]{0,1:T(8,128)S(1)}, f32[128,64]{0,1:T(8,128)}, u32[]{:S(2)}) copy-start(f32[128,64]{0,1:T(8,128)} %param.10) | copy-start | bytes 98308
  2.6 33.6 %all-to-all-start = ((f32[32,48,128]{2,1,0:T(8,128)}), f32[32,48,128]{2,1,0:T(8,128)S(1)}, u32[]{:S(2)}, u32[]{:S(2)}) async-start(f32[32,48,128]{2,1,0:T(8,128)} %get-tuple-element.18), calls=%async_computation | async-start | bytes 1572864 | tf_op jit(solution)/shard_map/all_to_all | solution.py:21
  36.8 28.2 %all-to-all-start.1 = ((f32[32,32,128]{2,1,0:T(8,128)}), f32[32,32,128]{2,1,0:T(8,128)S(1)}, u32[]{:S(2)}, u32[]{:S(2)}) async-start(f32[32,32,128]{2,1,0:T(8,128)} %get-tuple-element.21), calls=%async_computation.1 | async-start | bytes 1048576 | tf_op jit(solution)/shard_map/all_to_all | solution.py:21
  46.3 18.7 %copy-start = (f32[256,128]{1,0:T(8,128)S(1)}, f32[256,128]{1,0:T(8,128)}, u32[]{:S(2)}) copy-start(f32[256,128]{1,0:T(8,128)} %screened.3) | copy-start | bytes 393220

commit v6 on v5

--- a/solution.py
+++ b/solution.py
@@ -114,7 +114,9 @@
     )
     panel = halves(panel)
     points = dot_halves(halves(image.T), panel).T
-    out[...] = dot_halves(panel, halves(points * screened[...])).reshape(16, 64, 128)
+    back = dot_halves(panel, halves(points * screened[...])).reshape(8, 2, 64, 128)
+    out[0] = back[:, 0]
+    out[1] = back[:, 1]
 
 
 def first_weigh_body(image, first, second, screened, out):
@@ -124,6 +126,10 @@
 def second_weigh_body(arrived, first, second, screened, out, moments):
     weigh(arrived[:, 0:64, :].reshape(1024, 128), first, second, screened, out)
     moments[...] = jnp.sum(arrived[:, 64:72, :], axis=0)
+
+
+def pair_body(parts, out):
+    out[...] = parts[0] + parts[1]
 
 
 def conduct_body(parts, panel, out):
@@ -226,7 +232,8 @@
     panel_conduction = panel_conduction.reshape(32, 2, 16, 128)
 
     def returned(back):
-        back = exchange(back, ROW)
+        (back,) = call(pair_body, [(8, 64, 128)], "pair")(exchange(back, "row_1"))
+        back = exchange(back, "row_0")
         (kernel,) = call(conduct_body, [(32, 16, 128)], "conduct")(back, panel_conduction)
         return exchange(kernel, COL)
 
@@ -234,13 +241,13 @@
     image, second = lax.optimization_barrier((image, second))
     second = exchange(second, COL)
     image = lax.all_gather(image, ROW, axis=0, tiled=True)
-    (back,) = call(first_weigh_body, [(16, 64, 128)], "weigh_one")(image, first, second, screened)
+    (back,) = call(first_weigh_body, [(2, 8, 64, 128)], "weigh_one")(image, first, second, screened)
     y, spread = call(update_body, [(16, 128), (32, 16, 128)], "update")(returned(back), gap, x)
 
     y_rows = exchange(spread, COL)
     (image,) = call(second_points_body, [(72, 128)], "points_two")(first, y_rows, panel_conduction)
     image = lax.all_gather(image, ROW, axis=0, tiled=True).reshape(16, 72, 128)
-    back, moments = call(second_weigh_body, [(16, 64, 128), (8, 128)], "weigh_two")(
+    back, moments = call(second_weigh_body, [(2, 8, 64, 128), (8, 128)], "weigh_two")(
         image, first, second, screened
     )
     u, q_2, message, scalars = call(

time: 209 us -> 203 us (0.971)
  blocking collectives: 176 us -> 170 us
    all_to_all x7 -> x9, blocking collectives: 118 us -> 111 us  [exchange(): return lax.all_to_all(value, axis, 0, 0, tiled=True)]
where the time goes in v6:
time: 203 us; the launch traced here: 202 us
  blocking collectives  170 us (84%)
  starting transfers between devices  23.2 us (11%)
  Pallas kernels  8.51 us (4%)
    all_to_all x9, blocking collectives, exchange(): return lax.all_to_all(value, axis, 0, 0, tiled=True)  111 us
    all_to_all x2, starting transfers between devices, exchange(): return lax.all_to_all(value, axis, 0, 0, tiled=True)  23.2 us
    all_gather x1, blocking collectives, shards(): image = lax.all_gather(image, ROW, axis=0, tiled=True).reshape(16, 72, 128)  20.1 us
    all_gather x1, blocking collectives, shards(): panel_conduction = lax.all_gather(psi_conduction.T, ROW, axis=0, tiled=True)  19.8 us
    all_gather x1, blocking collectives, shards(): image = lax.all_gather(image, ROW, axis=0, tiled=True)  18.7 us
  transfers between devices with their start and end apart: 2, of which 0 were waited for; matrix products, arithmetic and copies ran while one was open for 0% of the time, Pallas kernels for 0%

profile of v6, /device:TPU:1, one launch (start us, length us, event | category | flops | bytes accessed | tf_op | source)
XLA Modules:
  0.0 202.1 jit_solution(18341329051213739620)
XLA Ops:
  0.6 2.0 start.1
  2.6 13.7 %all-to-all-start = ((f32[32,48,128]{2,1,0:T(8,128)}), f32[32,48,128]{2,1,0:T(8,128)S(1)}, u32[]{:S(2)}, u32[]{:S(2)}) async-start(f32[32,48,128]{2,1,0:T(8,128)} %get-tuple-element.18), calls=%async_computation | async-start | bytes 1572864 | tf_op jit(solution)/shard_map/all_to_all | solution.py:21
  16.3 19.8 %all_gather.9 = f32[1024,128]{1,0:T(8,128)S(1)} all-gather(f32[64,128]{1,0:T(8,128)S(1)} %bitcast.13), channel_id=1, replica_groups=mesh['row_0'=8,'row_1'=2,'col_0'=4,'col_1'=8] {'row_0','row_1'}, dimensions={0}, use_global_device_ids=true | all-gather | bytes 557056 | tf_op jit(solution)/shard_map/all_gather | solution.py:231
  36.2 0.6 points_one.1
  36.8 9.5 %all-to-all-start.1 = ((f32[32,32,128]{2,1,0:T(8,128)}), f32[32,32,128]{2,1,0:T(8,128)S(1)}, u32[]{:S(2)}, u32[]{:S(2)}) async-start(f32[32,32,128]{2,1,0:T(8,128)} %get-tuple-element.21), calls=%async_computation.1 | async-start | bytes 1048576 | tf_op jit(solution)/shard_map/all_to_all | solution.py:21
  46.3 18.7 %all_gather.10.image = f32[1024,128]{1,0:T(8,128)S(1)} all-gather(f32[64,128]{1,0:T(8,128)S(1)} %points_one.1), channel_id=1, replica_groups=mesh['row_0'=8,'row_1'=2,'col_0'=4,'col_1'=8] {'row_0','row_1'}, dimensions={0}, use_global_device_ids=true | all-gather | bytes 557056 | tf_op jit(solution)/shard_map/all_gather | solution.py:243
  65.0 1.4 weigh_one.1
  66.5 3.9 %all_to_all.55.parts = f32[2,8,64,128]{3,2,1,0:T(8,128)S(1)} all-to-all(f32[2,8,64,128]{3,2,1,0:T(8,128)S(1)} %weigh_one.1), channel_id=1, replica_groups=mesh['row_0'=8,'row_1'=2,'col_0'=4,'col_1'=8] {'row_1'}, dimensions={0} | all-to-all | bytes 1048576 | tf_op jit(solution)/shard_map/all_to_all | solution.py:21
  70.4 15.4 %all_to_all.56.parts = f32[8,64,128]{2,1,0:T(8,128)S(1)} all-to-all(f32[8,64,128]{2,1,0:T(8,128)S(1)} %pair.2), channel_id=1, replica_groups=mesh['row_0'=8,'row_1'=2,'col_0'=4,'col_1'=8] {'row_0'}, dimensions={0} | all-to-all | bytes 524288 | tf_op jit(solution)/shard_map/all_to_all | solution.py:21
  85.8 0.6 conduct.2
  86.4 18.5 %all_to_all.57.parts = f32[32,16,128]{2,1,0:T(8,128)S(1)} all-to-all(f32[32,16,128]{2,1,0:T(8,128)S(1)} %conduct.2), channel_id=1, replica_groups=mesh['row_0'=8,'row_1'=2,'col_0'=4,'col_1'=8] {'col_0','col_1'}, dimensions={0} | all-to-all | bytes 524288 | tf_op jit(solution)/shard_map/all_to_all | solution.py:21
  104.9 0.1 update.1
  105.0 14.6 %all_to_all.58.y_rows = f32[32,16,128]{2,1,0:T(8,128)S(1)} all-to-all(f32[32,16,128]{2,1,0:T(8,128)S(1)} %get-tuple-element.24), channel_id=1, replica_groups=mesh['row_0'=8,'row_1'=2,'col_0'=4,'col_1'=8] {'col_0','col_1'}, dimensions={0} | all-to-all | bytes 524288 | tf_op jit(solution)/shard_map/all_to_all | solution.py:21
  119.5 0.6 points_two.1
  120.2 20.1 %all_gather.11 = f32[1152,128]{1,0:T(8,128)S(1)} all-gather(f32[72,128]{1,0:T(8,128)S(1)} %points_two.1), channel_id=1, replica_groups=mesh['row_0'=8,'row_1'=2,'col_0'=4,'col_1'=8] {'row_0','row_1'}, dimensions={0}, use_global_device_ids=true | all-gather | bytes 626688 | tf_op jit(solution)/shard_map/all_gather | solution.py:249
  140.3 1.4 weigh_two.1
  141.7 3.9 %all_to_all.59.parts = f32[2,8,64,128]{3,2,1,0:T(8,128)S(1)} all-to-all(f32[2,8,64,128]{3,2,1,0:T(8,128)S(1)} %get-tuple-element.25), channel_id=1, replica_groups=mesh['row_0'=8,'row_1'=2,'col_0'=4,'col_1'=8] {'row_1'}, dimensions={0} | all-to-all | bytes 1048576 | tf_op jit(solution)/shard_map/all_to_all | solution.py:21
  145.7 15.2 %all_to_all.60.parts = f32[8,64,128]{2,1,0:T(8,128)S(1)} all-to-all(f32[8,64,128]{2,1,0:T(8,128)S(1)} %pair.3), channel_id=1, replica_groups=mesh['row_0'=8,'row_1'=2,'col_0'=4,'col_1'=8] {'row_0'}, dimensions={0} | all-to-all | bytes 524288 | tf_op jit(solution)/shard_map/all_to_all | solution.py:21
  160.9 0.6 conduct.3
  161.5 13.7 %all_to_all.61.parts = f32[32,16,128]{2,1,0:T(8,128)S(1)} all-to-all(f32[32,16,128]{2,1,0:T(8,128)S(1)} %conduct.3), channel_id=1, replica_groups=mesh['row_0'=8,'row_1'=2,'col_0'=4,'col_1'=8] {'col_0','col_1'}, dimensions={0} | all-to-all | bytes 524288 | tf_op jit(solution)/shard_map/all_to_all | solution.py:21
  175.1 0.2 last.1
  175.3 13.1 %all_to_all.62.parts = f32[16,1,128]{2,1,0:T(1,128)S(1)} all-to-all(f32[16,1,128]{2,1,0:T(1,128)S(1)} %get-tuple-element.28), channel_id=1, replica_groups=mesh['row_0'=8,'row_1'=2,'col_0'=4,'col_1'=8] {'row_0','row_1'}, dimensions={0} | all-to-all | bytes 16384 | tf_op jit(solution)/shard_map/all_to_all | solution.py:21
  188.5 12.6 %all_to_all.63.parts = f32[32,1,128]{2,1,0:T(1,128)S(1)} all-to-all(f32[32,1,128]{2,1,0:T(1,128)S(1)} %fold.1), channel_id=1, replica_groups=mesh['row_0'=8,'row_1'=2,'col_0'=4,'col_1'=8] {'col_0','col_1'}, dimensions={0} | all-to-all | bytes 32768 | tf_op jit(solution)/shard_map/all_to_all | solution.py:21
  201.1 1.0 finish.1
  (9 shorter events, 0.1 us)
Async XLA Ops:
  2.6 13.7 %copy-start.1 = (f32[128,64]{0,1:T(8,128)S(1)}, f32[128,64]{0,1:T(8,128)}, u32[]{:S(2)}) copy-start(f32[128,64]{0,1:T(8,128)} %param.10) | copy-start | bytes 98308
  2.6 33.6 %all-to-all-start = ((f32[32,48,128]{2,1,0:T(8,128)}), f32[32,48,128]{2,1,0:T(8,128)S(1)}, u32[]{:S(2)}, u32[]{:S(2)}) async-start(f32[32,48,128]{2,1,0:T(8,128)} %get-tuple-element.18), calls=%async_computation | async-start | bytes 1572864 | tf_op jit(solution)/shard_map/all_to_all | solution.py:21
  36.8 28.2 %all-to-all-start.1 = ((f32[32,32,128]{2,1,0:T(8,128)}), f32[32,32,128]{2,1,0:T(8,128)S(1)}, u32[]{:S(2)}, u32[]{:S(2)}) async-start(f32[32,32,128]{2,1,0:T(8,128)} %get-tuple-element.21), calls=%async_computation.1 | async-start | bytes 1048576 | tf_op jit(solution)/shard_map/all_to_all | solution.py:21
  46.3 18.7 %copy-start = (f32[256,128]{1,0:T(8,128)S(1)}, f32[256,128]{1,0:T(8,128)}, u32[]{:S(2)}) copy-start(f32[256,128]{1,0:T(8,128)} %screened.3) | copy-start | bytes 393220

commit v7 on v6

--- a/solution.py
+++ b/solution.py
@@ -101,11 +101,9 @@
 def second_points_body(first, y_rows, panel, out):
     x = first[:, 0:16, :].reshape(512, 128)
     y = y_rows[...].reshape(512, 128)
-    out[0:64, :] = points_of(y, panel)
-    out[64:65, :] = jnp.sum(x * x, axis=0, keepdims=True)
-    out[65:66, :] = jnp.sum(x * y, axis=0, keepdims=True)
-    out[66:67, :] = jnp.sum(y * y, axis=0, keepdims=True)
-    out[67:72, :] = jnp.zeros((5, 128), F32)
+    sums = [jnp.sum(a * b, axis=0, keepdims=True) for a, b in ((x, x), (x, y), (y, y))]
+    message = jnp.concatenate([points_of(y, panel), *sums, jnp.zeros((5, 128), F32)], axis=0)
+    out[...] = jnp.broadcast_to(message[None], out.shape)
 
 
 def weigh(image, first, second, screened, out):
@@ -124,8 +122,9 @@
 
 
 def second_weigh_body(arrived, first, second, screened, out, moments):
-    weigh(arrived[:, 0:64, :].reshape(1024, 128), first, second, screened, out)
-    moments[...] = jnp.sum(arrived[:, 64:72, :], axis=0)
+    image = jnp.stack([arrived[0, :, 0:64, :], arrived[1, :, 0:64, :]], axis=1)
+    weigh(image.reshape(1024, 128), first, second, screened, out)
+    moments[...] = jnp.sum(arrived[0, :, 64:72, :] + arrived[1, :, 64:72, :], axis=0)
 
 
 def pair_body(parts, out):
@@ -245,17 +244,19 @@
     y, spread = call(update_body, [(16, 128), (32, 16, 128)], "update")(returned(back), gap, x)
 
     y_rows = exchange(spread, COL)
-    (image,) = call(second_points_body, [(72, 128)], "points_two")(first, y_rows, panel_conduction)
-    image = lax.all_gather(image, ROW, axis=0, tiled=True).reshape(16, 72, 128)
+    (image,) = call(second_points_body, [(8, 72, 128)], "points_two")(
+        first, y_rows, panel_conduction
+    )
+    image = lax.all_gather(exchange(image, "row_0"), "row_1", axis=0)
     back, moments = call(second_weigh_body, [(2, 8, 64, 128), (8, 128)], "weigh_two")(
         image, first, second, screened
     )
     u, q_2, message, scalars = call(
-        last_body, [(16, 128), (16, 128), (16, 1, 128), (1, 128)], "last"
+        last_body, [(16, 128), (16, 128), (64, 1, 128), (1, 128)], "last"
     )(returned(back), gap, x, y, moments)
-    (message,) = call(fold_body, [(32, 1, 128)], "fold")(exchange(message, ROW))
+    (message,) = call(fold_body, [(8, 1, 128)], "fold")(exchange(message, (*ROW, "col_0")))
     out, coefficients = call(finish_body, [(32, 64), (4,)], "finish", smem=(1,))(
-        exchange(message, COL), u, q_2, scalars
+        exchange(message, "col_1"), u, q_2, scalars
     )
     return out.T, coefficients
 

time: 203 us -> 202 us (level)
    all_gather x1, blocking collectives: 20.1 us -> 6.94 us  [shards(): image = lax.all_gather(exchange(image, 'row_0'), 'row_1', axis=0)]
    all_to_all x9 -> x10, blocking collectives: 111 us -> 123 us  [exchange(): return lax.all_to_all(value, axis, 0, 0, tiled=True)]
where the time goes in v7:
time: 202 us; the launch traced here: 201 us
  blocking collectives  168 us (83%)
  starting transfers between devices  23.2 us (11%)
  Pallas kernels  8.55 us (4%)
    all_to_all x10, blocking collectives, exchange(): return lax.all_to_all(value, axis, 0, 0, tiled=True)  123 us
    all_to_all x2, starting transfers between devices, exchange(): return lax.all_to_all(value, axis, 0, 0, tiled=True)  23.2 us
    all_gather x1, blocking collectives, shards(): panel_conduction = lax.all_gather(psi_conduction.T, ROW, axis=0, tiled=True)  19.8 us
    all_gather x1, blocking collectives, shards(): image = lax.all_gather(image, ROW, axis=0, tiled=True)  18.7 us
    all_gather x1, blocking collectives, shards(): image = lax.all_gather(exchange(image, 'row_0'), 'row_1', axis=0)  6.94 us
  transfers between devices with their start and end apart: 2, of which 0 were waited for; matrix products, arithmetic and copies ran while one was open for 0% of the time, Pallas kernels for 0%

profile of v7, /device:TPU:1, one launch (start us, length us, event | category | flops | bytes accessed | tf_op | source)
XLA Modules:
  0.0 200.9 jit_solution(8872319305712352384)
XLA Ops:
  0.6 2.0 start.1
  2.6 13.7 %all-to-all-start = ((f32[32,48,128]{2,1,0:T(8,128)}), f32[32,48,128]{2,1,0:T(8,128)S(1)}, u32[]{:S(2)}, u32[]{:S(2)}) async-start(f32[32,48,128]{2,1,0:T(8,128)} %get-tuple-element.18), calls=%async_computation | async-start | bytes 1572864 | tf_op jit(solution)/shard_map/all_to_all | solution.py:21
  16.3 19.8 %all_gather.12 = f32[1024,128]{1,0:T(8,128)S(1)} all-gather(f32[64,128]{1,0:T(8,128)S(1)} %bitcast.13), channel_id=1, replica_groups=mesh['row_0'=8,'row_1'=2,'col_0'=4,'col_1'=8] {'row_0','row_1'}, dimensions={0}, use_global_device_ids=true | all-gather | bytes 557056 | tf_op jit(solution)/shard_map/all_gather | solution.py:230
  36.2 0.6 points_one.1
  36.8 9.5 %all-to-all-start.1 = ((f32[32,32,128]{2,1,0:T(8,128)}), f32[32,32,128]{2,1,0:T(8,128)S(1)}, u32[]{:S(2)}, u32[]{:S(2)}) async-start(f32[32,32,128]{2,1,0:T(8,128)} %get-tuple-element.21), calls=%async_computation.1 | async-start | bytes 1048576 | tf_op jit(solution)/shard_map/all_to_all | solution.py:21
  46.3 18.7 %all_gather.13.image = f32[1024,128]{1,0:T(8,128)S(1)} all-gather(f32[64,128]{1,0:T(8,128)S(1)} %points_one.1), channel_id=1, replica_groups=mesh['row_0'=8,'row_1'=2,'col_0'=4,'col_1'=8] {'row_0','row_1'}, dimensions={0}, use_global_device_ids=true | all-gather | bytes 557056 | tf_op jit(solution)/shard_map/all_gather | solution.py:242
  65.0 1.4 weigh_one.1
  66.5 3.9 %all_to_all.60.parts = f32[2,8,64,128]{3,2,1,0:T(8,128)S(1)} all-to-all(f32[2,8,64,128]{3,2,1,0:T(8,128)S(1)} %weigh_one.1), channel_id=1, replica_groups=mesh['row_0'=8,'row_1'=2,'col_0'=4,'col_1'=8] {'row_1'}, dimensions={0} | all-to-all | bytes 1048576 | tf_op jit(solution)/shard_map/all_to_all | solution.py:21
  70.4 15.4 %all_to_all.61.parts = f32[8,64,128]{2,1,0:T(8,128)S(1)} all-to-all(f32[8,64,128]{2,1,0:T(8,128)S(1)} %pair.2), channel_id=1, replica_groups=mesh['row_0'=8,'row_1'=2,'col_0'=4,'col_1'=8] {'row_0'}, dimensions={0} | all-to-all | bytes 524288 | tf_op jit(solution)/shard_map/all_to_all | solution.py:21
  85.8 0.6 conduct.2
  86.4 18.5 %all_to_all.62.parts = f32[32,16,128]{2,1,0:T(8,128)S(1)} all-to-all(f32[32,16,128]{2,1,0:T(8,128)S(1)} %conduct.2), channel_id=1, replica_groups=mesh['row_0'=8,'row_1'=2,'col_0'=4,'col_1'=8] {'col_0','col_1'}, dimensions={0} | all-to-all | bytes 524288 | tf_op jit(solution)/shard_map/all_to_all | solution.py:21
  105.0 14.6 %all_to_all.63.y_rows = f32[32,16,128]{2,1,0:T(8,128)S(1)} all-to-all(f32[32,16,128]{2,1,0:T(8,128)S(1)} %get-tuple-element.24), channel_id=1, replica_groups=mesh['row_0'=8,'row_1'=2,'col_0'=4,'col_1'=8] {'col_0','col_1'}, dimensions={0} | all-to-all | bytes 524288 | tf_op jit(solution)/shard_map/all_to_all | solution.py:21
  119.5 0.6 points_two.1
  120.2 12.4 %all_to_all.64 = f32[8,72,128]{2,1,0:T(8,128)S(1)} all-to-all(f32[8,72,128]{2,1,0:T(8,128)S(1)} %points_two.1), channel_id=1, replica_groups=mesh['row_0'=8,'row_1'=2,'col_0'=4,'col_1'=8] {'row_0'}, dimensions={0} | all-to-all | bytes 589824 | tf_op jit(solution)/shard_map/all_to_all | solution.py:21
  132.6 6.9 %all-gather = f32[16,72,128]{2,1,0:T(8,128)S(1)} all-gather(f32[8,72,128]{2,1,0:T(8,128)S(1)} %all_to_all.64), channel_id=2, replica_groups=mesh['row_0'=8,'row_1'=2,'col_0'=4,'col_1'=8] {'row_1'}, dimensions={0}, use_global_device_ids=true | all-gather | bytes 884736 | tf_op jit(solution)/shard_map/all_gather | solution.py:250
  139.6 1.4 weigh_two.1
  141.0 4.2 %all_to_all.65.parts = f32[2,8,64,128]{3,2,1,0:T(8,128)S(1)} all-to-all(f32[2,8,64,128]{3,2,1,0:T(8,128)S(1)} %get-tuple-element.25), channel_id=1, replica_groups=mesh['row_0'=8,'row_1'=2,'col_0'=4,'col_1'=8] {'row_1'}, dimensions={0} | all-to-all | bytes 1048576 | tf_op jit(solution)/shard_map/all_to_all | solution.py:21
  145.2 14.8 %all_to_all.66.parts = f32[8,64,128]{2,1,0:T(8,128)S(1)} all-to-all(f32[8,64,128]{2,1,0:T(8,128)S(1)} %pair.3), channel_id=1, replica_groups=mesh['row_0'=8,'row_1'=2,'col_0'=4,'col_1'=8] {'row_0'}, dimensions={0} | all-to-all | bytes 524288 | tf_op jit(solution)/shard_map/all_to_all | solution.py:21
  159.9 0.6 conduct.3
  160.5 13.7 %all_to_all.67.parts = f32[32,16,128]{2,1,0:T(8,128)S(1)} all-to-all(f32[32,16,128]{2,1,0:T(8,128)S(1)} %conduct.3), channel_id=1, replica_groups=mesh['row_0'=8,'row_1'=2,'col_0'=4,'col_1'=8] {'col_0','col_1'}, dimensions={0} | all-to-all | bytes 524288 | tf_op jit(solution)/shard_map/all_to_all | solution.py:21
  174.2 0.2 last.1
  174.4 16.2 %all_to_all.68.parts = f32[64,1,128]{2,1,0:T(1,128)S(1)} all-to-all(f32[64,1,128]{2,1,0:T(1,128)S(1)} %get-tuple-element.28), channel_id=1, replica_groups=mesh['row_0'=8,'row_1'=2,'col_0'=4,'col_1'=8] {'row_0','row_1','col_0'}, dimensions={0} | all-to-all | bytes 65536 | tf_op jit(solution)/shard_map/all_to_all | solution.py:21
  190.7 9.3 %all_to_all.69.parts = f32[8,1,128]{2,1,0:T(1,128)S(1)} all-to-all(f32[8,1,128]{2,1,0:T(1,128)S(1)} %fold.1), channel_id=1, replica_groups=mesh['row_0'=8,'row_1'=2,'col_0'=4,'col_1'=8] {'col_1'}, dimensions={0} | all-to-all | bytes 8192 | tf_op jit(solution)/shard_map/all_to_all | solution.py:21
  200.0 1.0 finish.1
  (10 shorter events, 0.2 us)
Async XLA Ops:
  2.6 13.7 %copy-start.1 = (f32[128,64]{0,1:T(8,128)S(1)}, f32[128,64]{0,1:T(8,128)}, u32[]{:S(2)}) copy-start(f32[128,64]{0,1:T(8,128)} %param.10) | copy-start | bytes 98308
  2.6 33.6 %all-to-all-start = ((f32[32,48,128]{2,1,0:T(8,128)}), f32[32,48,128]{2,1,0:T(8,128)S(1)}, u32[]{:S(2)}, u32[]{:S(2)}) async-start(f32[32,48,128]{2,1,0:T(8,128)} %get-tuple-element.18), calls=%async_computation | async-start | bytes 1572864 | tf_op jit(solution)/shard_map/all_to_all | solution.py:21
  36.8 28.2 %all-to-all-start.1 = ((f32[32,32,128]{2,1,0:T(8,128)}), f32[32,32,128]{2,1,0:T(8,128)S(1)}, u32[]{:S(2)}, u32[]{:S(2)}) async-start(f32[32,32,128]{2,1,0:T(8,128)} %get-tuple-element.21), calls=%async_computation.1 | async-start | bytes 1048576 | tf_op jit(solution)/shard_map/all_to_all | solution.py:21
  46.3 18.7 %copy-start = (f32[256,128]{1,0:T(8,128)S(1)}, f32[256,128]{1,0:T(8,128)}, u32[]{:S(2)}) copy-start(f32[256,128]{1,0:T(8,128)} %screened.3) | copy-start | bytes 393220

commit v8 on v7

--- a/solution.py
+++ b/solution.py
@@ -56,8 +56,17 @@
     )
 
 
+def mine(zero, one):
+    return jnp.where(lax.axis_index("row_1") == 0, zero, one)
+
+
+def spread_half(out, at, half):
+    out[:, at : at + 16, :] = jnp.broadcast_to(half[:, 0:128][None], (32, 16, 128))
+    out[:, at + 16 : at + 32, :] = jnp.broadcast_to(half[:, 128:256][None], (32, 16, 128))
+
+
 def start_body(
-    block_in, panel_in, valence_in, conduction_in, packed, gap, first, second,
+    block_in, panel_in, valence_in, conduction_in, packed, gap, first,
     block, panel, valence, conduction, arrived,
 ):
     moves = [
@@ -78,8 +87,7 @@
     value = jnp.concatenate([block[0:16, :], block[16:32, :]], axis=1)
     packed[...] = value
     first[:, 0:16, :] = jnp.broadcast_to(value[None], (32, 16, 128))
-    first[:, 16:48, :] = jnp.broadcast_to(panel[:, 0:128][None], (32, 32, 128))
-    second[...] = jnp.broadcast_to(panel[:, 128:256][None], second.shape)
+    spread_half(first, 16, mine(panel[0:16, :], panel[16:32, :]))
     rows = lax.broadcasted_iota(jnp.int32, (32, 32), 0)
     lanes = lax.broadcasted_iota(jnp.int32, (32, 32), 1)
     column = jnp.sum(jnp.where(rows == lanes, conduction[...], 0.0), axis=1, keepdims=True)
@@ -94,45 +102,57 @@
     return lo[0:64] + hi[64:128]
 
 
-def first_points_body(first, panel, out):
+def first_points_body(first, panel, blocks, out, second):
     out[...] = points_of(first[:, 0:16, :].reshape(512, 128), panel)
+    spread_half(second, 0, mine(blocks[1, 0:16, :], blocks[0, 16:32, :]))
 
 
 def second_points_body(first, y_rows, panel, out):
     x = first[:, 0:16, :].reshape(512, 128)
     y = y_rows[...].reshape(512, 128)
     sums = [jnp.sum(a * b, axis=0, keepdims=True) for a, b in ((x, x), (x, y), (y, y))]
-    message = jnp.concatenate([points_of(y, panel), *sums, jnp.zeros((5, 128), F32)], axis=0)
-    out[...] = jnp.broadcast_to(message[None], out.shape)
-
-
-def weigh(image, first, second, screened, out):
-    panel = jnp.concatenate(
-        [first[:, 16:48, :].reshape(1024, 128), second[...].reshape(1024, 128)], axis=1
-    )
-    panel = halves(panel)
-    points = dot_halves(halves(image.T), panel).T
-    back = dot_halves(panel, halves(points * screened[...])).reshape(8, 2, 64, 128)
-    out[0] = back[:, 0]
-    out[1] = back[:, 1]
-
-
-def first_weigh_body(image, first, second, screened, out):
-    weigh(image[...], first, second, screened, out)
-
-
-def second_weigh_body(arrived, first, second, screened, out, moments):
-    image = jnp.stack([arrived[0, :, 0:64, :], arrived[1, :, 0:64, :]], axis=1)
-    weigh(image.reshape(1024, 128), first, second, screened, out)
-    moments[...] = jnp.sum(arrived[0, :, 64:72, :] + arrived[1, :, 64:72, :], axis=0)
-
-
-def pair_body(parts, out):
-    out[...] = parts[0] + parts[1]
+    sums.append(jnp.zeros((5, 128), F32))
+    image = points_of(y, panel)
+    for core in range(2):
+        at = 16 * core
+        message = [image[at : at + 16], image[at + 32 : at + 48], *sums]
+        message = jnp.concatenate(message, axis=0)
+        out[:, core] = jnp.broadcast_to(message[None], (8, 40, 128))
+
+
+def shared_panel(first, second):
+    parts = [first[:, 16:32, :], first[:, 32:48, :], second[:, 0:16, :], second[:, 16:32, :]]
+    return halves(jnp.concatenate([part.reshape(512, 128) for part in parts], axis=1))
+
+
+def partial_points(image, first, second, out):
+    points = dot_halves(halves(image.T), shared_panel(first, second)).T
+    out[0] = mine(points[0:256], points[256:512])
+    out[1] = mine(points[256:512], points[0:256])
+
+
+def first_partial_body(image, first, second, out):
+    image = mine(image[:, 0], image[:, 1]).reshape(512, 128)
+    partial_points(image, first, second, out)
+
+
+def second_partial_body(arrived, first, second, out, moments):
+    partial_points(arrived[:, 0:32, :].reshape(512, 128), first, second, out)
+    moments[...] = jnp.sum(arrived[:, 32:40, :], axis=0)
+
+
+def weigh_body(partials, screened, first, second, out):
+    zero = (partials[0, 0] + partials[1, 0]) * screened[0]
+    one = (partials[0, 1] + partials[1, 1]) * screened[1]
+    weighted = jnp.concatenate([mine(zero, one), mine(one, zero)], axis=0)
+    back = dot_halves(shared_panel(first, second), halves(weighted))
+    out[...] = back.reshape(16, 32, 128)
 
 
 def conduct_body(parts, panel, out):
-    back = jnp.sum(parts[...], axis=0)
+    sums = jnp.sum(parts[...], axis=0)
+    back = jnp.stack([sums[0].reshape(2, 16, 128), sums[1].reshape(2, 16, 128)], axis=1)
+    back = back.reshape(64, 128)
     zero = jnp.zeros_like(back)
     lo = dot(panel[:, 0].reshape(512, 128), jnp.concatenate([back, zero], axis=0), 1, 1)
     hi = dot(panel[:, 1].reshape(512, 128), jnp.concatenate([zero, back], axis=0), 1, 1)
@@ -198,14 +218,13 @@
 
 
 def shards(excitons, valence_energy, conduction_energy, psi_valence, psi_conduction, screened):
-    x, gap, first, second = pl.pallas_call(
+    x, gap, first = pl.pallas_call(
         start_body,
         out_shape=tuple(
-            jax.ShapeDtypeStruct(shape, F32)
-            for shape in [(16, 128), (16, 128), (32, 48, 128), (32, 32, 128)]
+            jax.ShapeDtypeStruct(shape, F32) for shape in [(16, 128), (16, 128), (32, 48, 128)]
         ),
         in_specs=[pl.BlockSpec(memory_space=pltpu.HBM)] * 4,
-        out_specs=(pl.BlockSpec(memory_space=pltpu.VMEM),) * 4,
+        out_specs=(pl.BlockSpec(memory_space=pltpu.VMEM),) * 3,
         scratch_shapes=[
             pltpu.VMEM((32, 64), F32),
             pltpu.VMEM((32, 256), F32),
@@ -230,30 +249,38 @@
     panel_conduction = lax.all_gather(psi_conduction.T, ROW, axis=0, tiled=True)
     panel_conduction = panel_conduction.reshape(32, 2, 16, 128)
 
-    def returned(back):
-        (back,) = call(pair_body, [(8, 64, 128)], "pair")(exchange(back, "row_1"))
-        back = exchange(back, "row_0")
+    blocks = lax.all_gather(psi_valence.T, "row_1", axis=0)
+    pair_screened = lax.all_gather(screened, "row_1", axis=0)
+    blocks, pair_screened = lax.optimization_barrier((blocks, pair_screened))
+
+    def returned(partial):
+        partials = lax.all_gather(partial, "row_1", axis=0)
+        (back,) = call(weigh_body, [(16, 32, 128)], "weigh")(
+            partials, pair_screened, first, second
+        )
+        back = exchange(back, ROW).reshape(8, 2, 32, 128)
         (kernel,) = call(conduct_body, [(32, 16, 128)], "conduct")(back, panel_conduction)
         return exchange(kernel, COL)
 
-    (image,) = call(first_points_body, [(64, 128)], "points_one")(first, panel_conduction)
-    image, second = lax.optimization_barrier((image, second))
+    image, second = call(first_points_body, [(64, 128), (32, 32, 128)], "points_one")(
+        first, panel_conduction, blocks
+    )
     second = exchange(second, COL)
-    image = lax.all_gather(image, ROW, axis=0, tiled=True)
-    (back,) = call(first_weigh_body, [(2, 8, 64, 128)], "weigh_one")(image, first, second, screened)
-    y, spread = call(update_body, [(16, 128), (32, 16, 128)], "update")(returned(back), gap, x)
+    image = lax.all_gather(image, ROW, axis=0, tiled=True).reshape(32, 2, 16, 128)
+    (partial,) = call(first_partial_body, [(2, 256, 128)], "partial_one")(image, first, second)
+    y, spread = call(update_body, [(16, 128), (32, 16, 128)], "update")(returned(partial), gap, x)
 
     y_rows = exchange(spread, COL)
-    (image,) = call(second_points_body, [(8, 72, 128)], "points_two")(
+    (image,) = call(second_points_body, [(8, 2, 40, 128)], "points_two")(
         first, y_rows, panel_conduction
     )
-    image = lax.all_gather(exchange(image, "row_0"), "row_1", axis=0)
-    back, moments = call(second_weigh_body, [(2, 8, 64, 128), (8, 128)], "weigh_two")(
-        image, first, second, screened
+    image = exchange(image.reshape(16, 40, 128), ROW)
+    partial, moments = call(second_partial_body, [(2, 256, 128), (8, 128)], "partial_two")(
+        image, first, second
     )
     u, q_2, message, scalars = call(
         last_body, [(16, 128), (16, 128), (64, 1, 128), (1, 128)], "last"
-    )(returned(back), gap, x, y, moments)
+    )(returned(partial), gap, x, y, moments)
     (message,) = call(fold_body, [(8, 1, 128)], "fold")(exchange(message, (*ROW, "col_0")))
     out, coefficients = call(finish_body, [(32, 64), (4,)], "finish", smem=(1,))(
         exchange(message, "col_1"), u, q_2, scalars

time: 202 us -> 204 us (level)
    all_to_all x10 -> x8, blocking collectives: 123 us -> 125 us  [exchange(): return lax.all_to_all(value, axis, 0, 0, tiled=True)]
    all_gather x2 -> x5, blocking collectives: 25.6 us -> 26.3 us  [the longest x1 16.7 us: shards(): lax.all_gather(image, ROW, axis=0, tiled=True).reshape(32, 2, 16, 128)]
where the time goes in v8:
time: 204 us; the launch traced here: 203 us
  blocking collectives  170 us (83%)
  starting transfers between devices  23.4 us (11%)
  Pallas kernels  8.57 us (4%)
    all_to_all x8, blocking collectives, exchange(): return lax.all_to_all(value, axis, 0, 0, tiled=True)  125 us
    all_to_all x2, starting transfers between devices, exchange(): return lax.all_to_all(value, axis, 0, 0, tiled=True)  23.4 us
    all_gather x1, blocking collectives, shards(): panel_conduction = lax.all_gather(psi_conduction.T, ROW, axis=0, tiled=True)  19.2 us
    all_gather x1, blocking collectives, shards(): lax.all_gather(image, ROW, axis=0, tiled=True).reshape(32, 2, 16, 128)  16.7 us
    all_gather x2, blocking collectives, returned(): partials = lax.all_gather(partial, 'row_1', axis=0)  5.02 us
  transfers between devices with their start and end apart: 2, of which 0 were waited for; matrix products, arithmetic and copies ran while one was open for 0% of the time, Pallas kernels for 0%

profile of v8, /device:TPU:1, one launch (start us, length us, event | category | flops | bytes accessed | tf_op | source)
XLA Modules:
  0.0 202.8 jit_solution(2225779795854948781)
XLA Ops:
  0.6 1.8 start.1
  2.5 13.9 %all-to-all-start = ((f32[32,48,128]{2,1,0:T(8,128)}), f32[32,48,128]{2,1,0:T(8,128)S(1)}, u32[]{:S(2)}, u32[]{:S(2)}) async-start(f32[32,48,128]{2,1,0:T(8,128)} %get-tuple-element.19), calls=%async_computation | async-start | bytes 1572864 | tf_op jit(solution)/shard_map/all_to_all | solution.py:21
  16.3 2.5 %all-gather = f32[64,256]{1,0:T(8,128)S(1)} all-gather(f32[32,256]{1,0:T(8,128)S(1)} %bitcast.29), channel_id=2, replica_groups=mesh['row_0'=8,'row_1'=2,'col_0'=4,'col_1'=8] {'row_1'}, dimensions={0}, use_global_device_ids=true | all-gather | bytes 98304 | tf_op jit(solution)/shard_map/all_gather | solution.py:252
  18.8 2.1 %all-gather.1 = f32[512,128]{1,0:T(8,128)S(1)} all-gather(f32[256,128]{1,0:T(8,128)S(1)} %copy-done), channel_id=3, replica_groups=mesh['row_0'=8,'row_1'=2,'col_0'=4,'col_1'=8] {'row_1'}, dimensions={0}, use_global_device_ids=true | all-gather | bytes 393216 | tf_op jit(solution)/shard_map/all_gather | solution.py:253
  20.9 19.2 %all_gather.30 = f32[1024,128]{1,0:T(8,128)S(1)} all-gather(f32[64,128]{1,0:T(8,128)S(1)} %bitcast.30), channel_id=1, replica_groups=mesh['row_0'=8,'row_1'=2,'col_0'=4,'col_1'=8] {'row_0','row_1'}, dimensions={0}, use_global_device_ids=true | all-gather | bytes 557056 | tf_op jit(solution)/shard_map/all_gather | solution.py:249
  40.1 1.4 points_one.1
  41.5 9.5 %all-to-all-start.1 = ((f32[32,32,128]{2,1,0:T(8,128)}), f32[32,32,128]{2,1,0:T(8,128)S(1)}, u32[]{:S(2)}, u32[]{:S(2)}) async-start(f32[32,32,128]{2,1,0:T(8,128)} %get-tuple-element.22), calls=%async_computation.1 | async-start | bytes 1048576 | tf_op jit(solution)/shard_map/all_to_all | solution.py:21
  51.0 16.7 %all_gather.35 = f32[1024,128]{1,0:T(8,128)S(1)} all-gather(f32[64,128]{1,0:T(8,128)S(1)} %get-tuple-element.21), channel_id=1, replica_groups=mesh['row_0'=8,'row_1'=2,'col_0'=4,'col_1'=8] {'row_0','row_1'}, dimensions={0}, use_global_device_ids=true | all-gather | bytes 557056 | tf_op jit(solution)/shard_map/all_gather | solution.py:269
  68.2 2.8 %all-gather.2 = f32[4,256,128]{2,1,0:T(8,128)S(1)} all-gather(f32[2,256,128]{2,1,0:T(8,128)S(1)} %partial_one.1), channel_id=4, replica_groups=mesh['row_0'=8,'row_1'=2,'col_0'=4,'col_1'=8] {'row_1'}, dimensions={0}, use_global_device_ids=true | all-gather | bytes 786432 | tf_op jit(solution)/shard_map/all_gather | solution.py:257
  71.1 0.6 weigh.2
  71.7 16.2 %all_to_all.50 = f32[16,32,128]{2,1,0:T(8,128)S(1)} all-to-all(f32[16,32,128]{2,1,0:T(8,128)S(1)} %weigh.2), channel_id=1, replica_groups=mesh['row_0'=8,'row_1'=2,'col_0'=4,'col_1'=8] {'row_0','row_1'}, dimensions={0} | all-to-all | bytes 524288 | tf_op jit(solution)/shard_map/all_to_all | solution.py:21
  87.9 0.6 conduct.2
  88.5 19.8 %all_to_all.51.parts = f32[32,16,128]{2,1,0:T(8,128)S(1)} all-to-all(f32[32,16,128]{2,1,0:T(8,128)S(1)} %conduct.2), channel_id=1, replica_groups=mesh['row_0'=8,'row_1'=2,'col_0'=4,'col_1'=8] {'col_0','col_1'}, dimensions={0} | all-to-all | bytes 524288 | tf_op jit(solution)/shard_map/all_to_all | solution.py:21
  108.3 15.6 %all_to_all.52.y_rows = f32[32,16,128]{2,1,0:T(8,128)S(1)} all-to-all(f32[32,16,128]{2,1,0:T(8,128)S(1)} %get-tuple-element.26), channel_id=1, replica_groups=mesh['row_0'=8,'row_1'=2,'col_0'=4,'col_1'=8] {'col_0','col_1'}, dimensions={0} | all-to-all | bytes 524288 | tf_op jit(solution)/shard_map/all_to_all | solution.py:21
  123.9 0.6 points_two.1
  124.5 19.2 %all_to_all.53.arrived = f32[16,40,128]{2,1,0:T(8,128)S(1)} all-to-all(f32[16,40,128]{2,1,0:T(8,128)S(1)} %bitcast.24), channel_id=1, replica_groups=mesh['row_0'=8,'row_1'=2,'col_0'=4,'col_1'=8] {'row_0','row_1'}, dimensions={0} | all-to-all | bytes 655360 | tf_op jit(solution)/shard_map/all_to_all | solution.py:21
  144.2 2.2 %all-gather.3 = f32[4,256,128]{2,1,0:T(8,128)S(1)} all-gather(f32[2,256,128]{2,1,0:T(8,128)S(1)} %get-tuple-element.27), channel_id=5, replica_groups=mesh['row_0'=8,'row_1'=2,'col_0'=4,'col_1'=8] {'row_1'}, dimensions={0}, use_global_device_ids=true | all-gather | bytes 786432 | tf_op jit(solution)/shard_map/all_gather | solution.py:257
  146.4 0.6 weigh.3
  147.0 14.5 %all_to_all.54 = f32[16,32,128]{2,1,0:T(8,128)S(1)} all-to-all(f32[16,32,128]{2,1,0:T(8,128)S(1)} %weigh.3), channel_id=1, replica_groups=mesh['row_0'=8,'row_1'=2,'col_0'=4,'col_1'=8] {'row_0','row_1'}, dimensions={0} | all-to-all | bytes 524288 | tf_op jit(solution)/shard_map/all_to_all | solution.py:21
  161.5 0.6 conduct.3
  162.1 14.7 %all_to_all.55.parts = f32[32,16,128]{2,1,0:T(8,128)S(1)} all-to-all(f32[32,16,128]{2,1,0:T(8,128)S(1)} %conduct.3), channel_id=1, replica_groups=mesh['row_0'=8,'row_1'=2,'col_0'=4,'col_1'=8] {'col_0','col_1'}, dimensions={0} | all-to-all | bytes 524288 | tf_op jit(solution)/shard_map/all_to_all | solution.py:21
  177.0 15.6 %all_to_all.56.parts = f32[64,1,128]{2,1,0:T(1,128)S(1)} all-to-all(f32[64,1,128]{2,1,0:T(1,128)S(1)} %get-tuple-element.30), channel_id=1, replica_groups=mesh['row_0'=8,'row_1'=2,'col_0'=4,'col_1'=8] {'row_0','row_1','col_0'}, dimensions={0} | all-to-all | bytes 65536 | tf_op jit(solution)/shard_map/all_to_all | solution.py:21
  192.7 9.1 %all_to_all.57.parts = f32[8,1,128]{2,1,0:T(1,128)S(1)} all-to-all(f32[8,1,128]{2,1,0:T(1,128)S(1)} %fold.1), channel_id=1, replica_groups=mesh['row_0'=8,'row_1'=2,'col_0'=4,'col_1'=8] {'col_1'}, dimensions={0} | all-to-all | bytes 8192 | tf_op jit(solution)/shard_map/all_to_all | solution.py:21
  201.8 1.0 finish.1
  (13 shorter events, 1.4 us)
Async XLA Ops:
  2.4 13.9 %copy-start.1 = (f32[256,32]{0,1:T(8,128)S(1)}, f32[256,32]{0,1:T(8,128)}, u32[]{:S(2)}) copy-start(f32[256,32]{0,1:T(8,128)} %param.9) | copy-start | bytes 98308
  2.4 16.4 %copy-start = (f32[256,128]{1,0:T(8,128)S(1)}, f32[256,128]{1,0:T(8,128)}, u32[]{:S(2)}) copy-start(f32[256,128]{1,0:T(8,128)} %param.11) | copy-start | bytes 393220
  2.5 37.7 %all-to-all-start = ((f32[32,48,128]{2,1,0:T(8,128)}), f32[32,48,128]{2,1,0:T(8,128)S(1)}, u32[]{:S(2)}, u32[]{:S(2)}) async-start(f32[32,48,128]{2,1,0:T(8,128)} %get-tuple-element.19), calls=%async_computation | async-start | bytes 1572864 | tf_op jit(solution)/shard_map/all_to_all | solution.py:21
  18.8 2.1 %copy-start.2 = (f32[128,64]{0,1:T(8,128)S(1)}, f32[128,64]{0,1:T(8,128)}, u32[]{:S(2)}) copy-start(f32[128,64]{0,1:T(8,128)} %param.10) | copy-start | bytes 98308
  41.5 26.2 %all-to-all-start.1 = ((f32[32,32,128]{2,1,0:T(8,128)}), f32[32,32,128]{2,1,0:T(8,128)S(1)}, u32[]{:S(2)}, u32[]{:S(2)}) async-start(f32[32,32,128]{2,1,0:T(8,128)} %get-tuple-element.22), calls=%async_computation.1 | async-start | bytes 1048576 | tf_op jit(solution)/shard_map/all_to_all | solution.py:21

commit v9 on v7

--- a/solution.py
+++ b/solution.py
@@ -13,18 +13,11 @@
 ROW = ("row_0", "row_1")
 EPS = 1e-06
 SHIFT = 4.0
-HIGH = lax.Precision.HIGHEST
 F32 = jnp.float32
 
 
 def exchange(value, axis):
     return lax.all_to_all(value, axis, 0, 0, tiled=True)
-
-
-def dot(a, b, left, right):
-    return lax.dot_general(
-        a, b, (((left,), (right,)), ((), ())), precision=HIGH, preferred_element_type=F32
-    )
 
 
 def halves(value):
@@ -57,7 +50,7 @@
 
 
 def start_body(
-    block_in, panel_in, valence_in, conduction_in, packed, gap, first, second,
+    block_in, panel_in, valence_in, conduction_in, packed, gap, first,
     block, panel, valence, conduction, arrived,
 ):
     moves = [
@@ -79,7 +72,6 @@
     packed[...] = value
     first[:, 0:16, :] = jnp.broadcast_to(value[None], (32, 16, 128))
     first[:, 16:48, :] = jnp.broadcast_to(panel[:, 0:128][None], (32, 32, 128))
-    second[...] = jnp.broadcast_to(panel[:, 128:256][None], second.shape)
     rows = lax.broadcasted_iota(jnp.int32, (32, 32), 0)
     lanes = lax.broadcasted_iota(jnp.int32, (32, 32), 1)
     column = jnp.sum(jnp.where(rows == lanes, conduction[...], 0.0), axis=1, keepdims=True)
@@ -88,9 +80,14 @@
     gap[...] = upper - jnp.concatenate([valence[...], valence[...]], axis=1) - SHIFT
 
 
+def spread_body(panel, second):
+    second[...] = jnp.broadcast_to(panel[:, 128:256][None], second.shape)
+
+
 def points_of(rows, panel):
-    lo = dot(rows, panel[:, 0].reshape(512, 128), 0, 0)
-    hi = dot(rows, panel[:, 1].reshape(512, 128), 0, 0)
+    rows = halves(rows.T)
+    lo = dot_halves(rows, halves(panel[:, 0].reshape(512, 128)))
+    hi = dot_halves(rows, halves(panel[:, 1].reshape(512, 128)))
     return lo[0:64] + hi[64:128]
 
 
@@ -132,10 +129,14 @@
 
 
 def conduct_body(parts, panel, out):
-    back = jnp.sum(parts[...], axis=0)
+    back = jnp.sum(parts[...], axis=0).T
     zero = jnp.zeros_like(back)
-    lo = dot(panel[:, 0].reshape(512, 128), jnp.concatenate([back, zero], axis=0), 1, 1)
-    hi = dot(panel[:, 1].reshape(512, 128), jnp.concatenate([zero, back], axis=0), 1, 1)
+    lo = dot_halves(
+        halves(panel[:, 0].reshape(512, 128)), halves(jnp.concatenate([back, zero], axis=1))
+    )
+    hi = dot_halves(
+        halves(panel[:, 1].reshape(512, 128)), halves(jnp.concatenate([zero, back], axis=1))
+    )
     out[...] = (lo + hi).reshape(32, 16, 128)
 
 
@@ -198,14 +199,13 @@
 
 
 def shards(excitons, valence_energy, conduction_energy, psi_valence, psi_conduction, screened):
-    x, gap, first, second = pl.pallas_call(
+    x, gap, first = pl.pallas_call(
         start_body,
         out_shape=tuple(
-            jax.ShapeDtypeStruct(shape, F32)
-            for shape in [(16, 128), (16, 128), (32, 48, 128), (32, 32, 128)]
+            jax.ShapeDtypeStruct(shape, F32) for shape in [(16, 128), (16, 128), (32, 48, 128)]
         ),
         in_specs=[pl.BlockSpec(memory_space=pltpu.HBM)] * 4,
-        out_specs=(pl.BlockSpec(memory_space=pltpu.VMEM),) * 4,
+        out_specs=(pl.BlockSpec(memory_space=pltpu.VMEM),) * 3,
         scratch_shapes=[
             pltpu.VMEM((32, 64), F32),
             pltpu.VMEM((32, 256), F32),
@@ -229,6 +229,8 @@
     first = exchange(first, COL)
     panel_conduction = lax.all_gather(psi_conduction.T, ROW, axis=0, tiled=True)
     panel_conduction = panel_conduction.reshape(32, 2, 16, 128)
+    (second,) = call(spread_body, [(32, 32, 128)], "spread")(psi_valence.T)
+    panel_conduction, second = lax.optimization_barrier((panel_conduction, second))
 
     def returned(back):
         (back,) = call(pair_body, [(8, 64, 128)], "pair")(exchange(back, "row_1"))

time: 202 us -> 201 us (level)
  no operation moved by 1% of the time
where the time goes in v9:
time: 201 us; the launch traced here: 200 us
  blocking collectives  168 us (84%)
  starting transfers between devices  23.2 us (12%)
  Pallas kernels  8.76 us (4%)
    all_to_all x10, blocking collectives, exchange(): return lax.all_to_all(value, axis, 0, 0, tiled=True)  123 us
    all_to_all x2, starting transfers between devices, exchange(): return lax.all_to_all(value, axis, 0, 0, tiled=True)  23.2 us
    all_gather x1, blocking collectives, shards(): panel_conduction = lax.all_gather(psi_conduction.T, ROW, axis=0, tiled=True)  19.8 us
    all_gather x1, blocking collectives, shards(): image = lax.all_gather(image, ROW, axis=0, tiled=True)  17.8 us
    all_gather x1, blocking collectives, shards(): image = lax.all_gather(exchange(image, 'row_0'), 'row_1', axis=0)  6.95 us
  transfers between devices with their start and end apart: 2, of which 0 were waited for; matrix products, arithmetic and copies ran while one was open for 0% of the time, Pallas kernels for 0%

profile of v9, /device:TPU:1, one launch (start us, length us, event | category | flops | bytes accessed | tf_op | source)
XLA Modules:
  0.0 200.3 jit_solution(6248686909338424348)
XLA Ops:
  0.6 1.8 start.1
  2.5 13.7 %all-to-all-start = ((f32[32,48,128]{2,1,0:T(8,128)}), f32[32,48,128]{2,1,0:T(8,128)S(1)}, u32[]{:S(2)}, u32[]{:S(2)}) async-start(f32[32,48,128]{2,1,0:T(8,128)} %get-tuple-element.19), calls=%async_computation | async-start | bytes 1572864 | tf_op jit(solution)/shard_map/all_to_all | solution.py:20
  16.2 0.9 spread.1
  17.1 19.8 %all_gather.12 = f32[1024,128]{1,0:T(8,128)S(1)} all-gather(f32[64,128]{1,0:T(8,128)S(1)} %bitcast.15), channel_id=1, replica_groups=mesh['row_0'=8,'row_1'=2,'col_0'=4,'col_1'=8] {'row_0','row_1'}, dimensions={0}, use_global_device_ids=true | all-gather | bytes 557056 | tf_op jit(solution)/shard_map/all_gather | solution.py:230
  36.9 0.4 points_one.1
  37.3 9.5 %all-to-all-start.1 = ((f32[32,32,128]{2,1,0:T(8,128)}), f32[32,32,128]{2,1,0:T(8,128)S(1)}, u32[]{:S(2)}, u32[]{:S(2)}) async-start(f32[32,32,128]{2,1,0:T(8,128)} %spread.1), calls=%async_computation.1 | async-start | bytes 1048576 | tf_op jit(solution)/shard_map/all_to_all | solution.py:20
  46.9 17.8 %all_gather.13.image = f32[1024,128]{1,0:T(8,128)S(1)} all-gather(f32[64,128]{1,0:T(8,128)S(1)} %points_one.1), channel_id=1, replica_groups=mesh['row_0'=8,'row_1'=2,'col_0'=4,'col_1'=8] {'row_0','row_1'}, dimensions={0}, use_global_device_ids=true | all-gather | bytes 557056 | tf_op jit(solution)/shard_map/all_gather | solution.py:244
  64.7 1.4 weigh_one.1
  66.1 3.9 %all_to_all.60.parts = f32[2,8,64,128]{3,2,1,0:T(8,128)S(1)} all-to-all(f32[2,8,64,128]{3,2,1,0:T(8,128)S(1)} %weigh_one.1), channel_id=1, replica_groups=mesh['row_0'=8,'row_1'=2,'col_0'=4,'col_1'=8] {'row_1'}, dimensions={0} | all-to-all | bytes 1048576 | tf_op jit(solution)/shard_map/all_to_all | solution.py:20
  70.1 15.4 %all_to_all.61.parts = f32[8,64,128]{2,1,0:T(8,128)S(1)} all-to-all(f32[8,64,128]{2,1,0:T(8,128)S(1)} %pair.2), channel_id=1, replica_groups=mesh['row_0'=8,'row_1'=2,'col_0'=4,'col_1'=8] {'row_0'}, dimensions={0} | all-to-all | bytes 524288 | tf_op jit(solution)/shard_map/all_to_all | solution.py:20
  85.5 0.5 conduct.2
  86.0 18.5 %all_to_all.62.parts = f32[32,16,128]{2,1,0:T(8,128)S(1)} all-to-all(f32[32,16,128]{2,1,0:T(8,128)S(1)} %conduct.2), channel_id=1, replica_groups=mesh['row_0'=8,'row_1'=2,'col_0'=4,'col_1'=8] {'col_0','col_1'}, dimensions={0} | all-to-all | bytes 524288 | tf_op jit(solution)/shard_map/all_to_all | solution.py:20
  104.5 14.6 %all_to_all.63.y_rows = f32[32,16,128]{2,1,0:T(8,128)S(1)} all-to-all(f32[32,16,128]{2,1,0:T(8,128)S(1)} %get-tuple-element.26), channel_id=1, replica_groups=mesh['row_0'=8,'row_1'=2,'col_0'=4,'col_1'=8] {'col_0','col_1'}, dimensions={0} | all-to-all | bytes 524288 | tf_op jit(solution)/shard_map/all_to_all | solution.py:20
  119.1 0.5 points_two.1
  119.6 12.4 %all_to_all.64 = f32[8,72,128]{2,1,0:T(8,128)S(1)} all-to-all(f32[8,72,128]{2,1,0:T(8,128)S(1)} %points_two.1), channel_id=1, replica_groups=mesh['row_0'=8,'row_1'=2,'col_0'=4,'col_1'=8] {'row_0'}, dimensions={0} | all-to-all | bytes 589824 | tf_op jit(solution)/shard_map/all_to_all | solution.py:20
  132.0 6.9 %all-gather = f32[16,72,128]{2,1,0:T(8,128)S(1)} all-gather(f32[8,72,128]{2,1,0:T(8,128)S(1)} %all_to_all.64), channel_id=2, replica_groups=mesh['row_0'=8,'row_1'=2,'col_0'=4,'col_1'=8] {'row_1'}, dimensions={0}, use_global_device_ids=true | all-gather | bytes 884736 | tf_op jit(solution)/shard_map/all_gather | solution.py:252
  139.0 1.4 weigh_two.1
  140.4 4.2 %all_to_all.65.parts = f32[2,8,64,128]{3,2,1,0:T(8,128)S(1)} all-to-all(f32[2,8,64,128]{3,2,1,0:T(8,128)S(1)} %get-tuple-element.27), channel_id=1, replica_groups=mesh['row_0'=8,'row_1'=2,'col_0'=4,'col_1'=8] {'row_1'}, dimensions={0} | all-to-all | bytes 1048576 | tf_op jit(solution)/shard_map/all_to_all | solution.py:20
  144.6 14.8 %all_to_all.66.parts = f32[8,64,128]{2,1,0:T(8,128)S(1)} all-to-all(f32[8,64,128]{2,1,0:T(8,128)S(1)} %pair.3), channel_id=1, replica_groups=mesh['row_0'=8,'row_1'=2,'col_0'=4,'col_1'=8] {'row_0'}, dimensions={0} | all-to-all | bytes 524288 | tf_op jit(solution)/shard_map/all_to_all | solution.py:20
  159.3 0.5 conduct.3
  159.9 13.7 %all_to_all.67.parts = f32[32,16,128]{2,1,0:T(8,128)S(1)} all-to-all(f32[32,16,128]{2,1,0:T(8,128)S(1)} %conduct.3), channel_id=1, replica_groups=mesh['row_0'=8,'row_1'=2,'col_0'=4,'col_1'=8] {'col_0','col_1'}, dimensions={0} | all-to-all | bytes 524288 | tf_op jit(solution)/shard_map/all_to_all | solution.py:20
  173.8 16.2 %all_to_all.68.parts = f32[64,1,128]{2,1,0:T(1,128)S(1)} all-to-all(f32[64,1,128]{2,1,0:T(1,128)S(1)} %get-tuple-element.30), channel_id=1, replica_groups=mesh['row_0'=8,'row_1'=2,'col_0'=4,'col_1'=8] {'row_0','row_1','col_0'}, dimensions={0} | all-to-all | bytes 65536 | tf_op jit(solution)/shard_map/all_to_all | solution.py:20
  190.1 9.3 %all_to_all.69.parts = f32[8,1,128]{2,1,0:T(1,128)S(1)} all-to-all(f32[8,1,128]{2,1,0:T(1,128)S(1)} %fold.1), channel_id=1, replica_groups=mesh['row_0'=8,'row_1'=2,'col_0'=4,'col_1'=8] {'col_1'}, dimensions={0} | all-to-all | bytes 8192 | tf_op jit(solution)/shard_map/all_to_all | solution.py:20
  199.3 1.0 finish.1
  (13 shorter events, 0.4 us)
Async XLA Ops:
  2.4 13.7 %copy-start.1 = (f32[256,32]{0,1:T(8,128)S(1)}, f32[256,32]{0,1:T(8,128)}, u32[]{:S(2)}) copy-start(f32[256,32]{0,1:T(8,128)} %param.9) | copy-start | bytes 98308
  2.5 34.4 %all-to-all-start = ((f32[32,48,128]{2,1,0:T(8,128)}), f32[32,48,128]{2,1,0:T(8,128)S(1)}, u32[]{:S(2)}, u32[]{:S(2)}) async-start(f32[32,48,128]{2,1,0:T(8,128)} %get-tuple-element.19), calls=%async_computation | async-start | bytes 1572864 | tf_op jit(solution)/shard_map/all_to_all | solution.py:20
  16.2 0.9 copy-start.2
  37.3 27.4 %all-to-all-start.1 = ((f32[32,32,128]{2,1,0:T(8,128)}), f32[32,32,128]{2,1,0:T(8,128)S(1)}, u32[]{:S(2)}, u32[]{:S(2)}) async-start(f32[32,32,128]{2,1,0:T(8,128)} %spread.1), calls=%async_computation.1 | async-start | bytes 1048576 | tf_op jit(solution)/shard_map/all_to_all | solution.py:20
  46.9 17.9 %copy-start = (f32[256,128]{1,0:T(8,128)S(1)}, f32[256,128]{1,0:T(8,128)}, u32[]{:S(2)}) copy-start(f32[256,128]{1,0:T(8,128)} %screened.3) | copy-start | bytes 393220

commit v10 on v8

--- a/solution.py
+++ b/solution.py
@@ -13,18 +13,11 @@
 ROW = ("row_0", "row_1")
 EPS = 1e-06
 SHIFT = 4.0
-HIGH = lax.Precision.HIGHEST
 F32 = jnp.float32
 
 
 def exchange(value, axis):
     return lax.all_to_all(value, axis, 0, 0, tiled=True)
-
-
-def dot(a, b, left, right):
-    return lax.dot_general(
-        a, b, (((left,), (right,)), ((), ())), precision=HIGH, preferred_element_type=F32
-    )
 
 
 def halves(value):
@@ -60,13 +53,13 @@
     return jnp.where(lax.axis_index("row_1") == 0, zero, one)
 
 
-def spread_half(out, at, half):
-    out[:, at : at + 16, :] = jnp.broadcast_to(half[:, 0:128][None], (32, 16, 128))
-    out[:, at + 16 : at + 32, :] = jnp.broadcast_to(half[:, 128:256][None], (32, 16, 128))
+def spread_half(out, at, low, high):
+    out[:, at : at + 16, :] = jnp.broadcast_to(low[None], (32, 16, 128))
+    out[:, at + 16 : at + 32, :] = jnp.broadcast_to(high[None], (32, 16, 128))
 
 
 def start_body(
-    block_in, panel_in, valence_in, conduction_in, packed, gap, first,
+    block_in, panel_in, valence_in, conduction_in, screened_in, packed, gap, first, pair,
     block, panel, valence, conduction, arrived,
 ):
     moves = [
@@ -77,34 +70,44 @@
                 (panel_in, panel),
                 (valence_in, valence),
                 (conduction_in, conduction),
+                (screened_in, pair.at[64:320]),
             ]
         )
     ]
     for move in moves:
         move.start()
-    for move in moves:
+    for move in moves[:4]:
         move.wait()
     value = jnp.concatenate([block[0:16, :], block[16:32, :]], axis=1)
     packed[...] = value
     first[:, 0:16, :] = jnp.broadcast_to(value[None], (32, 16, 128))
-    spread_half(first, 16, mine(panel[0:16, :], panel[16:32, :]))
+    half = mine(panel[0:16, :], panel[16:32, :])
+    spread_half(first, 16, half[:, 0:128], half[:, 128:256])
     rows = lax.broadcasted_iota(jnp.int32, (32, 32), 0)
     lanes = lax.broadcasted_iota(jnp.int32, (32, 32), 1)
     column = jnp.sum(jnp.where(rows == lanes, conduction[...], 0.0), axis=1, keepdims=True)
     half = lax.broadcasted_iota(jnp.int32, (16, 128), 1) < 64
     upper = jnp.where(half, column[0:16], column[16:32])
     gap[...] = upper - jnp.concatenate([valence[...], valence[...]], axis=1) - SHIFT
+    pair[0:32, :] = panel[:, 0:128]
+    pair[32:64, :] = panel[:, 128:256]
+    moves[4].wait()
 
 
 def points_of(rows, panel):
-    lo = dot(rows, panel[:, 0].reshape(512, 128), 0, 0)
-    hi = dot(rows, panel[:, 1].reshape(512, 128), 0, 0)
+    rows = halves(rows.T)
+    lo = dot_halves(rows, halves(panel[:, 0].reshape(512, 128)))
+    hi = dot_halves(rows, halves(panel[:, 1].reshape(512, 128)))
     return lo[0:64] + hi[64:128]
 
 
-def first_points_body(first, panel, blocks, out, second):
+def spread_body(pair, second):
+    low = mine(pair[1, 0:16, :], pair[0, 16:32, :])
+    spread_half(second, 0, low, mine(pair[1, 32:48, :], pair[0, 48:64, :]))
+
+
+def first_points_body(first, panel, out):
     out[...] = points_of(first[:, 0:16, :].reshape(512, 128), panel)
-    spread_half(second, 0, mine(blocks[1, 0:16, :], blocks[0, 16:32, :]))
 
 
 def second_points_body(first, y_rows, panel, out):
@@ -141,9 +144,9 @@
     moments[...] = jnp.sum(arrived[:, 32:40, :], axis=0)
 
 
-def weigh_body(partials, screened, first, second, out):
-    zero = (partials[0, 0] + partials[1, 0]) * screened[0]
-    one = (partials[0, 1] + partials[1, 1]) * screened[1]
+def weigh_body(partials, pair, first, second, out):
+    zero = (partials[0, 0] + partials[1, 0]) * pair[0, 64:320, :]
+    one = (partials[0, 1] + partials[1, 1]) * pair[1, 64:320, :]
     weighted = jnp.concatenate([mine(zero, one), mine(one, zero)], axis=0)
     back = dot_halves(shared_panel(first, second), halves(weighted))
     out[...] = back.reshape(16, 32, 128)
@@ -152,10 +155,14 @@
 def conduct_body(parts, panel, out):
     sums = jnp.sum(parts[...], axis=0)
     back = jnp.stack([sums[0].reshape(2, 16, 128), sums[1].reshape(2, 16, 128)], axis=1)
-    back = back.reshape(64, 128)
+    back = back.reshape(64, 128).T
     zero = jnp.zeros_like(back)
-    lo = dot(panel[:, 0].reshape(512, 128), jnp.concatenate([back, zero], axis=0), 1, 1)
-    hi = dot(panel[:, 1].reshape(512, 128), jnp.concatenate([zero, back], axis=0), 1, 1)
+    lo = dot_halves(
+        halves(panel[:, 0].reshape(512, 128)), halves(jnp.concatenate([back, zero], axis=1))
+    )
+    hi = dot_halves(
+        halves(panel[:, 1].reshape(512, 128)), halves(jnp.concatenate([zero, back], axis=1))
+    )
     out[...] = (lo + hi).reshape(32, 16, 128)
 
 
@@ -218,19 +225,20 @@
 
 
 def shards(excitons, valence_energy, conduction_energy, psi_valence, psi_conduction, screened):
-    x, gap, first = pl.pallas_call(
+    x, gap, first, pair = pl.pallas_call(
         start_body,
         out_shape=tuple(
-            jax.ShapeDtypeStruct(shape, F32) for shape in [(16, 128), (16, 128), (32, 48, 128)]
+            jax.ShapeDtypeStruct(shape, F32)
+            for shape in [(16, 128), (16, 128), (32, 48, 128), (320, 128)]
         ),
-        in_specs=[pl.BlockSpec(memory_space=pltpu.HBM)] * 4,
-        out_specs=(pl.BlockSpec(memory_space=pltpu.VMEM),) * 3,
+        in_specs=[pl.BlockSpec(memory_space=pltpu.HBM)] * 5,
+        out_specs=(pl.BlockSpec(memory_space=pltpu.VMEM),) * 4,
         scratch_shapes=[
             pltpu.VMEM((32, 64), F32),
             pltpu.VMEM((32, 256), F32),
             pltpu.VMEM((1, 64), F32),
             pltpu.VMEM((1, 32), F32),
-            pltpu.SemaphoreType.DMA((4,)),
+            pltpu.SemaphoreType.DMA((5,)),
         ],
         name="start",
         compiler_params=pltpu.CompilerParams(vmem_limit_bytes=32 * 1024 * 1024),
@@ -242,6 +250,7 @@
                 psi_valence.T,
                 valence_energy[None],
                 conduction_energy[None],
+                screened,
             )
         )
     )
@@ -249,22 +258,21 @@
     panel_conduction = lax.all_gather(psi_conduction.T, ROW, axis=0, tiled=True)
     panel_conduction = panel_conduction.reshape(32, 2, 16, 128)
 
-    blocks = lax.all_gather(psi_valence.T, "row_1", axis=0)
-    pair_screened = lax.all_gather(screened, "row_1", axis=0)
-    blocks, pair_screened = lax.optimization_barrier((blocks, pair_screened))
+    pair = lax.all_gather(pair, "row_1", axis=0)
+    (second,) = call(spread_body, [(32, 32, 128)], "spread")(pair)
+    panel_conduction, second = lax.optimization_barrier((panel_conduction, second))
 
     def returned(partial):
         partials = lax.all_gather(partial, "row_1", axis=0)
         (back,) = call(weigh_body, [(16, 32, 128)], "weigh")(
-            partials, pair_screened, first, second
+            partials, pair, first, second
         )
         back = exchange(back, ROW).reshape(8, 2, 32, 128)
         (kernel,) = call(conduct_body, [(32, 16, 128)], "conduct")(back, panel_conduction)
         return exchange(kernel, COL)
 
-    image, second = call(first_points_body, [(64, 128), (32, 32, 128)], "points_one")(
-        first, panel_conduction, blocks
-    )
+    (image,) = call(first_points_body, [(64, 128)], "points_one")(first, panel_conduction)
+    image, second = lax.optimization_barrier((image, second))
     second = exchange(second, COL)
     image = lax.all_gather(image, ROW, axis=0, tiled=True).reshape(32, 2, 16, 128)
     (partial,) = call(first_partial_body, [(2, 256, 128)], "partial_one")(image, first, second)

time: 204 us -> 201 us (0.985)
    all_gather x2 -> x1, blocking collectives: 4.57 us -> 2.63 us  [shards(): pair = lax.all_gather(pair, 'row_1', axis=0)]
where the time goes in v10:
time: 201 us; the launch traced here: 200 us
  blocking collectives  168 us (84%)
  starting transfers between devices  23.2 us (12%)
  Pallas kernels  8.22 us (4%)
    all_to_all x8, blocking collectives, exchange(): return lax.all_to_all(value, axis, 0, 0, tiled=True)  125 us
    all_to_all x2, starting transfers between devices, exchange(): return lax.all_to_all(value, axis, 0, 0, tiled=True)  23.2 us
    all_gather x1, blocking collectives, shards(): panel_conduction = lax.all_gather(psi_conduction.T, ROW, axis=0, tiled=True)  19.2 us
    all_gather x1, blocking collectives, shards(): lax.all_gather(image, ROW, axis=0, tiled=True).reshape(32, 2, 16, 128)  16.6 us
    all_gather x2, blocking collectives, returned(): partials = lax.all_gather(partial, 'row_1', axis=0)  5.03 us
  transfers between devices with their start and end apart: 2, of which 0 were waited for; matrix products, arithmetic and copies ran while one was open for 0% of the time, Pallas kernels for 0%

profile of v10, /device:TPU:1, one launch (start us, length us, event | category | flops | bytes accessed | tf_op | source)
XLA Modules:
  0.0 200.3 jit_solution(6080849323427171388)
XLA Ops:
  0.6 1.9 start.1
  2.5 13.7 %all-to-all-start = ((f32[32,48,128]{2,1,0:T(8,128)}), f32[32,48,128]{2,1,0:T(8,128)S(1)}, u32[]{:S(2)}, u32[]{:S(2)}) async-start(f32[32,48,128]{2,1,0:T(8,128)} %get-tuple-element.20), calls=%async_computation | async-start | bytes 1572864 | tf_op jit(solution)/shard_map/all_to_all | solution.py:20
  16.3 2.6 %all-gather = f32[640,128]{1,0:T(8,128)S(1)} all-gather(f32[320,128]{1,0:T(8,128)S(1)} %get-tuple-element.21), channel_id=2, replica_groups=mesh['row_0'=8,'row_1'=2,'col_0'=4,'col_1'=8] {'row_1'}, dimensions={0}, use_global_device_ids=true | all-gather | bytes 491520 | tf_op jit(solution)/shard_map/all_gather | solution.py:261
  18.9 0.9 spread.1
  19.8 19.2 %all_gather.24 = f32[1024,128]{1,0:T(8,128)S(1)} all-gather(f32[64,128]{1,0:T(8,128)S(1)} %bitcast.27), channel_id=1, replica_groups=mesh['row_0'=8,'row_1'=2,'col_0'=4,'col_1'=8] {'row_0','row_1'}, dimensions={0}, use_global_device_ids=true | all-gather | bytes 557056 | tf_op jit(solution)/shard_map/all_gather | solution.py:258
  39.4 9.5 %all-to-all-start.1 = ((f32[32,32,128]{2,1,0:T(8,128)}), f32[32,32,128]{2,1,0:T(8,128)S(1)}, u32[]{:S(2)}, u32[]{:S(2)}) async-start(f32[32,32,128]{2,1,0:T(8,128)} %spread.1), calls=%async_computation.1 | async-start | bytes 1048576 | tf_op jit(solution)/shard_map/all_to_all | solution.py:20
  48.9 16.6 %all_gather.27 = f32[1024,128]{1,0:T(8,128)S(1)} all-gather(f32[64,128]{1,0:T(8,128)S(1)} %points_one.1), channel_id=1, replica_groups=mesh['row_0'=8,'row_1'=2,'col_0'=4,'col_1'=8] {'row_0','row_1'}, dimensions={0}, use_global_device_ids=true | all-gather | bytes 557056 | tf_op jit(solution)/shard_map/all_gather | solution.py:277
  65.6 0.5 partial_one.1
  66.1 2.8 %all-gather.1 = f32[4,256,128]{2,1,0:T(8,128)S(1)} all-gather(f32[2,256,128]{2,1,0:T(8,128)S(1)} %partial_one.1), channel_id=3, replica_groups=mesh['row_0'=8,'row_1'=2,'col_0'=4,'col_1'=8] {'row_1'}, dimensions={0}, use_global_device_ids=true | all-gather | bytes 786432 | tf_op jit(solution)/shard_map/all_gather | solution.py:266
  69.0 0.6 weigh.2
  69.6 16.2 %all_to_all.50 = f32[16,32,128]{2,1,0:T(8,128)S(1)} all-to-all(f32[16,32,128]{2,1,0:T(8,128)S(1)} %weigh.2), channel_id=1, replica_groups=mesh['row_0'=8,'row_1'=2,'col_0'=4,'col_1'=8] {'row_0','row_1'}, dimensions={0} | all-to-all | bytes 524288 | tf_op jit(solution)/shard_map/all_to_all | solution.py:20
  85.8 0.5 conduct.2
  86.3 19.8 %all_to_all.51.parts = f32[32,16,128]{2,1,0:T(8,128)S(1)} all-to-all(f32[32,16,128]{2,1,0:T(8,128)S(1)} %conduct.2), channel_id=1, replica_groups=mesh['row_0'=8,'row_1'=2,'col_0'=4,'col_1'=8] {'col_0','col_1'}, dimensions={0} | all-to-all | bytes 524288 | tf_op jit(solution)/shard_map/all_to_all | solution.py:20
  106.1 15.6 %all_to_all.52.y_rows = f32[32,16,128]{2,1,0:T(8,128)S(1)} all-to-all(f32[32,16,128]{2,1,0:T(8,128)S(1)} %get-tuple-element.28), channel_id=1, replica_groups=mesh['row_0'=8,'row_1'=2,'col_0'=4,'col_1'=8] {'col_0','col_1'}, dimensions={0} | all-to-all | bytes 524288 | tf_op jit(solution)/shard_map/all_to_all | solution.py:20
  122.2 19.2 %all_to_all.53.arrived = f32[16,40,128]{2,1,0:T(8,128)S(1)} all-to-all(f32[16,40,128]{2,1,0:T(8,128)S(1)} %bitcast.24), channel_id=1, replica_groups=mesh['row_0'=8,'row_1'=2,'col_0'=4,'col_1'=8] {'row_0','row_1'}, dimensions={0} | all-to-all | bytes 655360 | tf_op jit(solution)/shard_map/all_to_all | solution.py:20
  141.3 0.5 partial_two.1
  141.9 2.2 %all-gather.2 = f32[4,256,128]{2,1,0:T(8,128)S(1)} all-gather(f32[2,256,128]{2,1,0:T(8,128)S(1)} %get-tuple-element.29), channel_id=4, replica_groups=mesh['row_0'=8,'row_1'=2,'col_0'=4,'col_1'=8] {'row_1'}, dimensions={0}, use_global_device_ids=true | all-gather | bytes 786432 | tf_op jit(solution)/shard_map/all_gather | solution.py:266
  144.1 0.6 weigh.3
  144.7 14.5 %all_to_all.54 = f32[16,32,128]{2,1,0:T(8,128)S(1)} all-to-all(f32[16,32,128]{2,1,0:T(8,128)S(1)} %weigh.3), channel_id=1, replica_groups=mesh['row_0'=8,'row_1'=2,'col_0'=4,'col_1'=8] {'row_0','row_1'}, dimensions={0} | all-to-all | bytes 524288 | tf_op jit(solution)/shard_map/all_to_all | solution.py:20
  159.2 0.5 conduct.3
  159.7 14.7 %all_to_all.55.parts = f32[32,16,128]{2,1,0:T(8,128)S(1)} all-to-all(f32[32,16,128]{2,1,0:T(8,128)S(1)} %conduct.3), channel_id=1, replica_groups=mesh['row_0'=8,'row_1'=2,'col_0'=4,'col_1'=8] {'col_0','col_1'}, dimensions={0} | all-to-all | bytes 524288 | tf_op jit(solution)/shard_map/all_to_all | solution.py:20
  174.6 15.6 %all_to_all.56.parts = f32[64,1,128]{2,1,0:T(1,128)S(1)} all-to-all(f32[64,1,128]{2,1,0:T(1,128)S(1)} %get-tuple-element.32), channel_id=1, replica_groups=mesh['row_0'=8,'row_1'=2,'col_0'=4,'col_1'=8] {'row_0','row_1','col_0'}, dimensions={0} | all-to-all | bytes 65536 | tf_op jit(solution)/shard_map/all_to_all | solution.py:20
  190.2 9.1 %all_to_all.57.parts = f32[8,1,128]{2,1,0:T(1,128)S(1)} all-to-all(f32[8,1,128]{2,1,0:T(1,128)S(1)} %fold.1), channel_id=1, replica_groups=mesh['row_0'=8,'row_1'=2,'col_0'=4,'col_1'=8] {'col_1'}, dimensions={0} | all-to-all | bytes 8192 | tf_op jit(solution)/shard_map/all_to_all | solution.py:20
  199.4 1.0 finish.1
  (9 shorter events, 1.3 us)
Async XLA Ops:
  2.5 36.4 %all-to-all-start = ((f32[32,48,128]{2,1,0:T(8,128)}), f32[32,48,128]{2,1,0:T(8,128)S(1)}, u32[]{:S(2)}, u32[]{:S(2)}) async-start(f32[32,48,128]{2,1,0:T(8,128)} %get-tuple-element.20), calls=%async_computation | async-start | bytes 1572864 | tf_op jit(solution)/shard_map/all_to_all | solution.py:20
  18.9 0.9 copy-start
  39.4 26.2 %all-to-all-start.1 = ((f32[32,32,128]{2,1,0:T(8,128)}), f32[32,32,128]{2,1,0:T(8,128)S(1)}, u32[]{:S(2)}, u32[]{:S(2)}) async-start(f32[32,32,128]{2,1,0:T(8,128)} %spread.1), calls=%async_computation.1 | async-start | bytes 1048576 | tf_op jit(solution)/shard_map/all_to_all | solution.py:20

commit v11 on v10

--- a/solution.py
+++ b/solution.py
@@ -53,14 +53,9 @@
     return jnp.where(lax.axis_index("row_1") == 0, zero, one)
 
 
-def spread_half(out, at, low, high):
-    out[:, at : at + 16, :] = jnp.broadcast_to(low[None], (32, 16, 128))
-    out[:, at + 16 : at + 32, :] = jnp.broadcast_to(high[None], (32, 16, 128))
-
-
 def start_body(
     block_in, panel_in, valence_in, conduction_in, screened_in, packed, gap, first, pair,
-    block, panel, valence, conduction, arrived,
+    block, panel, valence, conduction, tile, arrived, sent,
 ):
     moves = [
         pltpu.make_async_copy(source, target, arrived.at[i])
@@ -80,9 +75,13 @@
         move.wait()
     value = jnp.concatenate([block[0:16, :], block[16:32, :]], axis=1)
     packed[...] = value
-    first[:, 0:16, :] = jnp.broadcast_to(value[None], (32, 16, 128))
     half = mine(panel[0:16, :], panel[16:32, :])
-    spread_half(first, 16, half[:, 0:128], half[:, 128:256])
+    tile[0:16, :] = value
+    tile[16:32, :] = half[:, 0:128]
+    tile[32:48, :] = half[:, 128:256]
+    spreads = [pltpu.make_async_copy(tile, first.at[i], sent.at[i]) for i in range(32)]
+    for spread in spreads:
+        spread.start()
     rows = lax.broadcasted_iota(jnp.int32, (32, 32), 0)
     lanes = lax.broadcasted_iota(jnp.int32, (32, 32), 1)
     column = jnp.sum(jnp.where(rows == lanes, conduction[...], 0.0), axis=1, keepdims=True)
@@ -92,6 +91,8 @@
     pair[0:32, :] = panel[:, 0:128]
     pair[32:64, :] = panel[:, 128:256]
     moves[4].wait()
+    for spread in spreads:
+        spread.wait()
 
 
 def points_of(rows, panel):
@@ -103,7 +104,9 @@
 
 def spread_body(pair, second):
     low = mine(pair[1, 0:16, :], pair[0, 16:32, :])
-    spread_half(second, 0, low, mine(pair[1, 32:48, :], pair[0, 48:64, :]))
+    high = mine(pair[1, 32:48, :], pair[0, 48:64, :])
+    second[:, 0:16, :] = jnp.broadcast_to(low[None], (32, 16, 128))
+    second[:, 16:32, :] = jnp.broadcast_to(high[None], (32, 16, 128))
 
 
 def first_points_body(first, panel, out):
@@ -232,13 +235,17 @@
             for shape in [(16, 128), (16, 128), (32, 48, 128), (320, 128)]
         ),
         in_specs=[pl.BlockSpec(memory_space=pltpu.HBM)] * 5,
-        out_specs=(pl.BlockSpec(memory_space=pltpu.VMEM),) * 4,
+        out_specs=tuple(
+            pl.BlockSpec(memory_space=pltpu.HBM if i == 2 else pltpu.VMEM) for i in range(4)
+        ),
         scratch_shapes=[
             pltpu.VMEM((32, 64), F32),
             pltpu.VMEM((32, 256), F32),
             pltpu.VMEM((1, 64), F32),
             pltpu.VMEM((1, 32), F32),
+            pltpu.VMEM((48, 128), F32),
             pltpu.SemaphoreType.DMA((5,)),
+            pltpu.SemaphoreType.DMA((32,)),
         ],
         name="start",
         compiler_params=pltpu.CompilerParams(vmem_limit_bytes=32 * 1024 * 1024),
@@ -287,11 +294,11 @@
         image, first, second
     )
     u, q_2, message, scalars = call(
-        last_body, [(16, 128), (16, 128), (64, 1, 128), (1, 128)], "last"
+        last_body, [(16, 128), (16, 128), (8, 1, 128), (1, 128)], "last"
     )(returned(partial), gap, x, y, moments)
-    (message,) = call(fold_body, [(8, 1, 128)], "fold")(exchange(message, (*ROW, "col_0")))
+    (message,) = call(fold_body, [(64, 1, 128)], "fold")(exchange(message, ("row_1", "col_0")))
     out, coefficients = call(finish_body, [(32, 64), (4,)], "finish", smem=(1,))(
-        exchange(message, "col_1"), u, q_2, scalars
+        exchange(message, ("row_0", "col_1")), u, q_2, scalars
     )
     return out.T, coefficients
 

time: 201 us -> 201 us (level)
  no operation moved by 1% of the time
where the time goes in v11:
time: 201 us
  blocking collectives  168 us (84%)
  starting transfers between devices  23.2 us (12%)
  Pallas kernels  8.39 us (4%)
    all_to_all x8, blocking collectives, exchange(): return lax.all_to_all(value, axis, 0, 0, tiled=True)  125 us
    all_to_all x2, starting transfers between devices, exchange(): return lax.all_to_all(value, axis, 0, 0, tiled=True)  23.2 us
    all_gather x1, blocking collectives, shards(): panel_conduction = lax.all_gather(psi_conduction.T, ROW, axis=0, tiled=True)  19.2 us
    all_gather x1, blocking collectives, shards(): lax.all_gather(image, ROW, axis=0, tiled=True).reshape(32, 2, 16, 128)  16.6 us
    all_gather x2, blocking collectives, returned(): partials = lax.all_gather(partial, 'row_1', axis=0)  5.03 us
  transfers between devices with their start and end apart: 2, of which 0 were waited for; matrix products, arithmetic and copies ran while one was open for 0% of the time, Pallas kernels for 0%

profile of v11, /device:TPU:1, one launch (start us, length us, event | category | flops | bytes accessed | tf_op | source)
XLA Modules:
  0.0 200.7 jit_solution(12509086108094365920)
XLA Ops:
  0.6 2.1 %start.1 = (f32[16,128]{1,0:T(8,128)S(1)}, f32[16,128]{1,0:T(8,128)S(1)}, f32[32,48,128]{2,1,0:T(8,128)}, f32[320,128]{1,0:T(8,128)S(1)}) custom-call(f32[32,64]{1,0:T(8,128)} %bitcast.29, f32[32,256]{1,0:T(8,128)} %bitcast.28, f32[1,64]{1,0:T(1,128)} %bitcast.30, f32[1,32]{1,0:T(1,128)} %bitcast.31, f32[256,128]{1,0:T(8,128)} %screened_in.1), custom_call_target="tpu_custom_call" | custom-call | tf_op jit(solution)/shard_map/start/pallas_call | solution.py:231
  2.7 13.7 %all-to-all-start = ((f32[32,48,128]{2,1,0:T(8,128)}), f32[32,48,128]{2,1,0:T(8,128)S(1)}, u32[]{:S(2)}, u32[]{:S(2)}) async-start(f32[32,48,128]{2,1,0:T(8,128)} %get-tuple-element.20), calls=%async_computation | async-start | bytes 1572864 | tf_op jit(solution)/shard_map/all_to_all | solution.py:20
  16.4 2.6 %all-gather = f32[640,128]{1,0:T(8,128)S(1)} all-gather(f32[320,128]{1,0:T(8,128)S(1)} %get-tuple-element.21), channel_id=2, replica_groups=mesh['row_0'=8,'row_1'=2,'col_0'=4,'col_1'=8] {'row_1'}, dimensions={0}, use_global_device_ids=true | all-gather | bytes 491520 | tf_op jit(solution)/shard_map/all_gather | solution.py:268
  19.1 0.9 spread.1
  19.9 19.2 %all_gather.24 = f32[1024,128]{1,0:T(8,128)S(1)} all-gather(f32[64,128]{1,0:T(8,128)S(1)} %bitcast.27), channel_id=1, replica_groups=mesh['row_0'=8,'row_1'=2,'col_0'=4,'col_1'=8] {'row_0','row_1'}, dimensions={0}, use_global_device_ids=true | all-gather | bytes 557056 | tf_op jit(solution)/shard_map/all_gather | solution.py:265
  39.6 9.5 %all-to-all-start.1 = ((f32[32,32,128]{2,1,0:T(8,128)}), f32[32,32,128]{2,1,0:T(8,128)S(1)}, u32[]{:S(2)}, u32[]{:S(2)}) async-start(f32[32,32,128]{2,1,0:T(8,128)} %spread.1), calls=%async_computation.1 | async-start | bytes 1048576 | tf_op jit(solution)/shard_map/all_to_all | solution.py:20
  49.1 16.6 %all_gather.27 = f32[1024,128]{1,0:T(8,128)S(1)} all-gather(f32[64,128]{1,0:T(8,128)S(1)} %points_one.1), channel_id=1, replica_groups=mesh['row_0'=8,'row_1'=2,'col_0'=4,'col_1'=8] {'row_0','row_1'}, dimensions={0}, use_global_device_ids=true | all-gather | bytes 557056 | tf_op jit(solution)/shard_map/all_gather | solution.py:284
  65.8 0.5 partial_one.1
  66.3 2.8 %all-gather.1 = f32[4,256,128]{2,1,0:T(8,128)S(1)} all-gather(f32[2,256,128]{2,1,0:T(8,128)S(1)} %partial_one.1), channel_id=3, replica_groups=mesh['row_0'=8,'row_1'=2,'col_0'=4,'col_1'=8] {'row_1'}, dimensions={0}, use_global_device_ids=true | all-gather | bytes 786432 | tf_op jit(solution)/shard_map/all_gather | solution.py:273
  69.2 0.6 weigh.2
  69.8 16.2 %all_to_all.50 = f32[16,32,128]{2,1,0:T(8,128)S(1)} all-to-all(f32[16,32,128]{2,1,0:T(8,128)S(1)} %weigh.2), channel_id=1, replica_groups=mesh['row_0'=8,'row_1'=2,'col_0'=4,'col_1'=8] {'row_0','row_1'}, dimensions={0} | all-to-all | bytes 524288 | tf_op jit(solution)/shard_map/all_to_all | solution.py:20
  86.0 0.5 conduct.2
  86.5 19.8 %all_to_all.51.parts = f32[32,16,128]{2,1,0:T(8,128)S(1)} all-to-all(f32[32,16,128]{2,1,0:T(8,128)S(1)} %conduct.2), channel_id=1, replica_groups=mesh['row_0'=8,'row_1'=2,'col_0'=4,'col_1'=8] {'col_0','col_1'}, dimensions={0} | all-to-all | bytes 524288 | tf_op jit(solution)/shard_map/all_to_all | solution.py:20
  106.3 15.6 %all_to_all.52.y_rows = f32[32,16,128]{2,1,0:T(8,128)S(1)} all-to-all(f32[32,16,128]{2,1,0:T(8,128)S(1)} %get-tuple-element.28), channel_id=1, replica_groups=mesh['row_0'=8,'row_1'=2,'col_0'=4,'col_1'=8] {'col_0','col_1'}, dimensions={0} | all-to-all | bytes 524288 | tf_op jit(solution)/shard_map/all_to_all | solution.py:20
  122.3 19.2 %all_to_all.53.arrived = f32[16,40,128]{2,1,0:T(8,128)S(1)} all-to-all(f32[16,40,128]{2,1,0:T(8,128)S(1)} %bitcast.24), channel_id=1, replica_groups=mesh['row_0'=8,'row_1'=2,'col_0'=4,'col_1'=8] {'row_0','row_1'}, dimensions={0} | all-to-all | bytes 655360 | tf_op jit(solution)/shard_map/all_to_all | solution.py:20
  141.5 0.5 partial_two.1
  142.0 2.2 %all-gather.2 = f32[4,256,128]{2,1,0:T(8,128)S(1)} all-gather(f32[2,256,128]{2,1,0:T(8,128)S(1)} %get-tuple-element.29), channel_id=4, replica_groups=mesh['row_0'=8,'row_1'=2,'col_0'=4,'col_1'=8] {'row_1'}, dimensions={0}, use_global_device_ids=true | all-gather | bytes 786432 | tf_op jit(solution)/shard_map/all_gather | solution.py:273
  144.2 0.6 weigh.3
  144.8 14.5 %all_to_all.54 = f32[16,32,128]{2,1,0:T(8,128)S(1)} all-to-all(f32[16,32,128]{2,1,0:T(8,128)S(1)} %weigh.3), channel_id=1, replica_groups=mesh['row_0'=8,'row_1'=2,'col_0'=4,'col_1'=8] {'row_0','row_1'}, dimensions={0} | all-to-all | bytes 524288 | tf_op jit(solution)/shard_map/all_to_all | solution.py:20
  159.3 0.5 conduct.3
  159.8 14.7 %all_to_all.55.parts = f32[32,16,128]{2,1,0:T(8,128)S(1)} all-to-all(f32[32,16,128]{2,1,0:T(8,128)S(1)} %conduct.3), channel_id=1, replica_groups=mesh['row_0'=8,'row_1'=2,'col_0'=4,'col_1'=8] {'col_0','col_1'}, dimensions={0} | all-to-all | bytes 524288 | tf_op jit(solution)/shard_map/all_to_all | solution.py:20
  174.8 9.5 %all_to_all.56.parts = f32[8,1,128]{2,1,0:T(1,128)S(1)} all-to-all(f32[8,1,128]{2,1,0:T(1,128)S(1)} %get-tuple-element.32), channel_id=1, replica_groups=mesh['row_0'=8,'row_1'=2,'col_0'=4,'col_1'=8] {'row_1','col_0'}, dimensions={0} | all-to-all | bytes 8192 | tf_op jit(solution)/shard_map/all_to_all | solution.py:20
  184.3 15.4 %all_to_all.57.parts = f32[64,1,128]{2,1,0:T(1,128)S(1)} all-to-all(f32[64,1,128]{2,1,0:T(1,128)S(1)} %fold.1), channel_id=1, replica_groups=mesh['row_0'=8,'row_1'=2,'col_0'=4,'col_1'=8] {'row_0','col_1'}, dimensions={0} | all-to-all | bytes 65536 | tf_op jit(solution)/shard_map/all_to_all | solution.py:20
  199.6 1.0 finish.1
  (9 shorter events, 1.2 us)
Async XLA Ops:
  2.7 36.4 %all-to-all-start = ((f32[32,48,128]{2,1,0:T(8,128)}), f32[32,48,128]{2,1,0:T(8,128)S(1)}, u32[]{:S(2)}, u32[]{:S(2)}) async-start(f32[32,48,128]{2,1,0:T(8,128)} %get-tuple-element.20), calls=%async_computation | async-start | bytes 1572864 | tf_op jit(solution)/shard_map/all_to_all | solution.py:20
  19.1 0.9 copy-start
  39.6 26.2 %all-to-all-start.1 = ((f32[32,32,128]{2,1,0:T(8,128)}), f32[32,32,128]{2,1,0:T(8,128)S(1)}, u32[]{:S(2)}, u32[]{:S(2)}) async-start(f32[32,32,128]{2,1,0:T(8,128)} %spread.1), calls=%async_computation.1 | async-start | bytes 1048576 | tf_op jit(solution)/shard_map/all_to_all | solution.py:20

commit v12 on v10

--- a/solution.py
+++ b/solution.py
@@ -11,6 +11,7 @@
 COUNT = NV * NC
 COL = ("col_0", "col_1")
 ROW = ("row_0", "row_1")
+CORE_MAJOR = ("row_1", "row_0")
 EPS = 1e-06
 SHIFT = 4.0
 F32 = jnp.float32
@@ -120,7 +121,7 @@
         at = 16 * core
         message = [image[at : at + 16], image[at + 32 : at + 48], *sums]
         message = jnp.concatenate(message, axis=0)
-        out[:, core] = jnp.broadcast_to(message[None], (8, 40, 128))
+        out[core] = jnp.broadcast_to(message[None], (8, 40, 128))
 
 
 def shared_panel(first, second):
@@ -140,8 +141,9 @@
 
 
 def second_partial_body(arrived, first, second, out, moments):
-    partial_points(arrived[:, 0:32, :].reshape(512, 128), first, second, out)
-    moments[...] = jnp.sum(arrived[:, 32:40, :], axis=0)
+    image = jnp.stack([arrived[0, :, 0:32, :], arrived[1, :, 0:32, :]], axis=1)
+    partial_points(image.reshape(512, 128), first, second, out)
+    moments[...] = jnp.sum(arrived[0, :, 32:40, :] + arrived[1, :, 32:40, :], axis=0)
 
 
 def weigh_body(partials, pair, first, second, out):
@@ -149,11 +151,13 @@
     one = (partials[0, 1] + partials[1, 1]) * pair[1, 64:320, :]
     weighted = jnp.concatenate([mine(zero, one), mine(one, zero)], axis=0)
     back = dot_halves(shared_panel(first, second), halves(weighted))
-    out[...] = back.reshape(16, 32, 128)
+    back = back.reshape(8, 2, 32, 128)
+    out[0] = back[:, 0]
+    out[1] = back[:, 1]
 
 
 def conduct_body(parts, panel, out):
-    sums = jnp.sum(parts[...], axis=0)
+    sums = jnp.sum(parts[...], axis=1)
     back = jnp.stack([sums[0].reshape(2, 16, 128), sums[1].reshape(2, 16, 128)], axis=1)
     back = back.reshape(64, 128).T
     zero = jnp.zeros_like(back)
@@ -264,10 +268,10 @@
 
     def returned(partial):
         partials = lax.all_gather(partial, "row_1", axis=0)
-        (back,) = call(weigh_body, [(16, 32, 128)], "weigh")(
+        (back,) = call(weigh_body, [(2, 8, 32, 128)], "weigh")(
             partials, pair, first, second
         )
-        back = exchange(back, ROW).reshape(8, 2, 32, 128)
+        back = exchange(back.reshape(16, 32, 128), CORE_MAJOR).reshape(2, 8, 32, 128)
         (kernel,) = call(conduct_body, [(32, 16, 128)], "conduct")(back, panel_conduction)
         return exchange(kernel, COL)
 
@@ -279,17 +283,17 @@
     y, spread = call(update_body, [(16, 128), (32, 16, 128)], "update")(returned(partial), gap, x)
 
     y_rows = exchange(spread, COL)
-    (image,) = call(second_points_body, [(8, 2, 40, 128)], "points_two")(
+    (image,) = call(second_points_body, [(2, 8, 40, 128)], "points_two")(
         first, y_rows, panel_conduction
     )
-    image = exchange(image.reshape(16, 40, 128), ROW)
+    image = exchange(image.reshape(16, 40, 128), CORE_MAJOR).reshape(2, 8, 40, 128)
     partial, moments = call(second_partial_body, [(2, 256, 128), (8, 128)], "partial_two")(
         image, first, second
     )
     u, q_2, message, scalars = call(
         last_body, [(16, 128), (16, 128), (64, 1, 128), (1, 128)], "last"
     )(returned(partial), gap, x, y, moments)
-    (message,) = call(fold_body, [(8, 1, 128)], "fold")(exchange(message, (*ROW, "col_0")))
+    (message,) = call(fold_body, [(8, 1, 128)], "fold")(exchange(message, (*CORE_MAJOR, "col_0")))
     out, coefficients = call(finish_body, [(32, 64), (4,)], "finish", smem=(1,))(
         exchange(message, "col_1"), u, q_2, scalars
     )

time: 201 us -> 200 us (level)
  no operation moved by 1% of the time
where the time goes in v12:
time: 200 us
  blocking collectives  167 us (84%)
  starting transfers between devices  23.2 us (12%)
  Pallas kernels  8.23 us (4%)
    all_to_all x8, blocking collectives, exchange(): return lax.all_to_all(value, axis, 0, 0, tiled=True)  123 us
    all_to_all x2, starting transfers between devices, exchange(): return lax.all_to_all(value, axis, 0, 0, tiled=True)  23.2 us
    all_gather x1, blocking collectives, shards(): panel_conduction = lax.all_gather(psi_conduction.T, ROW, axis=0, tiled=True)  19.2 us
    all_gather x1, blocking collectives, shards(): lax.all_gather(image, ROW, axis=0, tiled=True).reshape(32, 2, 16, 128)  16.6 us
    all_gather x2, blocking collectives, returned(): partials = lax.all_gather(partial, 'row_1', axis=0)  5.89 us
  transfers between devices with their start and end apart: 2, of which 0 were waited for; matrix products, arithmetic and copies ran while one was open for 0% of the time, Pallas kernels for 0%

profile of v12, /device:TPU:1, one launch (start us, length us, event | category | flops | bytes accessed | tf_op | source)
XLA Modules:
  0.0 199.6 jit_solution(12101360929426198608)
XLA Ops:
  0.6 1.9 start.1
  2.5 13.7 %all-to-all-start = ((f32[32,48,128]{2,1,0:T(8,128)}), f32[32,48,128]{2,1,0:T(8,128)S(1)}, u32[]{:S(2)}, u32[]{:S(2)}) async-start(f32[32,48,128]{2,1,0:T(8,128)} %get-tuple-element.20), calls=%async_computation | async-start | bytes 1572864 | tf_op jit(solution)/shard_map/all_to_all | solution.py:21
  16.3 2.6 %all-gather = f32[640,128]{1,0:T(8,128)S(1)} all-gather(f32[320,128]{1,0:T(8,128)S(1)} %get-tuple-element.21), channel_id=2, replica_groups=mesh['row_0'=8,'row_1'=2,'col_0'=4,'col_1'=8] {'row_1'}, dimensions={0}, use_global_device_ids=true | all-gather | bytes 491520 | tf_op jit(solution)/shard_map/all_gather | solution.py:265
  18.9 0.9 spread.1
  19.8 19.2 %all_gather.24 = f32[1024,128]{1,0:T(8,128)S(1)} all-gather(f32[64,128]{1,0:T(8,128)S(1)} %bitcast.33), channel_id=1, replica_groups=mesh['row_0'=8,'row_1'=2,'col_0'=4,'col_1'=8] {'row_0','row_1'}, dimensions={0}, use_global_device_ids=true | all-gather | bytes 557056 | tf_op jit(solution)/shard_map/all_gather | solution.py:262
  39.4 9.5 %all-to-all-start.1 = ((f32[32,32,128]{2,1,0:T(8,128)}), f32[32,32,128]{2,1,0:T(8,128)S(1)}, u32[]{:S(2)}, u32[]{:S(2)}) async-start(f32[32,32,128]{2,1,0:T(8,128)} %spread.1), calls=%async_computation.1 | async-start | bytes 1048576 | tf_op jit(solution)/shard_map/all_to_all | solution.py:21
  48.9 16.6 %all_gather.27 = f32[1024,128]{1,0:T(8,128)S(1)} all-gather(f32[64,128]{1,0:T(8,128)S(1)} %points_one.1), channel_id=1, replica_groups=mesh['row_0'=8,'row_1'=2,'col_0'=4,'col_1'=8] {'row_0','row_1'}, dimensions={0}, use_global_device_ids=true | all-gather | bytes 557056 | tf_op jit(solution)/shard_map/all_gather | solution.py:281
  65.6 0.5 partial_one.1
  66.1 2.8 %all-gather.1 = f32[4,256,128]{2,1,0:T(8,128)S(1)} all-gather(f32[2,256,128]{2,1,0:T(8,128)S(1)} %partial_one.1), channel_id=3, replica_groups=mesh['row_0'=8,'row_1'=2,'col_0'=4,'col_1'=8] {'row_1'}, dimensions={0}, use_global_device_ids=true | all-gather | bytes 786432 | tf_op jit(solution)/shard_map/all_gather | solution.py:270
  69.0 0.6 weigh.2
  69.6 13.9 %all_to_all.50 = f32[16,32,128]{2,1,0:T(8,128)S(1)} all-to-all(f32[16,32,128]{2,1,0:T(8,128)S(1)} %bitcast.30), channel_id=1, replica_groups=mesh['row_0'=8,'row_1'=2,'col_0'=4,'col_1'=8] {'row_1','row_0'}, dimensions={0} | all-to-all | bytes 524288 | tf_op jit(solution)/shard_map/all_to_all | solution.py:21
  83.5 0.5 conduct.2
  84.0 18.6 %all_to_all.51.parts = f32[32,16,128]{2,1,0:T(8,128)S(1)} all-to-all(f32[32,16,128]{2,1,0:T(8,128)S(1)} %conduct.2), channel_id=1, replica_groups=mesh['row_0'=8,'row_1'=2,'col_0'=4,'col_1'=8] {'col_0','col_1'}, dimensions={0} | all-to-all | bytes 524288 | tf_op jit(solution)/shard_map/all_to_all | solution.py:21
  102.7 15.6 %all_to_all.52.y_rows = f32[32,16,128]{2,1,0:T(8,128)S(1)} all-to-all(f32[32,16,128]{2,1,0:T(8,128)S(1)} %get-tuple-element.28), channel_id=1, replica_groups=mesh['row_0'=8,'row_1'=2,'col_0'=4,'col_1'=8] {'col_0','col_1'}, dimensions={0} | all-to-all | bytes 524288 | tf_op jit(solution)/shard_map/all_to_all | solution.py:21
  118.7 19.7 %all_to_all.53 = f32[16,40,128]{2,1,0:T(8,128)S(1)} all-to-all(f32[16,40,128]{2,1,0:T(8,128)S(1)} %bitcast.28), channel_id=1, replica_groups=mesh['row_0'=8,'row_1'=2,'col_0'=4,'col_1'=8] {'row_1','row_0'}, dimensions={0} | all-to-all | bytes 655360 | tf_op jit(solution)/shard_map/all_to_all | solution.py:21
  138.4 0.5 partial_two.1
  138.9 3.0 %all-gather.2 = f32[4,256,128]{2,1,0:T(8,128)S(1)} all-gather(f32[2,256,128]{2,1,0:T(8,128)S(1)} %get-tuple-element.29), channel_id=4, replica_groups=mesh['row_0'=8,'row_1'=2,'col_0'=4,'col_1'=8] {'row_1'}, dimensions={0}, use_global_device_ids=true | all-gather | bytes 786432 | tf_op jit(solution)/shard_map/all_gather | solution.py:270
  142.0 0.6 weigh.3
  142.6 13.6 %all_to_all.54 = f32[16,32,128]{2,1,0:T(8,128)S(1)} all-to-all(f32[16,32,128]{2,1,0:T(8,128)S(1)} %bitcast.29), channel_id=1, replica_groups=mesh['row_0'=8,'row_1'=2,'col_0'=4,'col_1'=8] {'row_1','row_0'}, dimensions={0} | all-to-all | bytes 524288 | tf_op jit(solution)/shard_map/all_to_all | solution.py:21
  156.2 0.5 conduct.3
  156.7 13.6 %all_to_all.55.parts = f32[32,16,128]{2,1,0:T(8,128)S(1)} all-to-all(f32[32,16,128]{2,1,0:T(8,128)S(1)} %conduct.3), channel_id=1, replica_groups=mesh['row_0'=8,'row_1'=2,'col_0'=4,'col_1'=8] {'col_0','col_1'}, dimensions={0} | all-to-all | bytes 524288 | tf_op jit(solution)/shard_map/all_to_all | solution.py:21
  170.5 19.0 %all_to_all.56.parts = f32[64,1,128]{2,1,0:T(1,128)S(1)} all-to-all(f32[64,1,128]{2,1,0:T(1,128)S(1)} %get-tuple-element.32), channel_id=1, replica_groups=mesh['row_0'=8,'row_1'=2,'col_0'=4,'col_1'=8] {'row_1','row_0','col_0'}, dimensions={0} | all-to-all | bytes 65536 | tf_op jit(solution)/shard_map/all_to_all | solution.py:21
  189.6 9.1 %all_to_all.57.parts = f32[8,1,128]{2,1,0:T(1,128)S(1)} all-to-all(f32[8,1,128]{2,1,0:T(1,128)S(1)} %fold.1), channel_id=1, replica_groups=mesh['row_0'=8,'row_1'=2,'col_0'=4,'col_1'=8] {'col_1'}, dimensions={0} | all-to-all | bytes 8192 | tf_op jit(solution)/shard_map/all_to_all | solution.py:21
  198.7 1.0 finish.1
  (9 shorter events, 1.3 us)
Async XLA Ops:
  2.5 36.4 %all-to-all-start = ((f32[32,48,128]{2,1,0:T(8,128)}), f32[32,48,128]{2,1,0:T(8,128)S(1)}, u32[]{:S(2)}, u32[]{:S(2)}) async-start(f32[32,48,128]{2,1,0:T(8,128)} %get-tuple-element.20), calls=%async_computation | async-start | bytes 1572864 | tf_op jit(solution)/shard_map/all_to_all | solution.py:21
  18.9 0.9 copy-start
  39.4 26.2 %all-to-all-start.1 = ((f32[32,32,128]{2,1,0:T(8,128)}), f32[32,32,128]{2,1,0:T(8,128)S(1)}, u32[]{:S(2)}, u32[]{:S(2)}) async-start(f32[32,32,128]{2,1,0:T(8,128)} %spread.1), calls=%async_computation.1 | async-start | bytes 1048576 | tf_op jit(solution)/shard_map/all_to_all | solution.py:21

commit v13 on v12

--- a/solution.py
+++ b/solution.py
@@ -12,6 +12,7 @@
 COL = ("col_0", "col_1")
 ROW = ("row_0", "row_1")
 CORE_MAJOR = ("row_1", "row_0")
+Z_MAJOR = ("col_1", "col_0")
 EPS = 1e-06
 SHIFT = 4.0
 F32 = jnp.float32
@@ -113,7 +114,7 @@
 
 def second_points_body(first, y_rows, panel, out):
     x = first[:, 0:16, :].reshape(512, 128)
-    y = y_rows[...].reshape(512, 128)
+    y = jnp.stack([y_rows[:, at] for at in range(4)], axis=0).reshape(512, 128)
     sums = [jnp.sum(a * b, axis=0, keepdims=True) for a, b in ((x, x), (x, y), (y, y))]
     sums.append(jnp.zeros((5, 128), F32))
     image = points_of(y, panel)
@@ -167,7 +168,9 @@
     hi = dot_halves(
         halves(panel[:, 1].reshape(512, 128)), halves(jnp.concatenate([zero, back], axis=1))
     )
-    out[...] = (lo + hi).reshape(32, 16, 128)
+    value = (lo + hi).reshape(4, 8, 16, 128)
+    for at in range(4):
+        out[:, at] = value[at]
 
 
 def update_body(parts, gap, x, packed, spread):
@@ -272,8 +275,8 @@
             partials, pair, first, second
         )
         back = exchange(back.reshape(16, 32, 128), CORE_MAJOR).reshape(2, 8, 32, 128)
-        (kernel,) = call(conduct_body, [(32, 16, 128)], "conduct")(back, panel_conduction)
-        return exchange(kernel, COL)
+        (kernel,) = call(conduct_body, [(8, 4, 16, 128)], "conduct")(back, panel_conduction)
+        return exchange(kernel.reshape(32, 16, 128), Z_MAJOR)
 
     (image,) = call(first_points_body, [(64, 128)], "points_one")(first, panel_conduction)
     image, second = lax.optimization_barrier((image, second))
@@ -282,7 +285,7 @@
     (partial,) = call(first_partial_body, [(2, 256, 128)], "partial_one")(image, first, second)
     y, spread = call(update_body, [(16, 128), (32, 16, 128)], "update")(returned(partial), gap, x)
 
-    y_rows = exchange(spread, COL)
+    y_rows = exchange(spread, Z_MAJOR).reshape(8, 4, 16, 128)
     (image,) = call(second_points_body, [(2, 8, 40, 128)], "points_two")(
         first, y_rows, panel_conduction
     )

time: 200 us -> 200 us (level)
  no operation moved by 1% of the time
where the time goes in v13:
time: 200 us; the launch traced here: 199 us
  blocking collectives  167 us (84%)
  starting transfers between devices  23.2 us (12%)
  Pallas kernels  8.22 us (4%)
    all_to_all x8, blocking collectives, exchange(): return lax.all_to_all(value, axis, 0, 0, tiled=True)  123 us
    all_to_all x2, starting transfers between devices, exchange(): return lax.all_to_all(value, axis, 0, 0, tiled=True)  23.2 us
    all_gather x1, blocking collectives, shards(): panel_conduction = lax.all_gather(psi_conduction.T, ROW, axis=0, tiled=True)  19.2 us
    all_gather x1, blocking collectives, shards(): lax.all_gather(image, ROW, axis=0, tiled=True).reshape(32, 2, 16, 128)  16.6 us
    all_gather x2, blocking collectives, returned(): partials = lax.all_gather(partial, 'row_1', axis=0)  5.89 us
  transfers between devices with their start and end apart: 2, of which 0 were waited for; matrix products, arithmetic and copies ran while one was open for 0% of the time, Pallas kernels for 0%

profile of v13, /device:TPU:1, one launch (start us, length us, event | category | flops | bytes accessed | tf_op | source)
XLA Modules:
  0.0 199.4 jit_solution(11757569337588074157)
XLA Ops:
  0.6 1.9 start.1
  2.5 13.7 %all-to-all-start = ((f32[32,48,128]{2,1,0:T(8,128)}), f32[32,48,128]{2,1,0:T(8,128)S(1)}, u32[]{:S(2)}, u32[]{:S(2)}) async-start(f32[32,48,128]{2,1,0:T(8,128)} %get-tuple-element.20), calls=%async_computation | async-start | bytes 1572864 | tf_op jit(solution)/shard_map/all_to_all | solution.py:22
  16.3 2.6 %all-gather = f32[640,128]{1,0:T(8,128)S(1)} all-gather(f32[320,128]{1,0:T(8,128)S(1)} %get-tuple-element.21), channel_id=2, replica_groups=mesh['row_0'=8,'row_1'=2,'col_0'=4,'col_1'=8] {'row_1'}, dimensions={0}, use_global_device_ids=true | all-gather | bytes 491520 | tf_op jit(solution)/shard_map/all_gather | solution.py:268
  18.9 0.9 spread.1
  19.8 19.2 %all_gather.24 = f32[1024,128]{1,0:T(8,128)S(1)} all-gather(f32[64,128]{1,0:T(8,128)S(1)} %bitcast.39), channel_id=1, replica_groups=mesh['row_0'=8,'row_1'=2,'col_0'=4,'col_1'=8] {'row_0','row_1'}, dimensions={0}, use_global_device_ids=true | all-gather | bytes 557056 | tf_op jit(solution)/shard_map/all_gather | solution.py:265
  39.4 9.5 %all-to-all-start.1 = ((f32[32,32,128]{2,1,0:T(8,128)}), f32[32,32,128]{2,1,0:T(8,128)S(1)}, u32[]{:S(2)}, u32[]{:S(2)}) async-start(f32[32,32,128]{2,1,0:T(8,128)} %spread.1), calls=%async_computation.1 | async-start | bytes 1048576 | tf_op jit(solution)/shard_map/all_to_all | solution.py:22
  48.9 16.6 %all_gather.27 = f32[1024,128]{1,0:T(8,128)S(1)} all-gather(f32[64,128]{1,0:T(8,128)S(1)} %points_one.1), channel_id=1, replica_groups=mesh['row_0'=8,'row_1'=2,'col_0'=4,'col_1'=8] {'row_0','row_1'}, dimensions={0}, use_global_device_ids=true | all-gather | bytes 557056 | tf_op jit(solution)/shard_map/all_gather | solution.py:284
  65.6 0.5 partial_one.1
  66.1 2.8 %all-gather.1 = f32[4,256,128]{2,1,0:T(8,128)S(1)} all-gather(f32[2,256,128]{2,1,0:T(8,128)S(1)} %partial_one.1), channel_id=3, replica_groups=mesh['row_0'=8,'row_1'=2,'col_0'=4,'col_1'=8] {'row_1'}, dimensions={0}, use_global_device_ids=true | all-gather | bytes 786432 | tf_op jit(solution)/shard_map/all_gather | solution.py:273
  69.0 0.6 weigh.2
  69.6 13.9 %all_to_all.50 = f32[16,32,128]{2,1,0:T(8,128)S(1)} all-to-all(f32[16,32,128]{2,1,0:T(8,128)S(1)} %bitcast.33), channel_id=1, replica_groups=mesh['row_0'=8,'row_1'=2,'col_0'=4,'col_1'=8] {'row_1','row_0'}, dimensions={0} | all-to-all | bytes 524288 | tf_op jit(solution)/shard_map/all_to_all | solution.py:22
  83.5 0.5 conduct.2
  84.0 19.5 %all_to_all.51.parts = f32[32,16,128]{2,1,0:T(8,128)S(1)} all-to-all(f32[32,16,128]{2,1,0:T(8,128)S(1)} %bitcast.37), channel_id=1, replica_groups=mesh['row_0'=8,'row_1'=2,'col_0'=4,'col_1'=8] {'col_1','col_0'}, dimensions={0} | all-to-all | bytes 524288 | tf_op jit(solution)/shard_map/all_to_all | solution.py:22
  103.5 15.4 %all_to_all.52 = f32[32,16,128]{2,1,0:T(8,128)S(1)} all-to-all(f32[32,16,128]{2,1,0:T(8,128)S(1)} %get-tuple-element.28), channel_id=1, replica_groups=mesh['row_0'=8,'row_1'=2,'col_0'=4,'col_1'=8] {'col_1','col_0'}, dimensions={0} | all-to-all | bytes 524288 | tf_op jit(solution)/shard_map/all_to_all | solution.py:22
  119.4 19.3 %all_to_all.53 = f32[16,40,128]{2,1,0:T(8,128)S(1)} all-to-all(f32[16,40,128]{2,1,0:T(8,128)S(1)} %bitcast.31), channel_id=1, replica_groups=mesh['row_0'=8,'row_1'=2,'col_0'=4,'col_1'=8] {'row_1','row_0'}, dimensions={0} | all-to-all | bytes 655360 | tf_op jit(solution)/shard_map/all_to_all | solution.py:22
  138.7 0.5 partial_two.1
  139.2 3.0 %all-gather.2 = f32[4,256,128]{2,1,0:T(8,128)S(1)} all-gather(f32[2,256,128]{2,1,0:T(8,128)S(1)} %get-tuple-element.29), channel_id=4, replica_groups=mesh['row_0'=8,'row_1'=2,'col_0'=4,'col_1'=8] {'row_1'}, dimensions={0}, use_global_device_ids=true | all-gather | bytes 786432 | tf_op jit(solution)/shard_map/all_gather | solution.py:273
  142.2 0.6 weigh.3
  142.8 13.6 %all_to_all.54 = f32[16,32,128]{2,1,0:T(8,128)S(1)} all-to-all(f32[16,32,128]{2,1,0:T(8,128)S(1)} %bitcast.32), channel_id=1, replica_groups=mesh['row_0'=8,'row_1'=2,'col_0'=4,'col_1'=8] {'row_1','row_0'}, dimensions={0} | all-to-all | bytes 524288 | tf_op jit(solution)/shard_map/all_to_all | solution.py:22
  156.5 0.5 conduct.3
  157.0 13.6 %all_to_all.55.parts = f32[32,16,128]{2,1,0:T(8,128)S(1)} all-to-all(f32[32,16,128]{2,1,0:T(8,128)S(1)} %bitcast.35), channel_id=1, replica_groups=mesh['row_0'=8,'row_1'=2,'col_0'=4,'col_1'=8] {'col_1','col_0'}, dimensions={0} | all-to-all | bytes 524288 | tf_op jit(solution)/shard_map/all_to_all | solution.py:22
  170.8 18.7 %all_to_all.56.parts = f32[64,1,128]{2,1,0:T(1,128)S(1)} all-to-all(f32[64,1,128]{2,1,0:T(1,128)S(1)} %get-tuple-element.32), channel_id=1, replica_groups=mesh['row_0'=8,'row_1'=2,'col_0'=4,'col_1'=8] {'row_1','row_0','col_0'}, dimensions={0} | all-to-all | bytes 65536 | tf_op jit(solution)/shard_map/all_to_all | solution.py:22
  189.6 8.9 %all_to_all.57.parts = f32[8,1,128]{2,1,0:T(1,128)S(1)} all-to-all(f32[8,1,128]{2,1,0:T(1,128)S(1)} %fold.1), channel_id=1, replica_groups=mesh['row_0'=8,'row_1'=2,'col_0'=4,'col_1'=8] {'col_1'}, dimensions={0} | all-to-all | bytes 8192 | tf_op jit(solution)/shard_map/all_to_all | solution.py:22
  198.5 1.0 finish.1
  (9 shorter events, 1.3 us)
Async XLA Ops:
  2.5 36.4 %all-to-all-start = ((f32[32,48,128]{2,1,0:T(8,128)}), f32[32,48,128]{2,1,0:T(8,128)S(1)}, u32[]{:S(2)}, u32[]{:S(2)}) async-start(f32[32,48,128]{2,1,0:T(8,128)} %get-tuple-element.20), calls=%async_computation | async-start | bytes 1572864 | tf_op jit(solution)/shard_map/all_to_all | solution.py:22
  18.9 0.9 copy-start
  39.4 26.2 %all-to-all-start.1 = ((f32[32,32,128]{2,1,0:T(8,128)}), f32[32,32,128]{2,1,0:T(8,128)S(1)}, u32[]{:S(2)}, u32[]{:S(2)}) async-start(f32[32,32,128]{2,1,0:T(8,128)} %spread.1), calls=%async_computation.1 | async-start | bytes 1048576 | tf_op jit(solution)/shard_map/all_to_all | solution.py:22

commit v14 on v13

--- a/solution.py
+++ b/solution.py
@@ -296,7 +296,7 @@
     u, q_2, message, scalars = call(
         last_body, [(16, 128), (16, 128), (64, 1, 128), (1, 128)], "last"
     )(returned(partial), gap, x, y, moments)
-    (message,) = call(fold_body, [(8, 1, 128)], "fold")(exchange(message, (*CORE_MAJOR, "col_0")))
+    (message,) = call(fold_body, [(8, 1, 128)], "fold")(exchange(message, ("col_0", *CORE_MAJOR)))
     out, coefficients = call(finish_body, [(32, 64), (4,)], "finish", smem=(1,))(
         exchange(message, "col_1"), u, q_2, scalars
     )

time: 200 us -> 200 us (level)
  no operation moved by 1% of the time
where the time goes in v14:
time: 200 us; the launch traced here: 199 us
  blocking collectives  167 us (84%)
  starting transfers between devices  23.2 us (12%)
  Pallas kernels  8.22 us (4%)
    all_to_all x8, blocking collectives, exchange(): return lax.all_to_all(value, axis, 0, 0, tiled=True)  123 us
    all_to_all x2, starting transfers between devices, exchange(): return lax.all_to_all(value, axis, 0, 0, tiled=True)  23.2 us
    all_gather x1, blocking collectives, shards(): panel_conduction = lax.all_gather(psi_conduction.T, ROW, axis=0, tiled=True)  19.2 us
    all_gather x1, blocking collectives, shards(): lax.all_gather(image, ROW, axis=0, tiled=True).reshape(32, 2, 16, 128)  16.6 us
    all_gather x2, blocking collectives, returned(): partials = lax.all_gather(partial, 'row_1', axis=0)  5.89 us
  transfers between devices with their start and end apart: 2, of which 0 were waited for; matrix products, arithmetic and copies ran while one was open for 0% of the time, Pallas kernels for 0%

profile of v14, /device:TPU:1, one launch (start us, length us, event | category | flops | bytes accessed | tf_op | source)
XLA Modules:
  0.0 199.4 jit_solution(8646598128773868816)
XLA Ops:
  0.6 1.9 start.1
  2.5 13.7 %all-to-all-start = ((f32[32,48,128]{2,1,0:T(8,128)}), f32[32,48,128]{2,1,0:T(8,128)S(1)}, u32[]{:S(2)}, u32[]{:S(2)}) async-start(f32[32,48,128]{2,1,0:T(8,128)} %get-tuple-element.20), calls=%async_computation | async-start | bytes 1572864 | tf_op jit(solution)/shard_map/all_to_all | solution.py:22
  16.3 2.6 %all-gather = f32[640,128]{1,0:T(8,128)S(1)} all-gather(f32[320,128]{1,0:T(8,128)S(1)} %get-tuple-element.21), channel_id=2, replica_groups=mesh['row_0'=8,'row_1'=2,'col_0'=4,'col_1'=8] {'row_1'}, dimensions={0}, use_global_device_ids=true | all-gather | bytes 491520 | tf_op jit(solution)/shard_map/all_gather | solution.py:268
  18.9 0.9 spread.1
  19.8 19.2 %all_gather.24 = f32[1024,128]{1,0:T(8,128)S(1)} all-gather(f32[64,128]{1,0:T(8,128)S(1)} %bitcast.39), channel_id=1, replica_groups=mesh['row_0'=8,'row_1'=2,'col_0'=4,'col_1'=8] {'row_0','row_1'}, dimensions={0}, use_global_device_ids=true | all-gather | bytes 557056 | tf_op jit(solution)/shard_map/all_gather | solution.py:265
  39.4 9.5 %all-to-all-start.1 = ((f32[32,32,128]{2,1,0:T(8,128)}), f32[32,32,128]{2,1,0:T(8,128)S(1)}, u32[]{:S(2)}, u32[]{:S(2)}) async-start(f32[32,32,128]{2,1,0:T(8,128)} %spread.1), calls=%async_computation.1 | async-start | bytes 1048576 | tf_op jit(solution)/shard_map/all_to_all | solution.py:22
  48.9 16.6 %all_gather.27 = f32[1024,128]{1,0:T(8,128)S(1)} all-gather(f32[64,128]{1,0:T(8,128)S(1)} %points_one.1), channel_id=1, replica_groups=mesh['row_0'=8,'row_1'=2,'col_0'=4,'col_1'=8] {'row_0','row_1'}, dimensions={0}, use_global_device_ids=true | all-gather | bytes 557056 | tf_op jit(solution)/shard_map/all_gather | solution.py:284
  65.6 0.5 partial_one.1
  66.1 2.8 %all-gather.1 = f32[4,256,128]{2,1,0:T(8,128)S(1)} all-gather(f32[2,256,128]{2,1,0:T(8,128)S(1)} %partial_one.1), channel_id=3, replica_groups=mesh['row_0'=8,'row_1'=2,'col_0'=4,'col_1'=8] {'row_1'}, dimensions={0}, use_global_device_ids=true | all-gather | bytes 786432 | tf_op jit(solution)/shard_map/all_gather | solution.py:273
  69.0 0.6 weigh.2
  69.6 13.9 %all_to_all.50 = f32[16,32,128]{2,1,0:T(8,128)S(1)} all-to-all(f32[16,32,128]{2,1,0:T(8,128)S(1)} %bitcast.33), channel_id=1, replica_groups=mesh['row_0'=8,'row_1'=2,'col_0'=4,'col_1'=8] {'row_1','row_0'}, dimensions={0} | all-to-all | bytes 524288 | tf_op jit(solution)/shard_map/all_to_all | solution.py:22
  83.5 0.5 conduct.2
  84.0 19.5 %all_to_all.51.parts = f32[32,16,128]{2,1,0:T(8,128)S(1)} all-to-all(f32[32,16,128]{2,1,0:T(8,128)S(1)} %bitcast.37), channel_id=1, replica_groups=mesh['row_0'=8,'row_1'=2,'col_0'=4,'col_1'=8] {'col_1','col_0'}, dimensions={0} | all-to-all | bytes 524288 | tf_op jit(solution)/shard_map/all_to_all | solution.py:22
  103.5 15.4 %all_to_all.52 = f32[32,16,128]{2,1,0:T(8,128)S(1)} all-to-all(f32[32,16,128]{2,1,0:T(8,128)S(1)} %get-tuple-element.28), channel_id=1, replica_groups=mesh['row_0'=8,'row_1'=2,'col_0'=4,'col_1'=8] {'col_1','col_0'}, dimensions={0} | all-to-all | bytes 524288 | tf_op jit(solution)/shard_map/all_to_all | solution.py:22
  119.4 19.3 %all_to_all.53 = f32[16,40,128]{2,1,0:T(8,128)S(1)} all-to-all(f32[16,40,128]{2,1,0:T(8,128)S(1)} %bitcast.31), channel_id=1, replica_groups=mesh['row_0'=8,'row_1'=2,'col_0'=4,'col_1'=8] {'row_1','row_0'}, dimensions={0} | all-to-all | bytes 655360 | tf_op jit(solution)/shard_map/all_to_all | solution.py:22
  138.7 0.5 partial_two.1
  139.2 3.0 %all-gather.2 = f32[4,256,128]{2,1,0:T(8,128)S(1)} all-gather(f32[2,256,128]{2,1,0:T(8,128)S(1)} %get-tuple-element.29), channel_id=4, replica_groups=mesh['row_0'=8,'row_1'=2,'col_0'=4,'col_1'=8] {'row_1'}, dimensions={0}, use_global_device_ids=true | all-gather | bytes 786432 | tf_op jit(solution)/shard_map/all_gather | solution.py:273
  142.2 0.6 weigh.3
  142.8 13.6 %all_to_all.54 = f32[16,32,128]{2,1,0:T(8,128)S(1)} all-to-all(f32[16,32,128]{2,1,0:T(8,128)S(1)} %bitcast.32), channel_id=1, replica_groups=mesh['row_0'=8,'row_1'=2,'col_0'=4,'col_1'=8] {'row_1','row_0'}, dimensions={0} | all-to-all | bytes 524288 | tf_op jit(solution)/shard_map/all_to_all | solution.py:22
  156.5 0.5 conduct.3
  157.0 13.6 %all_to_all.55.parts = f32[32,16,128]{2,1,0:T(8,128)S(1)} all-to-all(f32[32,16,128]{2,1,0:T(8,128)S(1)} %bitcast.35), channel_id=1, replica_groups=mesh['row_0'=8,'row_1'=2,'col_0'=4,'col_1'=8] {'col_1','col_0'}, dimensions={0} | all-to-all | bytes 524288 | tf_op jit(solution)/shard_map/all_to_all | solution.py:22
  170.8 18.7 %all_to_all.56.parts = f32[64,1,128]{2,1,0:T(1,128)S(1)} all-to-all(f32[64,1,128]{2,1,0:T(1,128)S(1)} %get-tuple-element.32), channel_id=1, replica_groups=mesh['row_0'=8,'row_1'=2,'col_0'=4,'col_1'=8] {'col_0','row_1','row_0'}, dimensions={0} | all-to-all | bytes 65536 | tf_op jit(solution)/shard_map/all_to_all | solution.py:22
  189.6 8.9 %all_to_all.57.parts = f32[8,1,128]{2,1,0:T(1,128)S(1)} all-to-all(f32[8,1,128]{2,1,0:T(1,128)S(1)} %fold.1), channel_id=1, replica_groups=mesh['row_0'=8,'row_1'=2,'col_0'=4,'col_1'=8] {'col_1'}, dimensions={0} | all-to-all | bytes 8192 | tf_op jit(solution)/shard_map/all_to_all | solution.py:22
  198.5 1.0 finish.1
  (9 shorter events, 1.3 us)
Async XLA Ops:
  2.5 36.4 %all-to-all-start = ((f32[32,48,128]{2,1,0:T(8,128)}), f32[32,48,128]{2,1,0:T(8,128)S(1)}, u32[]{:S(2)}, u32[]{:S(2)}) async-start(f32[32,48,128]{2,1,0:T(8,128)} %get-tuple-element.20), calls=%async_computation | async-start | bytes 1572864 | tf_op jit(solution)/shard_map/all_to_all | solution.py:22
  18.9 0.9 copy-start
  39.4 26.2 %all-to-all-start.1 = ((f32[32,32,128]{2,1,0:T(8,128)}), f32[32,32,128]{2,1,0:T(8,128)S(1)}, u32[]{:S(2)}, u32[]{:S(2)}) async-start(f32[32,32,128]{2,1,0:T(8,128)} %spread.1), calls=%async_computation.1 | async-start | bytes 1048576 | tf_op jit(solution)/shard_map/all_to_all | solution.py:22
